TPU v7x, 32 devices: a whole 2x2x4 slice. The times are simulated.
32 devices in a mesh: rep: 4 (over z), slab: 8 (over y, x, core).
Axes of the slice: x: 2, y: 2, z: 4, core: 2. Of those that a mesh axis runs over, the one named last changes fastest.
Arguments:
- feats: bfloat16 [4, 32, 12288], P('rep', None, 'slab'), may hold values from -6 to 6
- tile_weight: bfloat16 [4, 768, 64, 512], P('rep', 'slab'), may hold values from -0.25 to 0.25
- tile_atom: int32 [4, 768], P('rep', 'slab'), may hold values from 0 to 23
- tile_cell: int32 [4, 768], P('rep', 'slab'), may hold values from 0 to 31
- tile_live: int32 [4, 8], P('rep', 'slab'), may hold values from 24 to 96, as said below
- w_mix: bfloat16 [32, 32], replicated, may hold values from -1 to 1
- conv_w: bfloat16 [27, 32, 32], replicated, may hold values from -0.21875 to 0.21875
- cotangent: bfloat16 [4, 32, 12288], P('rep', None, 'slab'), may hold values from -6 to 6
Outputs:
- potential: bfloat16 [4, 32, 12288], P('rep', None, 'slab')
- grad_feats: bfloat16 [4, 32, 12288], P('rep', None, 'slab')
- grad_conv: float32 [27, 32, 32], replicated
- grad_mix: float32 [32, 32], replicated
Inputs may be any that keep to these rules, and one draw needn't show every extreme that they name: The first tile_live slots of a slab's list are live, the rest are ignored; in every system some slab has all 96 slots live. `tile_atom`: atom block within the tile's own slab. `tile_cell`: cell block within the slab's window of 8 planes that starts 2 planes below the slab.
All inputs are finite; a program needn't handle non-finite values.
Results may differ from a plain program's by a relative error of at most 0.013.
Values may be sent and summed in bfloat16 or wider, within the bound.
No kernel may reach another device: no remote copies, remote signals or barrier semaphores. Data moves between devices by JAX's collectives and lax.ppermute only.
A program may use at most 128 MiB of HBM per device.

v0:
```python
import functools
import math

import jax
import jax.numpy as jnp
from jax import lax
from jax.experimental import pallas as pl
from jax.experimental.pallas import tpu as pltpu
from jax.sharding import PartitionSpec as P

GY = 32
GX = 64
ZD = 4
ZH = 2
F32 = jnp.float32
BF16 = jnp.bfloat16
VMEM_LIMIT = 16 * 1024 * 1024


def params(*semantics):
    return pltpu.CompilerParams(
        dimension_semantics=semantics or None, vmem_limit_bytes=VMEM_LIMIT
    )


def whole():
    return pl.BlockSpec(memory_space=pltpu.VMEM)


def copies(pairs, sems):
    return [
        pltpu.make_async_copy(source, target, sems.at[i])
        for i, (source, target) in enumerate(pairs)
    ]


def add_tiles(tiles, atom_ref, cell_ref, live, source, weight_ref, total):
    for j in range(tiles.start, tiles.stop):
        picked = source[atom_ref[0, j]]
        picked = jnp.where(j < live, picked, jnp.zeros_like(picked))
        total[cell_ref[0, j]] += jnp.dot(
            picked, weight_ref[j], preferred_element_type=F32
        )


def split_atoms(field, source):
    tile_a = source.shape[2]
    for a in range(source.shape[0]):
        source[a] = field[:, a * tile_a : (a + 1) * tile_a]


def write_parts(total, refs):
    first = 0
    for ref in refs:
        count = ref.shape[0]
        ref[...] = total[first : first + count].astype(BF16)
        first += count


def first_deposit_kernel(
    atom_hbm, cell_hbm, live_ref, feats_hbm, weight_hbm,
    down_ref, middle_ref, up_ref, weight_ref,
    atom_ref, cell_ref, small_sems, source, total, feats, weight_sems,
):
    chunks = weight_sems.shape[0]
    per_chunk = weight_ref.shape[0] // chunks
    small = copies(
        ((atom_hbm, atom_ref), (cell_hbm, cell_ref), (feats_hbm, feats)), small_sems
    )
    parts = [slice(i * per_chunk, (i + 1) * per_chunk) for i in range(chunks)]
    large = copies([(weight_hbm.at[p], weight_ref.at[p]) for p in parts], weight_sems)
    for copy in small + large:
        copy.start()
    total[...] = jnp.zeros_like(total)
    for copy in small:
        copy.wait()
    split_atoms(feats[...], source)
    live = live_ref[0, 0]
    for part, copy in zip(parts, large):
        copy.wait()
        add_tiles(part, atom_ref, cell_ref, live, source, weight_ref, total)
    write_parts(total, (down_ref, middle_ref, up_ref))


def second_deposit_kernel(
    atom_hbm, cell_hbm, live_ref, cot_ref, weight_ref,
    down_ref, middle_ref, up_ref,
    atom_ref, cell_ref, small_sems, source, total,
):
    small = copies(((atom_hbm, atom_ref), (cell_hbm, cell_ref)), small_sems)
    for copy in small:
        copy.start()
    total[...] = jnp.zeros_like(total)
    split_atoms(cot_ref[...], source)
    for copy in small:
        copy.wait()
    tiles = slice(0, weight_ref.shape[0])
    add_tiles(tiles, atom_ref, cell_ref, live_ref[0, 0], source, weight_ref, total)
    write_parts(total, (down_ref, middle_ref, up_ref))


def in_hbm(*values):
    return [pltpu.with_memory_space_constraint(value, pltpu.HBM) for value in values]


def hbm():
    return pl.BlockSpec(memory_space=pltpu.HBM)


def list_scratch(atom_ids, cell_ids):
    return [
        pltpu.SMEM(atom_ids.shape, jnp.int32),
        pltpu.SMEM(cell_ids.shape, jnp.int32),
        pltpu.SemaphoreType.DMA((3,)),
    ]


def list_specs():
    return [hbm(), hbm(), pl.BlockSpec(memory_space=pltpu.SMEM)]


def deposit_shapes(field, weights):
    channels, atoms = field.shape
    _, tile_a, tile_c = weights.shape
    quarters = GY * GX // tile_c
    parts = [
        jax.ShapeDtypeStruct((planes * quarters, channels, tile_c), BF16)
        for planes in (ZH + 1, ZD - 2, ZH + 1)
    ]
    scratch = [
        pltpu.VMEM((atoms // tile_a, channels, tile_a), BF16),
        pltpu.VMEM(((ZD + 2 * ZH) * quarters, channels, tile_c), F32),
    ]
    return parts, scratch


def first_deposit(feats, weights, atom_ids, cell_ids, live):
    parts, scratch = deposit_shapes(feats, weights)
    return pl.pallas_call(
        first_deposit_kernel,
        in_specs=list_specs() + [hbm()] * 2,
        out_specs=[whole()] * 4,
        out_shape=parts + [jax.ShapeDtypeStruct(weights.shape, BF16)],
        scratch_shapes=list_scratch(atom_ids, cell_ids)
        + scratch
        + [pltpu.VMEM(feats.shape, BF16), pltpu.SemaphoreType.DMA((8,))],
        compiler_params=params(),
        name="first_deposit",
    )(*in_hbm(atom_ids, cell_ids), live, *in_hbm(feats, weights))


def second_deposit(cot, weights, atom_ids, cell_ids, live):
    parts, scratch = deposit_shapes(cot, weights)
    return pl.pallas_call(
        second_deposit_kernel,
        in_specs=list_specs() + [whole()] * 2,
        out_specs=[whole()] * 3,
        out_shape=parts,
        scratch_shapes=list_scratch(atom_ids, cell_ids) + scratch,
        compiler_params=params(),
        name="second_deposit",
    )(*in_hbm(atom_ids, cell_ids), live, cot, weights)


def toeplitz_kernel(conv_ref, forward_ref, backward_ref):
    channels = conv_ref.shape[1]
    for flip, out_ref in ((False, forward_ref), (True, backward_ref)):
        for dx in range(3):
            for dy in range(3):
                parts = []
                for dz in range(3):
                    if flip:
                        k = 9 * (2 - dz) + 3 * (2 - dy) + (2 - dx)
                        parts.append(conv_ref[k].astype(F32).T)
                    else:
                        parts.append(conv_ref[9 * dz + 3 * dy + dx].astype(F32))
                band = jnp.concatenate(parts, axis=1)
                for po in range(ZD):
                    pieces = []
                    if po:
                        pieces.append(jnp.zeros((channels, po * channels), F32))
                    pieces.append(band)
                    rest = (ZD - 1 - po) * channels
                    if rest:
                        pieces.append(jnp.zeros((channels, rest), F32))
                    row = (dy * ZD + po) * channels
                    out_ref[dx, row : row + channels] = jnp.concatenate(
                        pieces, axis=1
                    ).astype(BF16)


def toeplitz(conv_w):
    channels = conv_w.shape[1]
    shape = jax.ShapeDtypeStruct((3, 3 * ZD * channels, (ZD + 2) * channels), BF16)
    return pl.pallas_call(
        toeplitz_kernel,
        in_specs=[whole()],
        out_specs=[whole()] * 2,
        out_shape=[shape, shape],
        compiler_params=params(),
        name="toeplitz",
    )(conv_w)


def joined_planes(down, middle, up, from_below, from_above):
    quarters = middle.shape[0] // (ZD - 2)
    own = [down[q] for q in range(quarters, 3 * quarters)]
    own += [middle[q] for q in range(2 * quarters)]
    own += [up[q] for q in range(2 * quarters)]
    other = [from_below[q] for q in range(3 * quarters)]
    other += [from_above[q] for q in range(3 * quarters)]
    sums = [a.astype(F32) + b.astype(F32) for a, b in zip(own, other)]
    return [
        jnp.concatenate(sums[p * quarters : (p + 1) * quarters], axis=1)
        for p in range(ZD + 2)
    ]


def column(shape):
    return lax.rem(lax.broadcasted_iota(jnp.int32, shape, 1), GX)


def store_shifted(out_ref, row, value):
    rows, cells = value.shape
    x = column(value.shape)
    group = out_ref.shape[0] // 3
    left = jnp.where(
        x == 0, pltpu.roll(value, cells - GX + 1, 1), pltpu.roll(value, 1, 1)
    )
    right = jnp.where(
        x == GX - 1, pltpu.roll(value, GX - 1, 1), pltpu.roll(value, cells - 1, 1)
    )
    out_ref[row : row + rows] = left.astype(BF16)
    out_ref[group + row : group + row + rows] = value.astype(BF16)
    out_ref[2 * group + row : 2 * group + row + rows] = right.astype(BF16)


def conv_planes(matrix_ref, shifted, partial, low_ref, high_ref):
    cells = shifted.shape[1]
    group = shifted.shape[0] // 3
    chunk = low_ref.shape[2]
    for q in range(cells // chunk):
        cols = slice(q * chunk, (q + 1) * chunk)
        acc = None
        for dx in range(3):
            term = jnp.dot(
                matrix_ref[dx],
                shifted[dx * group : (dx + 1) * group, cols],
                preferred_element_type=F32,
            )
            acc = term if acc is None else acc + term
        partial[:, cols] = acc
    channels = low_ref.shape[1]
    quarters = cells // chunk
    for po in range(ZD):
        rows = slice(po * channels, (po + 1) * channels)
        third = ZD * channels
        before = partial[rows, :]
        here = partial[third + po * channels : third + (po + 1) * channels, :]
        after = partial[2 * third + po * channels : 2 * third + (po + 1) * channels, :]
        result = (
            here + pltpu.roll(before, GX, 1) + pltpu.roll(after, cells - GX, 1)
        ).astype(BF16)
        out_ref = low_ref if po < ZH else high_ref
        first = (po % ZH) * quarters
        for q in range(quarters):
            out_ref[first + q] = result[:, q * chunk : (q + 1) * chunk]


def forward_kernel(
    down, middle, up, below, above, mix_ref, matrix_ref,
    low_ref, high_ref, plain_ref, shifted, partial,
):
    channels = mix_ref.shape[0]
    for p, plane in enumerate(joined_planes(down, middle, up, below, above)):
        plane = plane.astype(BF16)
        plain_ref[p * channels : (p + 1) * channels] = plane
        mixed = jnp.dot(mix_ref[...], plane, preferred_element_type=F32)
        store_shifted(shifted, p * channels, mixed.astype(BF16).astype(F32))
    conv_planes(matrix_ref, shifted, partial, low_ref, high_ref)


def gradient_kernel(
    parity_ref, down, middle, up, below, above, plain_ref,
    keep_ref, send_ref, sums_ref, shifted, upstream,
):
    channels = down.shape[1]
    cells = plain_ref.shape[1]
    for p in range(ZD + 2):
        rows = slice(p * channels, (p + 1) * channels)
        store_shifted(shifted, p * channels, plain_ref[rows].astype(F32))
    planes = joined_planes(down, middle, up, below, above)
    third = ZD * channels
    for p in range(ZD + 2):
        sums_ref[p * channels : (p + 1) * channels] = planes[p].astype(BF16)
    for p in range(ZD):
        plane = planes[p + 1]
        row = p * channels
        upstream[row : row + channels] = pltpu.roll(plane, cells - GX, 1).astype(BF16)
        upstream[third + row : third + row + channels] = plane.astype(BF16)
        upstream[2 * third + row : 2 * third + row + channels] = pltpu.roll(
            plane, GX, 1
        ).astype(BF16)
    wide = (ZD + 2) * channels
    blocks = []
    for dx in range(3):
        product = lax.dot_general(
            upstream[...],
            shifted[dx * wide : (dx + 1) * wide],
            (((1,), (1,)), ((), ())),
            preferred_element_type=F32,
        )
        for dy in range(3):
            block = None
            for po in range(ZD):
                row = (dy * ZD + po) * channels
                piece = product[
                    row : row + channels, po * channels : (po + 3) * channels
                ]
                block = piece if block is None else block + piece
            blocks.append(
                jnp.concatenate([block, jnp.zeros((channels, channels), F32)], axis=1)
            )
    half = keep_ref.shape[0]
    grads = jnp.concatenate(blocks, axis=0)
    first, second = grads[:half], grads[half:]
    odd = parity_ref[0] == 1

    @pl.when(odd)
    def _():
        keep_ref[...] = second
        send_ref[...] = first

    @pl.when(jnp.logical_not(odd))
    def _():
        keep_ref[...] = first
        send_ref[...] = second


def backward_kernel(sums_ref, matrix_ref, low_ref, high_ref, shifted, partial):
    channels = low_ref.shape[1]
    for p in range(ZD + 2):
        rows = slice(p * channels, (p + 1) * channels)
        store_shifted(shifted, p * channels, sums_ref[rows].astype(F32))
    conv_planes(matrix_ref, shifted, partial, low_ref, high_ref)


def gather_kernel(
    atom_hbm, cell_hbm, live_ref, weight_ref, mix_ref,
    a0, a1, a2, a3, b0, b1, b2, b3, potential_ref, grad_ref,
    atom_ref, cell_ref, small_sems, field, total,
):
    channels = mix_ref.shape[0]
    tiles, tile_a, _ = weight_ref.shape
    small = copies(((atom_hbm, atom_ref), (cell_hbm, cell_ref)), small_sems)
    for copy in small:
        copy.start()
    first = 0
    for a, b in ((a0, b0), (a1, b1), (a2, b2), (a3, b3)):
        count = a.shape[0]
        field[first : first + count, :channels] = a[...]
        field[first : first + count, channels:] = b[...]
        first += count
    total[...] = jnp.zeros_like(total)
    for copy in small:
        copy.wait()
    live = live_ref[0, 0]
    for j in range(tiles):
        product = lax.dot_general(
            field[cell_ref[0, j]],
            weight_ref[j],
            (((1,), (1,)), ((), ())),
            preferred_element_type=F32,
        )
        total[atom_ref[0, j]] += jnp.where(j < live, product, jnp.zeros_like(product))

    mix_t = mix_ref[...].astype(F32).T.astype(BF16)
    for a in range(0, total.shape[0], 2):
        pair = jnp.concatenate([total[a], total[a + 1]], axis=1).astype(BF16)
        cols = slice(a * tile_a, (a + 2) * tile_a)
        potential_ref[:, cols] = pair[:channels]
        grad_ref[:, cols] = jnp.dot(
            mix_t, pair[channels:], preferred_element_type=F32
        ).astype(BF16)


def gather(phi, drho, weights, atom_ids, cell_ids, live, w_mix, atoms):
    _, tile_a, tile_c = weights.shape
    channels = w_mix.shape[0]
    blocks = sum(part.shape[0] for part in phi)
    shape = jax.ShapeDtypeStruct((channels, atoms), BF16)
    return pl.pallas_call(
        gather_kernel,
        in_specs=list_specs() + [whole()] * 10,
        out_specs=[whole()] * 2,
        out_shape=[shape, shape],
        scratch_shapes=list_scratch(atom_ids, cell_ids)
        + [
            pltpu.VMEM((blocks, 2 * channels, tile_c), BF16),
            pltpu.VMEM((atoms // tile_a, 2 * channels, tile_a), F32),
        ],
        compiler_params=params(),
        name="gather",
    )(*in_hbm(atom_ids, cell_ids), live, weights, w_mix, *phi, *drho)


def finish_kernel(
    parity_ref, mine_ref, other_ref, mix_ref, conv_ref, conv_out, mix_out,
    *, conv_scale, mix_scale,
):
    channels = mix_ref.shape[0]
    mine, other = mine_ref[...], other_ref[...]
    odd = parity_ref[0] == 1
    total = jnp.concatenate(
        [jnp.where(odd, other, mine), jnp.where(odd, mine, other)], axis=0
    )
    mix = mix_ref[...].astype(F32)
    acc = jnp.zeros((channels, channels), F32)
    for dz in range(3):
        part = total[:, dz * channels : (dz + 1) * channels]
        scaled = lax.dot_general(
            part, mix, (((1,), (1,)), ((), ())),
            precision=lax.Precision.HIGHEST, preferred_element_type=F32,
        ) * (1.0 / conv_scale)
        kernels = []
        for dx in range(3):
            for dy in range(3):
                row = (3 * dx + dy) * channels
                k = 9 * dz + 3 * dy + dx
                conv_out[k] = scaled[row : row + channels]
                kernels.append(conv_ref[k].astype(F32))
        acc = acc + lax.dot_general(
            jnp.concatenate(kernels, axis=0), part, (((0,), (0,)), ((), ())),
            precision=lax.Precision.HIGHEST, preferred_element_type=F32,
        )
    mix_out[...] = acc * (1.0 / mix_scale)


def ring(value, axis, steps):
    count = lax.axis_size(axis)
    pairs = [(source, (source + steps) % count) for source in range(count)]
    return lax.ppermute(value, axis, pairs)


def exchanged(value, axis, stride):
    count = lax.axis_size(axis)
    return lax.ppermute(value, axis, [(i, i ^ stride) for i in range(count)])


def local(feats, tile_weight, tile_atom, tile_cell, tile_live, w_mix, conv_w, cotangent):
    return step(
        feats[0], tile_weight[0], tile_atom, tile_cell, tile_live,
        w_mix, conv_w, cotangent[0],
    )


def step(feats, weights, atom_ids, cell_ids, live, w_mix, conv_w, cot):
    channels, atoms = feats.shape
    tile_c = weights.shape[2]
    quarters = GY * GX // tile_c
    cells = GY * GX
    smem = pl.BlockSpec(memory_space=pltpu.SMEM)
    parity = jnp.reshape(lax.axis_index("slab") % 2, (1,)).astype(jnp.int32)

    dd, dm, du, held = first_deposit(feats, weights, atom_ids, cell_ids, live)
    d_below, d_above = ring(du, "slab", 1), ring(dd, "slab", -1)
    ed, em, eu = second_deposit(cot, held, atom_ids, cell_ids, live)
    e_below, e_above = ring(eu, "slab", 1), ring(ed, "slab", -1)
    forward, backward = toeplitz(conv_w)

    half = jax.ShapeDtypeStruct((ZH * quarters, channels, tile_c), BF16)
    rows = (ZD + 2) * channels
    scratch = [
        pltpu.VMEM((3 * rows, cells), BF16),
        pltpu.VMEM((3 * ZD * channels, cells), F32),
    ]
    phi_low, phi_high, plain = pl.pallas_call(
        forward_kernel,
        in_specs=[whole()] * 7,
        out_specs=[whole()] * 3,
        out_shape=[half, half, jax.ShapeDtypeStruct((rows, cells), BF16)],
        scratch_shapes=scratch,
        compiler_params=params(),
        name="forward",
    )(dd, dm, du, d_below, d_above, w_mix, forward)
    phi_below, phi_above = ring(phi_high, "slab", 1), ring(phi_low, "slab", -1)

    part = jax.ShapeDtypeStruct((9 * channels // 2, 4 * channels), F32)
    keep, send, sums = pl.pallas_call(
        gradient_kernel,
        in_specs=[smem] + [whole()] * 6,
        out_specs=[whole()] * 3,
        out_shape=[part, part, jax.ShapeDtypeStruct((rows, cells), BF16)],
        scratch_shapes=[scratch[0], pltpu.VMEM((3 * ZD * channels, cells), BF16)],
        compiler_params=params(),
        name="gradient",
    )(parity, ed, em, eu, e_below, e_above, plain)
    arrived = exchanged(send, "slab", 1)
    drho_low, drho_high = pl.pallas_call(
        backward_kernel,
        in_specs=[whole()] * 2,
        out_specs=[whole()] * 2,
        out_shape=[half, half],
        scratch_shapes=scratch,
        compiler_params=params(),
        name="backward",
    )(sums, backward)
    drho_below, drho_above = ring(drho_high, "slab", 1), ring(drho_low, "slab", -1)

    total = keep + arrived
    for axis, first in (("rep", 1), ("slab", 4), ("slab", 2)):
        stride = first
        while stride < lax.axis_size(axis) and (axis == "rep" or stride == 2 or stride >= 4):
            arrived = exchanged(total, axis, stride)
            total = total + arrived
            if stride == 2 and axis == "slab":
                break
            stride *= 2
    other = exchanged(total, "slab", 1)

    groups = lax.axis_size("rep") * lax.axis_size("slab")
    conv_grad, mix_grad = pl.pallas_call(
        functools.partial(
            finish_kernel,
            conv_scale=math.sqrt(groups * ZD * cells),
            mix_scale=math.sqrt(groups * atoms),
        ),
        in_specs=[smem] + [whole()] * 4,
        out_specs=[whole()] * 2,
        out_shape=[
            jax.ShapeDtypeStruct(conv_w.shape, F32),
            jax.ShapeDtypeStruct(w_mix.shape, F32),
        ],
        compiler_params=params(),
        name="finish",
    )(parity, total, other, w_mix, conv_w)

    potential, feats_grad = gather(
        (phi_below, phi_low, phi_high, phi_above),
        (drho_below, drho_low, drho_high, drho_above),
        weights, atom_ids, cell_ids, live, w_mix, atoms,
    )
    return potential[None], feats_grad[None], conv_grad, mix_grad


def solution(mesh):
    return jax.shard_map(
        local,
        mesh=mesh,
        in_specs=(
            P("rep", None, "slab"),
            P("rep", "slab", None, None),
            P("rep", "slab"),
            P("rep", "slab"),
            P("rep", "slab"),
            P(),
            P(),
            P("rep", None, "slab"),
        ),
        out_specs=(P("rep", None, "slab"), P("rep", None, "slab"), P(), P()),
        check_vma=False,
    )
```

profile of v0, /device:TPU:0, one launch (start us, length us, event | category | flops | bytes accessed | tf_op | source)
XLA Modules:
  0.0 64.8 jit_solution(12383709091175070717)
XLA Ops:
  0.6 0.0 copy-start.5
  1.3 0.0 copy-start
  1.3 0.0 copy-start.6
  1.3 5.8 %first_deposit.1 = (bf16[12,32,512]{2,1,0:T(8,128)(2,1)}, bf16[8,32,512]{2,1,0:T(8,128)(2,1)S(1)}, bf16[12,32,512]{2,1,0:T(8,128)(2,1)}, bf16[96,64,512]{2,1,0:T(8,128)(2,1)S(1)}) custom-call(s32[1,96]{1,0:T(1,128)} %atom_hbm.5, s32[1,96]{1,0:T(1,128)} %cell_hbm.5, s32[1,1]{1,0:T(1,128)S(6)} %copy.12.live_ref, bf16[32,1536]{1,0:T(8,128)(2,1)} %bitcast.11, ...), custom_call_target="tpu_custom_call" | custom-call | tf_op jit(solution)/shard_map/first_deposit/pallas_call | solution.py:139
  7.1 0.0 copy-start.1
  7.1 0.5 collective-permute-start
  7.7 2.9 %collective-permute-start.1 = (bf16[12,32,512]{2,1,0:T(8,128)(2,1)}, bf16[12,32,512]{2,1,0:T(8,128)(2,1)}, u32[]{:S(2)}, u32[]{:S(2)}) collective-permute-start(bf16[12,32,512]{2,1,0:T(8,128)(2,1)} %get-tuple-element.25.down), channel_id=1, source_target_pairs={{0,7},{1,0},{2,1},{3,2},{4,3},{5,4},{6,5},{7,6},{8,15},{9,8},{10,9... | collective-permute-start | bytes 1179656 | tf_op jit(solution)/shard_map/ppermute | solution.py:442
  10.6 0.0 copy-done.5
  10.6 0.0 slice-start
  10.6 2.8 %second_deposit.1 = (bf16[12,32,512]{2,1,0:T(8,128)(2,1)}, bf16[8,32,512]{2,1,0:T(8,128)(2,1)S(1)}, bf16[12,32,512]{2,1,0:T(8,128)(2,1)}) custom-call(s32[1,96]{1,0:T(1,128)} %atom_hbm.5, s32[1,96]{1,0:T(1,128)} %cell_hbm.5, s32[1,1]{1,0:T(1,128)S(6)} %copy.12.live_ref, bf16[32,1536]{1,0:T(8,128)(2,1)S(1)} %bitcast.10, ...), custom_call_target="tpu_custom_call" | custom-call | tf_op jit(solution)/shard_map/second_deposit/pallas_call | solution.py:154
  13.4 0.0 copy-done.1
  13.4 0.0 copy-start.3
  13.4 0.7 %copy-done.3 = bf16[8,32,512]{2,1,0:T(8,128)(2,1)} copy-done((bf16[8,32,512]{2,1,0:T(8,128)(2,1)}, bf16[8,32,512]{2,1,0:T(8,128)(2,1)S(1)}, u32[]{:S(2)}) %copy-start.3) | copy-done | bytes 262168
  14.1 0.0 collective-permute-start.4
  14.1 2.6 %collective-permute-start.5 = (bf16[12,32,512]{2,1,0:T(8,128)(2,1)}, bf16[12,32,512]{2,1,0:T(8,128)(2,1)}, u32[]{:S(2)}, u32[]{:S(2)}) collective-permute-start(bf16[12,32,512]{2,1,0:T(8,128)(2,1)} %get-tuple-element.32.down), channel_id=1, source_target_pairs={{0,7},{1,0},{2,1},{3,2},{4,3},{5,4},{6,5},{7,6},{8,15},{9,8},{10,9... | collective-permute-start | bytes 1179656 | tf_op jit(solution)/shard_map/ppermute | solution.py:442
  16.8 0.0 copy-done
  16.8 1.4 %toeplitz.1 = (bf16[3,384,192]{2,1,0:T(8,128)(2,1)S(1)}, bf16[3,384,192]{2,1,0:T(8,128)(2,1)S(1)}) custom-call(bf16[27,32,32]{2,1,0:T(8,128)(2,1)S(1)} %copy-done), custom_call_target="tpu_custom_call" | custom-call | tf_op jit(solution)/shard_map/toeplitz/pallas_call | solution.py:195
  18.2 0.0 collective-permute-done.below
  18.2 2.2 %collective-permute-done.1.above = bf16[12,32,512]{2,1,0:T(8,128)(2,1)} collective-permute-done((bf16[12,32,512]{2,1,0:T(8,128)(2,1)}, bf16[12,32,512]{2,1,0:T(8,128)(2,1)}, u32[]{:S(2)}, u32[]{:S(2)}) %collective-permute-start.1) | collective-permute-done | bytes 393248 | tf_op jit(solution)/shard_map/ppermute | solution.py:442
  20.4 0.0 copy-done.6
  20.4 0.0 copy-start.2
  20.4 0.9 %copy-done.2 = bf16[8,32,512]{2,1,0:T(8,128)(2,1)S(1)} copy-done((bf16[8,32,512]{2,1,0:T(8,128)(2,1)S(1)}, bf16[8,32,512]{2,1,0:T(8,128)(2,1)}, u32[]{:S(2)}) %copy-start.2) | copy-done | bytes 262168
  21.4 0.0 slice-start.1
  21.4 4.0 %forward.1 = (bf16[8,32,512]{2,1,0:T(8,128)(2,1)S(1)}, bf16[8,32,512]{2,1,0:T(8,128)(2,1)S(1)}, bf16[192,2048]{1,0:T(8,128)(2,1)S(1)}) custom-call(bf16[12,32,512]{2,1,0:T(8,128)(2,1)} %get-tuple-element.25.down, bf16[8,32,512]{2,1,0:T(8,128)(2,1)S(1)} %copy-done.2, bf16[12,32,512]{2,1,0:T(8,128)(2,1)} %get-tuple-element.27.up, ...), custom_call_target="tpu_custom_call" | custom-call | tf_op jit(solution)/shard_map/forward/pallas_call | solution.py:477
  25.4 1.4 %collective-permute-done.4.below = bf16[12,32,512]{2,1,0:T(8,128)(2,1)} collective-permute-done((bf16[12,32,512]{2,1,0:T(8,128)(2,1)}, bf16[12,32,512]{2,1,0:T(8,128)(2,1)}, u32[]{:S(2)}, u32[]{:S(2)}) %collective-permute-start.4) | collective-permute-done | bytes 393248 | tf_op jit(solution)/shard_map/ppermute | solution.py:442
  26.8 1.0 %collective-permute-done.5.above = bf16[12,32,512]{2,1,0:T(8,128)(2,1)} collective-permute-done((bf16[12,32,512]{2,1,0:T(8,128)(2,1)}, bf16[12,32,512]{2,1,0:T(8,128)(2,1)}, u32[]{:S(2)}, u32[]{:S(2)}) %collective-permute-start.5) | collective-permute-done | bytes 393248 | tf_op jit(solution)/shard_map/ppermute | solution.py:442
  27.8 0.0 copy-start.4
  27.8 0.9 %copy-done.4 = bf16[8,32,512]{2,1,0:T(8,128)(2,1)S(1)} copy-done((bf16[8,32,512]{2,1,0:T(8,128)(2,1)S(1)}, bf16[8,32,512]{2,1,0:T(8,128)(2,1)}, u32[]{:S(2)}) %copy-start.4) | copy-done | bytes 262168
  28.8 3.6 %gradient.1 = (f32[144,128]{1,0:T(8,128)S(1)}, f32[144,128]{1,0:T(8,128)S(1)}, bf16[192,2048]{1,0:T(8,128)(2,1)S(1)}) custom-call(s32[1]{0:T(128)} %bitcast.2.parity_ref, bf16[12,32,512]{2,1,0:T(8,128)(2,1)} %get-tuple-element.32.down, bf16[8,32,512]{2,1,0:T(8,128)(2,1)S(1)} %copy-done.4, bf16[12,32,512]{2,1,0:T(8,128)(2,1)} %get-tuple-element.34.up, ...), custom_call_target="tpu_custom_call" | custom-call | tf_op jit(solution)/shard_map/gradient/pallas_call | solution.py:489
  32.4 1.8 %collective-permute-start.8 = (f32[144,128]{1,0:T(8,128)S(1)}, f32[144,128]{1,0:T(8,128)S(1)}, u32[]{:S(2)}, u32[]{:S(2)}) collective-permute-start(f32[144,128]{1,0:T(8,128)S(1)} %get-tuple-element.43), channel_id=1, source_target_pairs={{0,1},{1,0},{2,3},{3,2},{4,5},{5,4},{6,7},{7,6},{8,9},{9,8},{10,11... | collective-permute-start | bytes 221192 | tf_op jit(solution)/shard_map/ppermute | solution.py:447
  34.2 0.9 %collective-permute-done.8 = f32[144,128]{1,0:T(8,128)S(1)} collective-permute-done((f32[144,128]{1,0:T(8,128)S(1)}, f32[144,128]{1,0:T(8,128)S(1)}, u32[]{:S(2)}, u32[]{:S(2)}) %collective-permute-start.8) | collective-permute-done | bytes 73760 | tf_op jit(solution)/shard_map/ppermute | solution.py:447
  35.2 1.6 %collective-permute-start.9 = (f32[144,128]{1,0:T(8,128)S(1)}, f32[144,128]{1,0:T(8,128)S(1)}, u32[]{:S(2)}, u32[]{:S(2)}) collective-permute-start(f32[144,128]{1,0:T(8,128)S(1)} %add.20), channel_id=1, source_target_pairs={{0,8},{8,0},{16,24},{24,16},{1,9},{9,1},{17,25},{25,17},{2,10},{10... | collective-permute-start | bytes 221192 | tf_op jit(solution)/shard_map/ppermute | solution.py:447
  36.8 3.0 %collective-permute-done.9 = f32[144,128]{1,0:T(8,128)S(1)} collective-permute-done((f32[144,128]{1,0:T(8,128)S(1)}, f32[144,128]{1,0:T(8,128)S(1)}, u32[]{:S(2)}, u32[]{:S(2)}) %collective-permute-start.9) | collective-permute-done | bytes 73760 | tf_op jit(solution)/shard_map/ppermute | solution.py:447
  39.8 2.6 %collective-permute-start.10 = (f32[144,128]{1,0:T(8,128)S(1)}, f32[144,128]{1,0:T(8,128)S(1)}, u32[]{:S(2)}, u32[]{:S(2)}) collective-permute-start(f32[144,128]{1,0:T(8,128)S(1)} %add.21), channel_id=1, source_target_pairs={{0,16},{8,24},{16,0},{24,8},{1,17},{9,25},{17,1},{25,9},{2,18},{10... | collective-permute-start | bytes 221192 | tf_op jit(solution)/shard_map/ppermute | solution.py:447
  42.4 0.0 collective-permute-start.2
  42.4 2.6 %collective-permute-start.3 = (bf16[8,32,512]{2,1,0:T(8,128)(2,1)S(1)}, bf16[8,32,512]{2,1,0:T(8,128)(2,1)S(1)}, u32[]{:S(2)}, u32[]{:S(2)}) collective-permute-start(bf16[8,32,512]{2,1,0:T(8,128)(2,1)S(1)} %get-tuple-element.30.a1), channel_id=1, source_target_pairs={{0,7},{1,0},{2,1},{3,2},{4,3},{5,4},{6,5},{7,6},{8,15},{9,8},{10,9... | collective-permute-start | bytes 786440 | tf_op jit(solution)/shard_map/ppermute | solution.py:442
  45.0 2.2 %backward.1 = (bf16[8,32,512]{2,1,0:T(8,128)(2,1)S(1)}, bf16[8,32,512]{2,1,0:T(8,128)(2,1)S(1)}) custom-call(bf16[192,2048]{1,0:T(8,128)(2,1)S(1)} %get-tuple-element.36.sums_ref, bf16[3,384,192]{2,1,0:T(8,128)(2,1)S(1)} %get-tuple-element.37.matrix_ref), custom_call_target="tpu_custom_call" | custom-call | tf_op jit(solution)/shard_map/backward/pallas_call | solution.py:499
  47.3 0.1 collective-permute-start.6
  47.3 2.6 %collective-permute-start.7 = (bf16[8,32,512]{2,1,0:T(8,128)(2,1)S(1)}, bf16[8,32,512]{2,1,0:T(8,128)(2,1)S(1)}, u32[]{:S(2)}, u32[]{:S(2)}) collective-permute-start(bf16[8,32,512]{2,1,0:T(8,128)(2,1)S(1)} %get-tuple-element.39.b1), channel_id=1, source_target_pairs={{0,7},{1,0},{2,1},{3,2},{4,3},{5,4},{6,5},{7,6},{8,15},{9,8},{10,9... | collective-permute-start | bytes 786440 | tf_op jit(solution)/shard_map/ppermute | solution.py:442
  50.0 0.0 collective-permute-done.10
  50.0 1.1 %collective-permute-start.11 = (f32[144,128]{1,0:T(8,128)S(1)}, f32[144,128]{1,0:T(8,128)S(1)}, u32[]{:S(2)}, u32[]{:S(2)}) collective-permute-start(f32[144,128]{1,0:T(8,128)S(1)} %add.22), channel_id=1, source_target_pairs={{0,4},{1,5},{2,6},{3,7},{4,0},{5,1},{6,2},{7,3},{8,12},{9,13},{10,... | collective-permute-start | bytes 221192 | tf_op jit(solution)/shard_map/ppermute | solution.py:447
  51.0 4.1 %collective-permute-done.11 = f32[144,128]{1,0:T(8,128)S(1)} collective-permute-done((f32[144,128]{1,0:T(8,128)S(1)}, f32[144,128]{1,0:T(8,128)S(1)}, u32[]{:S(2)}, u32[]{:S(2)}) %collective-permute-start.11) | collective-permute-done | bytes 73760 | tf_op jit(solution)/shard_map/ppermute | solution.py:447
  55.2 0.6 collective-permute-start.12
  55.8 3.8 %collective-permute-done.12 = f32[144,128]{1,0:T(8,128)S(1)} collective-permute-done((f32[144,128]{1,0:T(8,128)S(1)}, f32[144,128]{1,0:T(8,128)S(1)}, u32[]{:S(2)}, u32[]{:S(2)}) %collective-permute-start.12) | collective-permute-done | bytes 73760 | tf_op jit(solution)/shard_map/ppermute | solution.py:447
  59.6 0.1 collective-permute-start.13
  59.7 0.0 collective-permute-done.2.a0
  59.7 0.0 collective-permute-done.3.a3
  59.7 0.0 collective-permute-done.6.b0
  59.7 0.0 collective-permute-done.7.b3
  59.8 0.0 slice-done
  59.8 0.0 slice-done.1
  59.8 3.4 %gather.1 = (bf16[32,1536]{1,0:T(8,128)(2,1)}, bf16[32,1536]{1,0:T(8,128)(2,1)}) custom-call(s32[1,96]{1,0:T(1,128)} %atom_hbm.5, s32[1,96]{1,0:T(1,128)} %cell_hbm.5, s32[1,1]{1,0:T(1,128)S(6)} %copy.12.live_ref, bf16[96,64,512]{2,1,0:T(8,128)(2,1)S(1)} %bitcast.9, bf16[32,32]{1,0:T(8,128)(2,1)S(1)} %copy-done.6, ...), custom_call_target="tpu_custom_call" | custom-call | tf_op jit(solution)/shard_map/gather/pallas_call | solution.py:392
  63.2 0.0 collective-permute-done.13.other_ref
  63.2 1.6 %finish.1 = (f32[27,32,32]{2,1,0:T(8,128)}, f32[32,32]{1,0:T(8,128)}) custom-call(s32[1]{0:T(128)} %bitcast.2.parity_ref, f32[144,128]{1,0:T(8,128)S(1)} %add.24.mine_ref, f32[144,128]{1,0:T(8,128)S(1)} %collective-permute-done.13.other_ref, bf16[32,32]{1,0:T(8,128)(2,1)S(1)} %copy-done.6, bf16[27,32,32]{2,1,0:T(8,128)(2,1)S(1)} %copy-done), custom_call_target="tpu_custom_call" | custom-call | tf_op jit(solution)/shard_map/finish/pallas_call | solution.py:522
  (6 shorter events, 0.1 us)
Async XLA Ops:
  0.6 10.0 %copy-start.5 = (bf16[1,32,1536]{2,1,0:T(8,128)(2,1)S(1)}, bf16[1,32,1536]{2,1,0:T(8,128)(2,1)}, u32[]{:S(2)}) copy-start(bf16[1,32,1536]{2,1,0:T(8,128)(2,1)} %param.15) | copy-start | bytes 294916
  1.3 15.5 %copy-start = (bf16[27,32,32]{2,1,0:T(8,128)(2,1)S(1)}, bf16[27,32,32]{2,1,0:T(8,128)(2,1)}, u32[]{:S(2)}) copy-start(bf16[27,32,32]{2,1,0:T(8,128)(2,1)} %conv_ref.3) | copy-start | bytes 165892
  1.3 19.1 %copy-start.6 = (bf16[32,32]{1,0:T(8,128)(2,1)S(1)}, bf16[32,32]{1,0:T(8,128)(2,1)}, u32[]{:S(2)}) copy-start(bf16[32,32]{1,0:T(8,128)(2,1)} %mix_ref.5) | copy-start | bytes 6148
  7.1 6.3 %copy-start.1 = (bf16[8,32,512]{2,1,0:T(8,128)(2,1)}, bf16[8,32,512]{2,1,0:T(8,128)(2,1)S(1)}, u32[]{:S(2)}) copy-start(bf16[8,32,512]{2,1,0:T(8,128)(2,1)S(1)} %get-tuple-element.26.middle) | copy-start | bytes 786436
  7.1 11.1 %collective-permute-start = (bf16[12,32,512]{2,1,0:T(8,128)(2,1)}, bf16[12,32,512]{2,1,0:T(8,128)(2,1)}, u32[]{:S(2)}, u32[]{:S(2)}) collective-permute-start(bf16[12,32,512]{2,1,0:T(8,128)(2,1)} %get-tuple-element.27.up), channel_id=1, source_target_pairs={{0,1},{1,2},{2,3},{3,4},{4,5},{5,6},{6,7},{7,0},{8,9},{9,10},{10,1... | collective-permute-start | bytes 1179656 | tf_op jit(solution)/shard_map/ppermute | solution.py:442
  7.7 12.8 %collective-permute-start.1 = (bf16[12,32,512]{2,1,0:T(8,128)(2,1)}, bf16[12,32,512]{2,1,0:T(8,128)(2,1)}, u32[]{:S(2)}, u32[]{:S(2)}) collective-permute-start(bf16[12,32,512]{2,1,0:T(8,128)(2,1)} %get-tuple-element.25.down), channel_id=1, source_target_pairs={{0,7},{1,0},{2,1},{3,2},{4,3},{5,4},{6,5},{7,6},{8,15},{9,8},{10,9... | collective-permute-start | bytes 1179656 | tf_op jit(solution)/shard_map/ppermute | solution.py:442
  10.6 49.2 %slice-start = ((s8[6291456]{0:T(1024)(128)(4,1)}), s8[2097152]{0:T(1024)(128)(4,1)S(1)}, s32[]{:S(2)}) async-start(s8[6291456]{0:T(1024)(128)(4,1)} %bitcast.7), calls=%async_computation | async-start | bytes 4194304
  13.4 0.7 %copy-start.3 = (bf16[8,32,512]{2,1,0:T(8,128)(2,1)}, bf16[8,32,512]{2,1,0:T(8,128)(2,1)S(1)}, u32[]{:S(2)}) copy-start(bf16[8,32,512]{2,1,0:T(8,128)(2,1)S(1)} %get-tuple-element.33.middle) | copy-start | bytes 786436
  14.1 12.6 %collective-permute-start.4 = (bf16[12,32,512]{2,1,0:T(8,128)(2,1)}, bf16[12,32,512]{2,1,0:T(8,128)(2,1)}, u32[]{:S(2)}, u32[]{:S(2)}) collective-permute-start(bf16[12,32,512]{2,1,0:T(8,128)(2,1)} %get-tuple-element.34.up), channel_id=1, source_target_pairs={{0,1},{1,2},{2,3},{3,4},{4,5},{5,6},{6,7},{7,0},{8,9},{9,10},{10,1... | collective-permute-start | bytes 1179656 | tf_op jit(solution)/shard_map/ppermute | solution.py:442
  14.1 13.7 %collective-permute-start.5 = (bf16[12,32,512]{2,1,0:T(8,128)(2,1)}, bf16[12,32,512]{2,1,0:T(8,128)(2,1)}, u32[]{:S(2)}, u32[]{:S(2)}) collective-permute-start(bf16[12,32,512]{2,1,0:T(8,128)(2,1)} %get-tuple-element.32.down), channel_id=1, source_target_pairs={{0,7},{1,0},{2,1},{3,2},{4,3},{5,4},{6,5},{7,6},{8,15},{9,8},{10,9... | collective-permute-start | bytes 1179656 | tf_op jit(solution)/shard_map/ppermute | solution.py:442
  20.4 1.0 %copy-start.2 = (bf16[8,32,512]{2,1,0:T(8,128)(2,1)S(1)}, bf16[8,32,512]{2,1,0:T(8,128)(2,1)}, u32[]{:S(2)}) copy-start(bf16[8,32,512]{2,1,0:T(8,128)(2,1)} %copy-done.1) | copy-start | bytes 786436
  21.4 38.4 %slice-start.1 = ((s8[6291456]{0:T(1024)(128)(4,1)}), s8[4194304]{0:T(1024)(128)(4,1)S(1)}, s32[]{:S(2)}) async-start(s8[6291456]{0:T(1024)(128)(4,1)} %bitcast.7), calls=%async_computation.1 | async-start | bytes 8388608
  27.8 0.9 %copy-start.4 = (bf16[8,32,512]{2,1,0:T(8,128)(2,1)S(1)}, bf16[8,32,512]{2,1,0:T(8,128)(2,1)}, u32[]{:S(2)}) copy-start(bf16[8,32,512]{2,1,0:T(8,128)(2,1)} %copy-done.3) | copy-start | bytes 786436
  32.4 2.7 %collective-permute-start.8 = (f32[144,128]{1,0:T(8,128)S(1)}, f32[144,128]{1,0:T(8,128)S(1)}, u32[]{:S(2)}, u32[]{:S(2)}) collective-permute-start(f32[144,128]{1,0:T(8,128)S(1)} %get-tuple-element.43), channel_id=1, source_target_pairs={{0,1},{1,0},{2,3},{3,2},{4,5},{5,4},{6,7},{7,6},{8,9},{9,8},{10,11... | collective-permute-start | bytes 221192 | tf_op jit(solution)/shard_map/ppermute | solution.py:447
  35.2 4.6 %collective-permute-start.9 = (f32[144,128]{1,0:T(8,128)S(1)}, f32[144,128]{1,0:T(8,128)S(1)}, u32[]{:S(2)}, u32[]{:S(2)}) collective-permute-start(f32[144,128]{1,0:T(8,128)S(1)} %add.20), channel_id=1, source_target_pairs={{0,8},{8,0},{16,24},{24,16},{1,9},{9,1},{17,25},{25,17},{2,10},{10... | collective-permute-start | bytes 221192 | tf_op jit(solution)/shard_map/ppermute | solution.py:447
  39.8 10.2 %collective-permute-start.10 = (f32[144,128]{1,0:T(8,128)S(1)}, f32[144,128]{1,0:T(8,128)S(1)}, u32[]{:S(2)}, u32[]{:S(2)}) collective-permute-start(f32[144,128]{1,0:T(8,128)S(1)} %add.21), channel_id=1, source_target_pairs={{0,16},{8,24},{16,0},{24,8},{1,17},{9,25},{17,1},{25,9},{2,18},{10... | collective-permute-start | bytes 221192 | tf_op jit(solution)/shard_map/ppermute | solution.py:447
  42.4 17.3 %collective-permute-start.2 = (bf16[8,32,512]{2,1,0:T(8,128)(2,1)S(1)}, bf16[8,32,512]{2,1,0:T(8,128)(2,1)S(1)}, u32[]{:S(2)}, u32[]{:S(2)}) collective-permute-start(bf16[8,32,512]{2,1,0:T(8,128)(2,1)S(1)} %get-tuple-element.29.a2), channel_id=1, source_target_pairs={{0,1},{1,2},{2,3},{3,4},{4,5},{5,6},{6,7},{7,0},{8,9},{9,10},{10,1... | collective-permute-start | bytes 786440 | tf_op jit(solution)/shard_map/ppermute | solution.py:442
  42.4 17.3 %collective-permute-start.3 = (bf16[8,32,512]{2,1,0:T(8,128)(2,1)S(1)}, bf16[8,32,512]{2,1,0:T(8,128)(2,1)S(1)}, u32[]{:S(2)}, u32[]{:S(2)}) collective-permute-start(bf16[8,32,512]{2,1,0:T(8,128)(2,1)S(1)} %get-tuple-element.30.a1), channel_id=1, source_target_pairs={{0,7},{1,0},{2,1},{3,2},{4,3},{5,4},{6,5},{7,6},{8,15},{9,8},{10,9... | collective-permute-start | bytes 786440 | tf_op jit(solution)/shard_map/ppermute | solution.py:442
  47.3 12.5 %collective-permute-start.6 = (bf16[8,32,512]{2,1,0:T(8,128)(2,1)S(1)}, bf16[8,32,512]{2,1,0:T(8,128)(2,1)S(1)}, u32[]{:S(2)}, u32[]{:S(2)}) collective-permute-start(bf16[8,32,512]{2,1,0:T(8,128)(2,1)S(1)} %get-tuple-element.38.b2), channel_id=1, source_target_pairs={{0,1},{1,2},{2,3},{3,4},{4,5},{5,6},{6,7},{7,0},{8,9},{9,10},{10,1... | collective-permute-start | bytes 786440 | tf_op jit(solution)/shard_map/ppermute | solution.py:442
  47.3 12.4 %collective-permute-start.7 = (bf16[8,32,512]{2,1,0:T(8,128)(2,1)S(1)}, bf16[8,32,512]{2,1,0:T(8,128)(2,1)S(1)}, u32[]{:S(2)}, u32[]{:S(2)}) collective-permute-start(bf16[8,32,512]{2,1,0:T(8,128)(2,1)S(1)} %get-tuple-element.39.b1), channel_id=1, source_target_pairs={{0,7},{1,0},{2,1},{3,2},{4,3},{5,4},{6,5},{7,6},{8,15},{9,8},{10,9... | collective-permute-start | bytes 786440 | tf_op jit(solution)/shard_map/ppermute | solution.py:442
  50.0 5.2 %collective-permute-start.11 = (f32[144,128]{1,0:T(8,128)S(1)}, f32[144,128]{1,0:T(8,128)S(1)}, u32[]{:S(2)}, u32[]{:S(2)}) collective-permute-start(f32[144,128]{1,0:T(8,128)S(1)} %add.22), channel_id=1, source_target_pairs={{0,4},{1,5},{2,6},{3,7},{4,0},{5,1},{6,2},{7,3},{8,12},{9,13},{10,... | collective-permute-start | bytes 221192 | tf_op jit(solution)/shard_map/ppermute | solution.py:447
  55.2 4.4 %collective-permute-start.12 = (f32[144,128]{1,0:T(8,128)S(1)}, f32[144,128]{1,0:T(8,128)S(1)}, u32[]{:S(2)}, u32[]{:S(2)}) collective-permute-start(f32[144,128]{1,0:T(8,128)S(1)} %add.23), channel_id=1, source_target_pairs={{0,2},{1,3},{2,0},{3,1},{4,6},{5,7},{6,4},{7,5},{8,10},{9,11},{10,... | collective-permute-start | bytes 221192 | tf_op jit(solution)/shard_map/ppermute | solution.py:447
  59.6 3.6 %collective-permute-start.13 = (f32[144,128]{1,0:T(8,128)S(1)}, f32[144,128]{1,0:T(8,128)S(1)}, u32[]{:S(2)}, u32[]{:S(2)}) collective-permute-start(f32[144,128]{1,0:T(8,128)S(1)} %add.24.mine_ref), channel_id=1, source_target_pairs={{0,1},{1,0},{2,3},{3,2},{4,5},{5,4},{6,7},{7,6},{8,9},{9,8},{10,11... | collective-permute-start | bytes 221192 | tf_op jit(solution)/shard_map/ppermute | solution.py:447
where the time goes:
time: 65 us; the launch traced here: 64.8 us
  Pallas kernels  24.7 us (38%)
  starting transfers between devices  19.3 us (30%)
  waiting for transfers between devices  16.5 us (25%)
  local copies, waits for them, and re-layouts  2.62 us (4%)
  between operations  1.54 us (2%)
    ppermute x6, waiting for transfers between devices, exchanged(): return lax.ppermute(value, axis, [(i, i ^ stride) for i in range(count)])  11.8 us
    ppermute x8, starting transfers between devices, ring(): return lax.ppermute(value, axis, pairs)  11.5 us
    ppermute x6, starting transfers between devices, exchanged(): return lax.ppermute(value, axis, [(i, i ^ stride) for i in range(count)])  7.85 us
    pallas_call x1, Pallas kernels, first_deposit(): pl.pallas_call(first_deposit_kernel, in_specs=list_specs() + [hbm()] * 2,...  5.75 us
    ppermute x8, waiting for transfers between devices, ring(): return lax.ppermute(value, axis, pairs)  4.65 us
    pallas_call x1, Pallas kernels, step(): pl.pallas_call(forward_kernel, in_specs=[whole()] * 7, out_specs=[whole()...  3.98 us
    pallas_call x1, Pallas kernels, step(): pl.pallas_call(gradient_kernel, in_specs=[smem] + [whole()] * 6, out_spec...  3.63 us
    pallas_call x1, Pallas kernels, gather(): pl.pallas_call(gather_kernel, in_specs=list_specs() + [whole()] * 10, out...  3.39 us
  transfers between devices with their start and end apart: 14, of which 7 were waited for; matrix products, arithmetic and copies ran while one was open for 0% of the time, Pallas kernels for 21%

commit v1 on v0

--- a/solution.py
+++ b/solution.py
@@ -84,9 +84,9 @@
 
 def second_deposit_kernel(
     atom_hbm, cell_hbm, live_ref, cot_ref, weight_ref,
-    down_ref, middle_ref, up_ref,
-    atom_ref, cell_ref, small_sems, source, total,
-):
+    *rest,
+):
+    *parts, atom_ref, cell_ref, small_sems, source, total = rest
     small = copies(((atom_hbm, atom_ref), (cell_hbm, cell_ref)), small_sems)
     for copy in small:
         copy.start()
@@ -96,7 +96,7 @@
         copy.wait()
     tiles = slice(0, weight_ref.shape[0])
     add_tiles(tiles, atom_ref, cell_ref, live_ref[0, 0], source, weight_ref, total)
-    write_parts(total, (down_ref, middle_ref, up_ref))
+    write_parts(total, parts)
 
 
 def in_hbm(*values):
@@ -119,13 +119,13 @@
     return [hbm(), hbm(), pl.BlockSpec(memory_space=pltpu.SMEM)]
 
 
-def deposit_shapes(field, weights):
+def deposit_shapes(field, weights, planes_of):
     channels, atoms = field.shape
     _, tile_a, tile_c = weights.shape
     quarters = GY * GX // tile_c
     parts = [
-        jax.ShapeDtypeStruct((planes * quarters, channels, tile_c), BF16)
-        for planes in (ZH + 1, ZD - 2, ZH + 1)
+        pltpu.VMEM((planes * quarters, channels, tile_c), BF16)
+        for planes in planes_of
     ]
     scratch = [
         pltpu.VMEM((atoms // tile_a, channels, tile_a), BF16),
@@ -135,12 +135,12 @@
 
 
 def first_deposit(feats, weights, atom_ids, cell_ids, live):
-    parts, scratch = deposit_shapes(feats, weights)
+    parts, scratch = deposit_shapes(feats, weights, (ZH + 1, ZD - 2, ZH + 1))
     return pl.pallas_call(
         first_deposit_kernel,
         in_specs=list_specs() + [hbm()] * 2,
         out_specs=[whole()] * 4,
-        out_shape=parts + [jax.ShapeDtypeStruct(weights.shape, BF16)],
+        out_shape=parts + [pltpu.VMEM(weights.shape, BF16)],
         scratch_shapes=list_scratch(atom_ids, cell_ids)
         + scratch
         + [pltpu.VMEM(feats.shape, BF16), pltpu.SemaphoreType.DMA((8,))],
@@ -150,11 +150,11 @@
 
 
 def second_deposit(cot, weights, atom_ids, cell_ids, live):
-    parts, scratch = deposit_shapes(cot, weights)
+    parts, scratch = deposit_shapes(cot, weights, (ZH, 1, ZD - 2, 1, ZH))
     return pl.pallas_call(
         second_deposit_kernel,
         in_specs=list_specs() + [whole()] * 2,
-        out_specs=[whole()] * 3,
+        out_specs=[whole()] * len(parts),
         out_shape=parts,
         scratch_shapes=list_scratch(atom_ids, cell_ids) + scratch,
         compiler_params=params(),
@@ -191,7 +191,7 @@
 
 def toeplitz(conv_w):
     channels = conv_w.shape[1]
-    shape = jax.ShapeDtypeStruct((3, 3 * ZD * channels, (ZD + 2) * channels), BF16)
+    shape = pltpu.VMEM((3, 3 * ZD * channels, (ZD + 2) * channels), BF16)
     return pl.pallas_call(
         toeplitz_kernel,
         in_specs=[whole()],
@@ -202,17 +202,18 @@
     )(conv_w)
 
 
-def joined_planes(down, middle, up, from_below, from_above):
-    quarters = middle.shape[0] // (ZD - 2)
-    own = [down[q] for q in range(quarters, 3 * quarters)]
-    own += [middle[q] for q in range(2 * quarters)]
-    own += [up[q] for q in range(2 * quarters)]
-    other = [from_below[q] for q in range(3 * quarters)]
-    other += [from_above[q] for q in range(3 * quarters)]
-    sums = [a.astype(F32) + b.astype(F32) for a, b in zip(own, other)]
+def joined_planes(own, other, quarters):
+    def blocks(pieces):
+        return [
+            ref[q]
+            for ref, first, count in pieces
+            for q in range(first * quarters, (first + count) * quarters)
+        ]
+
+    sums = [a.astype(F32) + b.astype(F32) for a, b in zip(blocks(own), blocks(other))]
     return [
-        jnp.concatenate(sums[p * quarters : (p + 1) * quarters], axis=1)
-        for p in range(ZD + 2)
+        jnp.concatenate(sums[i : i + quarters], axis=1)
+        for i in range(0, len(sums), quarters)
     ]
 
 
@@ -272,7 +273,10 @@
     low_ref, high_ref, plain_ref, shifted, partial,
 ):
     channels = mix_ref.shape[0]
-    for p, plane in enumerate(joined_planes(down, middle, up, below, above)):
+    quarters = low_ref.shape[0] // ZH
+    own = ((down, 1, ZH), (middle, 0, ZD - 2), (up, 0, ZH))
+    other = ((below, 0, ZH + 1), (above, 0, ZH + 1))
+    for p, plane in enumerate(joined_planes(own, other, quarters)):
         plane = plane.astype(BF16)
         plain_ref[p * channels : (p + 1) * channels] = plane
         mixed = jnp.dot(mix_ref[...], plane, preferred_element_type=F32)
@@ -281,21 +285,21 @@
 
 
 def gradient_kernel(
-    parity_ref, down, middle, up, below, above, plain_ref,
+    low, middle, high, below, above, plain_ref,
     keep_ref, send_ref, sums_ref, shifted, upstream,
 ):
-    channels = down.shape[1]
+    channels = low.shape[1]
+    quarters = low.shape[0]
     cells = plain_ref.shape[1]
     for p in range(ZD + 2):
         rows = slice(p * channels, (p + 1) * channels)
         store_shifted(shifted, p * channels, plain_ref[rows].astype(F32))
-    planes = joined_planes(down, middle, up, below, above)
+    own = ((low, 0, 1), (middle, 0, ZD - 2), (high, 0, 1))
+    planes = joined_planes(own, ((below, 0, ZH), (above, 0, ZH)), quarters)
     third = ZD * channels
-    for p in range(ZD + 2):
-        sums_ref[p * channels : (p + 1) * channels] = planes[p].astype(BF16)
-    for p in range(ZD):
-        plane = planes[p + 1]
+    for p, plane in enumerate(planes):
         row = p * channels
+        sums_ref[row : row + channels] = plane.astype(BF16)
         upstream[row : row + channels] = pltpu.roll(plane, cells - GX, 1).astype(BF16)
         upstream[third + row : third + row + channels] = plane.astype(BF16)
         upstream[2 * third + row : 2 * third + row + channels] = pltpu.roll(
@@ -324,24 +328,31 @@
     half = keep_ref.shape[0]
     grads = jnp.concatenate(blocks, axis=0)
     first, second = grads[:half], grads[half:]
-    odd = parity_ref[0] == 1
+    odd = lax.rem(lax.axis_index("slab"), 2) == 1
 
     @pl.when(odd)
     def _():
-        keep_ref[...] = second
-        send_ref[...] = first
+        keep_ref[...] = second.astype(keep_ref.dtype)
+        send_ref[...] = first.astype(send_ref.dtype)
 
     @pl.when(jnp.logical_not(odd))
     def _():
-        keep_ref[...] = first
-        send_ref[...] = second
-
-
-def backward_kernel(sums_ref, matrix_ref, low_ref, high_ref, shifted, partial):
+        keep_ref[...] = first.astype(keep_ref.dtype)
+        send_ref[...] = second.astype(send_ref.dtype)
+
+
+def backward_kernel(
+    down, up, below, above, sums_ref, matrix_ref, low_ref, high_ref, shifted, partial
+):
     channels = low_ref.shape[1]
-    for p in range(ZD + 2):
+    quarters = below.shape[0]
+    (first,) = joined_planes(((down, 1, 1),), ((below, 0, 1),), quarters)
+    (last,) = joined_planes(((up, 0, 1),), ((above, 0, 1),), quarters)
+    store_shifted(shifted, 0, first.astype(BF16).astype(F32))
+    for p in range(ZD):
         rows = slice(p * channels, (p + 1) * channels)
-        store_shifted(shifted, p * channels, sums_ref[rows].astype(F32))
+        store_shifted(shifted, (p + 1) * channels, sums_ref[rows].astype(F32))
+    store_shifted(shifted, (ZD + 1) * channels, last.astype(BF16).astype(F32))
     conv_planes(matrix_ref, shifted, partial, low_ref, high_ref)
 
 
@@ -405,12 +416,12 @@
 
 
 def finish_kernel(
-    parity_ref, mine_ref, other_ref, mix_ref, conv_ref, conv_out, mix_out,
+    mine_ref, other_ref, mix_ref, conv_ref, conv_out, mix_out,
     *, conv_scale, mix_scale,
 ):
     channels = mix_ref.shape[0]
-    mine, other = mine_ref[...], other_ref[...]
-    odd = parity_ref[0] == 1
+    mine, other = mine_ref[...].astype(F32), other_ref[...].astype(F32)
+    odd = lax.rem(lax.axis_index("slab"), 2) == 1
     total = jnp.concatenate(
         [jnp.where(odd, other, mine), jnp.where(odd, mine, other)], axis=0
     )
@@ -439,7 +450,9 @@
 def ring(value, axis, steps):
     count = lax.axis_size(axis)
     pairs = [(source, (source + steps) % count) for source in range(count)]
-    return lax.ppermute(value, axis, pairs)
+    return pltpu.with_memory_space_constraint(
+        lax.ppermute(value, axis, pairs), pltpu.VMEM
+    )
 
 
 def exchanged(value, axis, stride):
@@ -460,15 +473,15 @@
     quarters = GY * GX // tile_c
     cells = GY * GX
     smem = pl.BlockSpec(memory_space=pltpu.SMEM)
-    parity = jnp.reshape(lax.axis_index("slab") % 2, (1,)).astype(jnp.int32)
 
     dd, dm, du, held = first_deposit(feats, weights, atom_ids, cell_ids, live)
     d_below, d_above = ring(du, "slab", 1), ring(dd, "slab", -1)
-    ed, em, eu = second_deposit(cot, held, atom_ids, cell_ids, live)
+    ed, el, em, eh, eu = second_deposit(cot, held, atom_ids, cell_ids, live)
     e_below, e_above = ring(eu, "slab", 1), ring(ed, "slab", -1)
+    f_below, f_above = ring(eh, "slab", 1), ring(el, "slab", -1)
     forward, backward = toeplitz(conv_w)
 
-    half = jax.ShapeDtypeStruct((ZH * quarters, channels, tile_c), BF16)
+    half = pltpu.VMEM((ZH * quarters, channels, tile_c), BF16)
     rows = (ZD + 2) * channels
     scratch = [
         pltpu.VMEM((3 * rows, cells), BF16),
@@ -478,44 +491,44 @@
         forward_kernel,
         in_specs=[whole()] * 7,
         out_specs=[whole()] * 3,
-        out_shape=[half, half, jax.ShapeDtypeStruct((rows, cells), BF16)],
+        out_shape=[half, half, pltpu.VMEM((rows, cells), BF16)],
         scratch_shapes=scratch,
         compiler_params=params(),
         name="forward",
     )(dd, dm, du, d_below, d_above, w_mix, forward)
     phi_below, phi_above = ring(phi_high, "slab", 1), ring(phi_low, "slab", -1)
 
-    part = jax.ShapeDtypeStruct((9 * channels // 2, 4 * channels), F32)
+    part = pltpu.VMEM((9 * channels // 2, 4 * channels), BF16)
     keep, send, sums = pl.pallas_call(
         gradient_kernel,
-        in_specs=[smem] + [whole()] * 6,
+        in_specs=[whole()] * 6,
         out_specs=[whole()] * 3,
-        out_shape=[part, part, jax.ShapeDtypeStruct((rows, cells), BF16)],
+        out_shape=[part, part, pltpu.VMEM((ZD * channels, cells), BF16)],
         scratch_shapes=[scratch[0], pltpu.VMEM((3 * ZD * channels, cells), BF16)],
         compiler_params=params(),
         name="gradient",
-    )(parity, ed, em, eu, e_below, e_above, plain)
+    )(el, em, eh, e_below, e_above, plain)
     arrived = exchanged(send, "slab", 1)
     drho_low, drho_high = pl.pallas_call(
         backward_kernel,
-        in_specs=[whole()] * 2,
+        in_specs=[whole()] * 6,
         out_specs=[whole()] * 2,
         out_shape=[half, half],
         scratch_shapes=scratch,
         compiler_params=params(),
         name="backward",
-    )(sums, backward)
+    )(ed, eu, f_below, f_above, sums, backward)
     drho_below, drho_above = ring(drho_high, "slab", 1), ring(drho_low, "slab", -1)
 
     total = keep + arrived
-    for axis, first in (("rep", 1), ("slab", 4), ("slab", 2)):
-        stride = first
-        while stride < lax.axis_size(axis) and (axis == "rep" or stride == 2 or stride >= 4):
-            arrived = exchanged(total, axis, stride)
-            total = total + arrived
-            if stride == 2 and axis == "slab":
-                break
-            stride *= 2
+    turns = [("rep", 1 << i) for i in range((lax.axis_size("rep") - 1).bit_length())]
+    turns += [
+        ("slab", 1 << i)
+        for i in reversed(range(1, (lax.axis_size("slab") - 1).bit_length()))
+    ]
+    for axis, stride in turns:
+        arrived = exchanged(total, axis, stride)
+        total = total + arrived
     other = exchanged(total, "slab", 1)
 
     groups = lax.axis_size("rep") * lax.axis_size("slab")
@@ -525,7 +538,7 @@
             conv_scale=math.sqrt(groups * ZD * cells),
             mix_scale=math.sqrt(groups * atoms),
         ),
-        in_specs=[smem] + [whole()] * 4,
+        in_specs=[whole()] * 4,
         out_specs=[whole()] * 2,
         out_shape=[
             jax.ShapeDtypeStruct(conv_w.shape, F32),
@@ -533,7 +546,7 @@
         ],
         compiler_params=params(),
         name="finish",
-    )(parity, total, other, w_mix, conv_w)
+    )(total, other, w_mix, conv_w)
 
     potential, feats_grad = gather(
         (phi_below, phi_low, phi_high, phi_above),

time: 65 us -> 60.8 us (0.935)
  Pallas kernels: 24.7 us -> 20.2 us
  waiting for transfers between devices: 16.5 us -> 19.4 us
  local copies, waits for them, and re-layouts: 2.62 us -> 0.02 us
    ppermute x6, starting transfers between devices: 7.85 us -> 4.91 us  [exchanged(): return lax.ppermute(value, axis, [(i, i ^ stride) for i in range(count)])]
    ppermute x8 -> x10, starting transfers between devices: 11.5 us -> 14.3 us  [ring(): lax.ppermute(value, axis, pairs)]
    ppermute x6, waiting for transfers between devices: 11.8 us -> 14.6 us  [exchanged(): return lax.ppermute(value, axis, [(i, i ^ stride) for i in range(count)])]
    unnamed x18 -> x10, local copies, waits for them, and re-layouts: 2.62 us -> 0.02 us
    pallas_call x1, Pallas kernels: 3.98 us -> 2.38 us  [step(): pl.pallas_call(forward_kernel, in_specs=[whole()] * 7, out_specs=[whole()...]
    pallas_call x2, Pallas kernels: 5.84 us -> 4.42 us  [the longest x1 2.21 us: step(): pl.pallas_call(backward_kernel, in_specs=[whole()] * 6, out_specs=[whole(...]
    pallas_call x1, Pallas kernels: 2.8 us -> 1.97 us  [second_deposit(): pl.pallas_call(second_deposit_kernel, in_specs=list_specs() + [whole()] *...]
    pallas_call x1, Pallas kernels: 5.75 us -> 5.03 us  [first_deposit(): pl.pallas_call(first_deposit_kernel, in_specs=list_specs() + [hbm()] * 2,...]
  transfers between devices with their start and end apart: 14 -> 16, of which waited for: 7 -> 7; matrix products, arithmetic and copies ran while one was open for 0% -> 0% of each run, Pallas kernels for 21% -> 19%
where the time goes in v1:
time: 60.8 us; the launch traced here: 60.6 us
  Pallas kernels  20.2 us (33%)
  waiting for transfers between devices  19.4 us (32%)
  starting transfers between devices  19.2 us (32%)
  between operations  1.69 us (3%)
    ppermute x6, waiting for transfers between devices, exchanged(): return lax.ppermute(value, axis, [(i, i ^ stride) for i in range(count)])  14.6 us
    ppermute x10, starting transfers between devices, ring(): lax.ppermute(value, axis, pairs)  14.3 us
    pallas_call x1, Pallas kernels, first_deposit(): pl.pallas_call(first_deposit_kernel, in_specs=list_specs() + [hbm()] * 2,...  5.03 us
    ppermute x6, starting transfers between devices, exchanged(): return lax.ppermute(value, axis, [(i, i ^ stride) for i in range(count)])  4.91 us
    ppermute x10, waiting for transfers between devices, ring(): lax.ppermute(value, axis, pairs)  4.85 us
    pallas_call x1, Pallas kernels, gather(): pl.pallas_call(gather_kernel, in_specs=list_specs() + [whole()] * 10, out...  3.39 us
    pallas_call x1, Pallas kernels, step(): pl.pallas_call(forward_kernel, in_specs=[whole()] * 7, out_specs=[whole()...  2.38 us
    pallas_call x1, Pallas kernels, step(): pl.pallas_call(backward_kernel, in_specs=[whole()] * 6, out_specs=[whole(...  2.21 us
  transfers between devices with their start and end apart: 16, of which 7 were waited for; matrix products, arithmetic and copies ran while one was open for 0% of the time, Pallas kernels for 19%

profile of v1, /device:TPU:0, one launch (start us, length us, event | category | flops | bytes accessed | tf_op | source)
XLA Modules:
  0.0 60.6 jit_solution(13496425369851884078)
XLA Ops:
  0.6 0.0 copy-start.1
  1.3 0.0 copy-start
  1.3 0.0 copy-start.2
  1.3 0.0 slice-start
  1.4 5.0 %first_deposit.1 = (bf16[12,32,512]{2,1,0:T(8,128)(2,1)S(1)}, bf16[8,32,512]{2,1,0:T(8,128)(2,1)S(1)}, bf16[12,32,512]{2,1,0:T(8,128)(2,1)S(1)}, bf16[96,64,512]{2,1,0:T(8,128)(2,1)S(1)}) custom-call(s32[1,96]{1,0:T(1,128)} %atom_hbm.5, s32[1,96]{1,0:T(1,128)} %cell_hbm.5, s32[1,1]{1,0:T(1,128)S(6)} %copy.12.live_ref, bf16[32,1536]{1,0:T(8,128)(2,1)} %bitcast.10, ...), custom_call_target="tpu_custom_call" | custom-call | tf_op jit(solution)/shard_map/first_deposit/pallas_call | solution.py:139
  6.4 3.4 %collective-permute-start.1 = (bf16[12,32,512]{2,1,0:T(8,128)(2,1)S(1)}, bf16[12,32,512]{2,1,0:T(8,128)(2,1)S(1)}, u32[]{:S(2)}, u32[]{:S(2)}) collective-permute-start(bf16[12,32,512]{2,1,0:T(8,128)(2,1)S(1)} %get-tuple-element.27.down), channel_id=1, source_target_pairs={{0,7},{1,0},{2,1},{3,2},{4,3},{5,4},{6,5},{7,6},{8,15},{9,8},{10,9... | collective-permute-start | bytes 1179656 | tf_op jit(solution)/shard_map/ppermute | solution.py:454
  9.8 0.0 collective-permute-start
  9.8 0.0 copy-done.1
  9.8 0.0 slice-start.1
  9.8 2.0 %second_deposit.1 = (bf16[8,32,512]{2,1,0:T(8,128)(2,1)S(1)}, bf16[4,32,512]{2,1,0:T(8,128)(2,1)S(1)}, bf16[8,32,512]{2,1,0:T(8,128)(2,1)S(1)}, bf16[4,32,512]{2,1,0:T(8,128)(2,1)S(1)}, bf16[8,32,512]{2,1,0:T(8,128)(2,1)S(1)}) custom-call(s32[1,96]{1,0:T(1,128)} %atom_hbm.5, s32[1,96]{1,0:T(1,128)} %cell_hbm.5, s32[1,1]{1,0:T(1,128)S(6)} %copy.12.live_ref, ...), custom_call_target="tpu_custom_call" | custom-call | tf_op jit(solution)/shard_map/second_deposit/pallas_call | solution.py:154
  11.8 2.7 %collective-permute-start.7 = (bf16[8,32,512]{2,1,0:T(8,128)(2,1)S(1)}, bf16[8,32,512]{2,1,0:T(8,128)(2,1)S(1)}, u32[]{:S(2)}, u32[]{:S(2)}) collective-permute-start(bf16[8,32,512]{2,1,0:T(8,128)(2,1)S(1)} %get-tuple-element.34.down), channel_id=1, source_target_pairs={{0,7},{1,0},{2,1},{3,2},{4,3},{5,4},{6,5},{7,6},{8,15},{9,8},{10,9... | collective-permute-start | bytes 786440 | tf_op jit(solution)/shard_map/ppermute | solution.py:454
  14.5 0.0 collective-permute-start.6
  14.5 0.0 collective-permute-start.4
  14.5 4.8 %collective-permute-done.1.above = bf16[12,32,512]{2,1,0:T(8,128)(2,1)S(1)} collective-permute-done((bf16[12,32,512]{2,1,0:T(8,128)(2,1)S(1)}, bf16[12,32,512]{2,1,0:T(8,128)(2,1)S(1)}, u32[]{:S(2)}, u32[]{:S(2)}) %collective-permute-start.1) | collective-permute-done | bytes 393248 | tf_op jit(solution)/shard_map/ppermute | solution.py:454
  19.3 2.8 %collective-permute-start.5 = (bf16[4,32,512]{2,1,0:T(8,128)(2,1)S(1)}, bf16[4,32,512]{2,1,0:T(8,128)(2,1)S(1)}, u32[]{:S(2)}, u32[]{:S(2)}) collective-permute-start(bf16[4,32,512]{2,1,0:T(8,128)(2,1)S(1)} %get-tuple-element.37.low), channel_id=1, source_target_pairs={{0,7},{1,0},{2,1},{3,2},{4,3},{5,4},{6,5},{7,6},{8,15},{9,8},{10,9... | collective-permute-start | bytes 393224 | tf_op jit(solution)/shard_map/ppermute | solution.py:454
  22.1 0.0 copy-done
  22.1 1.4 %toeplitz.1 = (bf16[3,384,192]{2,1,0:T(8,128)(2,1)S(1)}, bf16[3,384,192]{2,1,0:T(8,128)(2,1)S(1)}) custom-call(bf16[27,32,32]{2,1,0:T(8,128)(2,1)S(1)} %copy-done), custom_call_target="tpu_custom_call" | custom-call | tf_op jit(solution)/shard_map/toeplitz/pallas_call | solution.py:195
  23.6 0.0 collective-permute-done.below
  23.6 0.0 copy-done.2
  23.6 2.4 %forward.1 = (bf16[8,32,512]{2,1,0:T(8,128)(2,1)S(1)}, bf16[8,32,512]{2,1,0:T(8,128)(2,1)S(1)}, bf16[192,2048]{1,0:T(8,128)(2,1)S(1)}) custom-call(bf16[12,32,512]{2,1,0:T(8,128)(2,1)S(1)} %get-tuple-element.27.down, bf16[8,32,512]{2,1,0:T(8,128)(2,1)S(1)} %get-tuple-element.28.middle, bf16[12,32,512]{2,1,0:T(8,128)(2,1)S(1)} %get-tuple-element.29.up, ...), custom_call_target="tpu_custom_call" | custom-call | tf_op jit(solution)/shard_map/forward/pallas_call | solution.py:490
  26.0 0.1 collective-permute-start.2
  26.0 0.0 collective-permute-done.7.above
  26.0 2.6 %collective-permute-start.3 = (bf16[8,32,512]{2,1,0:T(8,128)(2,1)S(1)}, bf16[8,32,512]{2,1,0:T(8,128)(2,1)S(1)}, u32[]{:S(2)}, u32[]{:S(2)}) collective-permute-start(bf16[8,32,512]{2,1,0:T(8,128)(2,1)S(1)} %get-tuple-element.32.a1), channel_id=1, source_target_pairs={{0,7},{1,0},{2,1},{3,2},{4,3},{5,4},{6,5},{7,6},{8,15},{9,8},{10,9... | collective-permute-start | bytes 786440 | tf_op jit(solution)/shard_map/ppermute | solution.py:454
  28.7 0.0 collective-permute-done.6.below
  28.7 2.2 %gradient.1 = (bf16[144,128]{1,0:T(8,128)(2,1)S(1)}, bf16[144,128]{1,0:T(8,128)(2,1)S(1)}, bf16[128,2048]{1,0:T(8,128)(2,1)S(1)}) custom-call(bf16[4,32,512]{2,1,0:T(8,128)(2,1)S(1)} %get-tuple-element.37.low, bf16[8,32,512]{2,1,0:T(8,128)(2,1)S(1)} %get-tuple-element.38.middle, bf16[4,32,512]{2,1,0:T(8,128)(2,1)S(1)} %get-tuple-element.36.high, ...), custom_call_target="tpu_custom_call" | custom-call | tf_op jit(solution)/shard_map/gradient/pallas_call | solution.py:502
  30.9 0.0 collective-permute-done.4.below
  30.9 0.0 collective-permute-done.5.above
  30.9 2.2 %backward.1 = (bf16[8,32,512]{2,1,0:T(8,128)(2,1)S(1)}, bf16[8,32,512]{2,1,0:T(8,128)(2,1)S(1)}) custom-call(bf16[8,32,512]{2,1,0:T(8,128)(2,1)S(1)} %get-tuple-element.34.down, bf16[8,32,512]{2,1,0:T(8,128)(2,1)S(1)} %get-tuple-element.35.up, bf16[4,32,512]{2,1,0:T(8,128)(2,1)S(1)} %collective-permute-done.4.below, ...), custom_call_target="tpu_custom_call" | custom-call | tf_op jit(solution)/shard_map/backward/pallas_call | solution.py:512
  33.1 0.1 collective-permute-start.8
  33.2 2.6 %collective-permute-start.9 = (bf16[8,32,512]{2,1,0:T(8,128)(2,1)S(1)}, bf16[8,32,512]{2,1,0:T(8,128)(2,1)S(1)}, u32[]{:S(2)}, u32[]{:S(2)}) collective-permute-start(bf16[8,32,512]{2,1,0:T(8,128)(2,1)S(1)} %get-tuple-element.43.b1), channel_id=1, source_target_pairs={{0,7},{1,0},{2,1},{3,2},{4,3},{5,4},{6,5},{7,6},{8,15},{9,8},{10,9... | collective-permute-start | bytes 786440 | tf_op jit(solution)/shard_map/ppermute | solution.py:454
  35.8 0.0 collective-permute-start.10
  35.8 1.2 %collective-permute-done.10 = bf16[144,128]{1,0:T(8,128)(2,1)S(1)} collective-permute-done((bf16[144,128]{1,0:T(8,128)(2,1)S(1)}, bf16[144,128]{1,0:T(8,128)(2,1)S(1)}, u32[]{:S(2)}, u32[]{:S(2)}) %collective-permute-start.10) | collective-permute-done | bytes 36896 | tf_op jit(solution)/shard_map/ppermute | solution.py:460
  37.1 1.6 %collective-permute-start.11 = (bf16[144,128]{1,0:T(8,128)(2,1)S(1)}, bf16[144,128]{1,0:T(8,128)(2,1)S(1)}, u32[]{:S(2)}, u32[]{:S(2)}) collective-permute-start(bf16[144,128]{1,0:T(8,128)(2,1)S(1)} %add.15), channel_id=1, source_target_pairs={{0,8},{8,0},{16,24},{24,16},{1,9},{9,1},{17,25},{25,17},{2,10},{10... | collective-permute-start | bytes 110600 | tf_op jit(solution)/shard_map/ppermute | solution.py:460
  38.7 2.4 %collective-permute-done.11 = bf16[144,128]{1,0:T(8,128)(2,1)S(1)} collective-permute-done((bf16[144,128]{1,0:T(8,128)(2,1)S(1)}, bf16[144,128]{1,0:T(8,128)(2,1)S(1)}, u32[]{:S(2)}, u32[]{:S(2)}) %collective-permute-start.11) | collective-permute-done | bytes 36896 | tf_op jit(solution)/shard_map/ppermute | solution.py:460
  41.1 2.6 %collective-permute-start.12 = (bf16[144,128]{1,0:T(8,128)(2,1)S(1)}, bf16[144,128]{1,0:T(8,128)(2,1)S(1)}, u32[]{:S(2)}, u32[]{:S(2)}) collective-permute-start(bf16[144,128]{1,0:T(8,128)(2,1)S(1)} %add.16), channel_id=1, source_target_pairs={{0,16},{8,24},{16,0},{24,8},{1,17},{9,25},{17,1},{25,9},{2,18},{10... | collective-permute-start | bytes 110600 | tf_op jit(solution)/shard_map/ppermute | solution.py:460
  43.7 2.3 %collective-permute-done.12 = bf16[144,128]{1,0:T(8,128)(2,1)S(1)} collective-permute-done((bf16[144,128]{1,0:T(8,128)(2,1)S(1)}, bf16[144,128]{1,0:T(8,128)(2,1)S(1)}, u32[]{:S(2)}, u32[]{:S(2)}) %collective-permute-start.12) | collective-permute-done | bytes 36896 | tf_op jit(solution)/shard_map/ppermute | solution.py:460
  46.0 0.5 collective-permute-start.13
  46.5 3.6 %collective-permute-done.13 = bf16[144,128]{1,0:T(8,128)(2,1)S(1)} collective-permute-done((bf16[144,128]{1,0:T(8,128)(2,1)S(1)}, bf16[144,128]{1,0:T(8,128)(2,1)S(1)}, u32[]{:S(2)}, u32[]{:S(2)}) %collective-permute-start.13) | collective-permute-done | bytes 36896 | tf_op jit(solution)/shard_map/ppermute | solution.py:460
  50.1 0.1 collective-permute-start.14
  50.2 3.9 %collective-permute-done.14 = bf16[144,128]{1,0:T(8,128)(2,1)S(1)} collective-permute-done((bf16[144,128]{1,0:T(8,128)(2,1)S(1)}, bf16[144,128]{1,0:T(8,128)(2,1)S(1)}, u32[]{:S(2)}, u32[]{:S(2)}) %collective-permute-start.14) | collective-permute-done | bytes 36896 | tf_op jit(solution)/shard_map/ppermute | solution.py:460
  54.1 0.1 collective-permute-start.15
  54.2 1.2 %collective-permute-done.15.other_ref = bf16[144,128]{1,0:T(8,128)(2,1)S(1)} collective-permute-done((bf16[144,128]{1,0:T(8,128)(2,1)S(1)}, bf16[144,128]{1,0:T(8,128)(2,1)S(1)}, u32[]{:S(2)}, u32[]{:S(2)}) %collective-permute-start.15) | collective-permute-done | bytes 36896 | tf_op jit(solution)/shard_map/ppermute | solution.py:460
  55.4 1.6 %finish.1 = (f32[27,32,32]{2,1,0:T(8,128)}, f32[32,32]{1,0:T(8,128)}) custom-call(bf16[144,128]{1,0:T(8,128)(2,1)S(1)} %add.19.mine_ref, bf16[144,128]{1,0:T(8,128)(2,1)S(1)} %collective-permute-done.15.other_ref, bf16[32,32]{1,0:T(8,128)(2,1)S(1)} %copy-done.2, bf16[27,32,32]{2,1,0:T(8,128)(2,1)S(1)} %copy-done), custom_call_target="tpu_custom_call" | custom-call | tf_op jit(solution)/shard_map/finish/pallas_call | solution.py:535
  57.0 0.0 collective-permute-done.2.a0
  57.0 0.0 collective-permute-done.3.a3
  57.0 0.0 collective-permute-done.8.b0
  57.0 0.0 collective-permute-done.9.b3
  57.0 0.0 slice-done
  57.0 0.0 slice-done.1
  57.0 3.4 %gather.1 = (bf16[32,1536]{1,0:T(8,128)(2,1)}, bf16[32,1536]{1,0:T(8,128)(2,1)}) custom-call(s32[1,96]{1,0:T(1,128)} %atom_hbm.5, s32[1,96]{1,0:T(1,128)} %cell_hbm.5, s32[1,1]{1,0:T(1,128)S(6)} %copy.12.live_ref, bf16[96,64,512]{2,1,0:T(8,128)(2,1)S(1)} %bitcast.8, bf16[32,32]{1,0:T(8,128)(2,1)S(1)} %copy-done.2, ...), custom_call_target="tpu_custom_call" | custom-call | tf_op jit(solution)/shard_map/gather/pallas_call | solution.py:403
  (6 shorter events, 0.1 us)
Async XLA Ops:
  0.6 9.2 %copy-start.1 = (bf16[1,32,1536]{2,1,0:T(8,128)(2,1)S(1)}, bf16[1,32,1536]{2,1,0:T(8,128)(2,1)}, u32[]{:S(2)}) copy-start(bf16[1,32,1536]{2,1,0:T(8,128)(2,1)} %param.15) | copy-start | bytes 294916
  1.3 20.8 %copy-start = (bf16[27,32,32]{2,1,0:T(8,128)(2,1)S(1)}, bf16[27,32,32]{2,1,0:T(8,128)(2,1)}, u32[]{:S(2)}) copy-start(bf16[27,32,32]{2,1,0:T(8,128)(2,1)} %conv_ref.3) | copy-start | bytes 165892
  1.3 22.2 %copy-start.2 = (bf16[32,32]{1,0:T(8,128)(2,1)S(1)}, bf16[32,32]{1,0:T(8,128)(2,1)}, u32[]{:S(2)}) copy-start(bf16[32,32]{1,0:T(8,128)(2,1)} %mix_ref.5) | copy-start | bytes 6148
  1.3 55.7 %slice-start = ((s8[6291456]{0:T(1024)(128)(4,1)}), s8[4194304]{0:T(1024)(128)(4,1)S(1)}, s32[]{:S(2)}) async-start(s8[6291456]{0:T(1024)(128)(4,1)} %bitcast.6), calls=%async_computation | async-start | bytes 8388608
  6.4 12.9 %collective-permute-start.1 = (bf16[12,32,512]{2,1,0:T(8,128)(2,1)S(1)}, bf16[12,32,512]{2,1,0:T(8,128)(2,1)S(1)}, u32[]{:S(2)}, u32[]{:S(2)}) collective-permute-start(bf16[12,32,512]{2,1,0:T(8,128)(2,1)S(1)} %get-tuple-element.27.down), channel_id=1, source_target_pairs={{0,7},{1,0},{2,1},{3,2},{4,3},{5,4},{6,5},{7,6},{8,15},{9,8},{10,9... | collective-permute-start | bytes 1179656 | tf_op jit(solution)/shard_map/ppermute | solution.py:454
  9.8 13.7 %collective-permute-start = (bf16[12,32,512]{2,1,0:T(8,128)(2,1)S(1)}, bf16[12,32,512]{2,1,0:T(8,128)(2,1)S(1)}, u32[]{:S(2)}, u32[]{:S(2)}) collective-permute-start(bf16[12,32,512]{2,1,0:T(8,128)(2,1)S(1)} %get-tuple-element.29.up), channel_id=1, source_target_pairs={{0,1},{1,2},{2,3},{3,4},{4,5},{5,6},{6,7},{7,0},{8,9},{9,10},{10,1... | collective-permute-start | bytes 1179656 | tf_op jit(solution)/shard_map/ppermute | solution.py:454
  9.8 47.2 %slice-start.1 = ((s8[6291456]{0:T(1024)(128)(4,1)}), s8[2097152]{0:T(1024)(128)(4,1)S(1)}, s32[]{:S(2)}) async-start(s8[6291456]{0:T(1024)(128)(4,1)} %bitcast.6), calls=%async_computation.1 | async-start | bytes 4194304
  11.8 14.2 %collective-permute-start.7 = (bf16[8,32,512]{2,1,0:T(8,128)(2,1)S(1)}, bf16[8,32,512]{2,1,0:T(8,128)(2,1)S(1)}, u32[]{:S(2)}, u32[]{:S(2)}) collective-permute-start(bf16[8,32,512]{2,1,0:T(8,128)(2,1)S(1)} %get-tuple-element.34.down), channel_id=1, source_target_pairs={{0,7},{1,0},{2,1},{3,2},{4,3},{5,4},{6,5},{7,6},{8,15},{9,8},{10,9... | collective-permute-start | bytes 786440 | tf_op jit(solution)/shard_map/ppermute | solution.py:454
  14.5 14.2 %collective-permute-start.6 = (bf16[8,32,512]{2,1,0:T(8,128)(2,1)S(1)}, bf16[8,32,512]{2,1,0:T(8,128)(2,1)S(1)}, u32[]{:S(2)}, u32[]{:S(2)}) collective-permute-start(bf16[8,32,512]{2,1,0:T(8,128)(2,1)S(1)} %get-tuple-element.35.up), channel_id=1, source_target_pairs={{0,1},{1,2},{2,3},{3,4},{4,5},{5,6},{6,7},{7,0},{8,9},{9,10},{10,1... | collective-permute-start | bytes 786440 | tf_op jit(solution)/shard_map/ppermute | solution.py:454
  14.5 16.4 %collective-permute-start.4 = (bf16[4,32,512]{2,1,0:T(8,128)(2,1)S(1)}, bf16[4,32,512]{2,1,0:T(8,128)(2,1)S(1)}, u32[]{:S(2)}, u32[]{:S(2)}) collective-permute-start(bf16[4,32,512]{2,1,0:T(8,128)(2,1)S(1)} %get-tuple-element.36.high), channel_id=1, source_target_pairs={{0,1},{1,2},{2,3},{3,4},{4,5},{5,6},{6,7},{7,0},{8,9},{9,10},{10,1... | collective-permute-start | bytes 393224 | tf_op jit(solution)/shard_map/ppermute | solution.py:454
  19.3 11.6 %collective-permute-start.5 = (bf16[4,32,512]{2,1,0:T(8,128)(2,1)S(1)}, bf16[4,32,512]{2,1,0:T(8,128)(2,1)S(1)}, u32[]{:S(2)}, u32[]{:S(2)}) collective-permute-start(bf16[4,32,512]{2,1,0:T(8,128)(2,1)S(1)} %get-tuple-element.37.low), channel_id=1, source_target_pairs={{0,7},{1,0},{2,1},{3,2},{4,3},{5,4},{6,5},{7,6},{8,15},{9,8},{10,9... | collective-permute-start | bytes 393224 | tf_op jit(solution)/shard_map/ppermute | solution.py:454
  26.0 31.0 %collective-permute-start.2 = (bf16[8,32,512]{2,1,0:T(8,128)(2,1)S(1)}, bf16[8,32,512]{2,1,0:T(8,128)(2,1)S(1)}, u32[]{:S(2)}, u32[]{:S(2)}) collective-permute-start(bf16[8,32,512]{2,1,0:T(8,128)(2,1)S(1)} %get-tuple-element.31.a2), channel_id=1, source_target_pairs={{0,1},{1,2},{2,3},{3,4},{4,5},{5,6},{6,7},{7,0},{8,9},{9,10},{10,1... | collective-permute-start | bytes 786440 | tf_op jit(solution)/shard_map/ppermute | solution.py:454
  26.0 30.9 %collective-permute-start.3 = (bf16[8,32,512]{2,1,0:T(8,128)(2,1)S(1)}, bf16[8,32,512]{2,1,0:T(8,128)(2,1)S(1)}, u32[]{:S(2)}, u32[]{:S(2)}) collective-permute-start(bf16[8,32,512]{2,1,0:T(8,128)(2,1)S(1)} %get-tuple-element.32.a1), channel_id=1, source_target_pairs={{0,7},{1,0},{2,1},{3,2},{4,3},{5,4},{6,5},{7,6},{8,15},{9,8},{10,9... | collective-permute-start | bytes 786440 | tf_op jit(solution)/shard_map/ppermute | solution.py:454
  33.1 23.9 %collective-permute-start.8 = (bf16[8,32,512]{2,1,0:T(8,128)(2,1)S(1)}, bf16[8,32,512]{2,1,0:T(8,128)(2,1)S(1)}, u32[]{:S(2)}, u32[]{:S(2)}) collective-permute-start(bf16[8,32,512]{2,1,0:T(8,128)(2,1)S(1)} %get-tuple-element.42.b2), channel_id=1, source_target_pairs={{0,1},{1,2},{2,3},{3,4},{4,5},{5,6},{6,7},{7,0},{8,9},{9,10},{10,1... | collective-permute-start | bytes 786440 | tf_op jit(solution)/shard_map/ppermute | solution.py:454
  33.2 23.8 %collective-permute-start.9 = (bf16[8,32,512]{2,1,0:T(8,128)(2,1)S(1)}, bf16[8,32,512]{2,1,0:T(8,128)(2,1)S(1)}, u32[]{:S(2)}, u32[]{:S(2)}) collective-permute-start(bf16[8,32,512]{2,1,0:T(8,128)(2,1)S(1)} %get-tuple-element.43.b1), channel_id=1, source_target_pairs={{0,7},{1,0},{2,1},{3,2},{4,3},{5,4},{6,5},{7,6},{8,15},{9,8},{10,9... | collective-permute-start | bytes 786440 | tf_op jit(solution)/shard_map/ppermute | solution.py:454
  35.8 1.2 %collective-permute-start.10 = (bf16[144,128]{1,0:T(8,128)(2,1)S(1)}, bf16[144,128]{1,0:T(8,128)(2,1)S(1)}, u32[]{:S(2)}, u32[]{:S(2)}) collective-permute-start(bf16[144,128]{1,0:T(8,128)(2,1)S(1)} %get-tuple-element.47), channel_id=1, source_target_pairs={{0,1},{1,0},{2,3},{3,2},{4,5},{5,4},{6,7},{7,6},{8,9},{9,8},{10,11... | collective-permute-start | bytes 110600 | tf_op jit(solution)/shard_map/ppermute | solution.py:460
  37.1 4.0 %collective-permute-start.11 = (bf16[144,128]{1,0:T(8,128)(2,1)S(1)}, bf16[144,128]{1,0:T(8,128)(2,1)S(1)}, u32[]{:S(2)}, u32[]{:S(2)}) collective-permute-start(bf16[144,128]{1,0:T(8,128)(2,1)S(1)} %add.15), channel_id=1, source_target_pairs={{0,8},{8,0},{16,24},{24,16},{1,9},{9,1},{17,25},{25,17},{2,10},{10... | collective-permute-start | bytes 110600 | tf_op jit(solution)/shard_map/ppermute | solution.py:460
  41.1 4.9 %collective-permute-start.12 = (bf16[144,128]{1,0:T(8,128)(2,1)S(1)}, bf16[144,128]{1,0:T(8,128)(2,1)S(1)}, u32[]{:S(2)}, u32[]{:S(2)}) collective-permute-start(bf16[144,128]{1,0:T(8,128)(2,1)S(1)} %add.16), channel_id=1, source_target_pairs={{0,16},{8,24},{16,0},{24,8},{1,17},{9,25},{17,1},{25,9},{2,18},{10... | collective-permute-start | bytes 110600 | tf_op jit(solution)/shard_map/ppermute | solution.py:460
  46.0 4.0 %collective-permute-start.13 = (bf16[144,128]{1,0:T(8,128)(2,1)S(1)}, bf16[144,128]{1,0:T(8,128)(2,1)S(1)}, u32[]{:S(2)}, u32[]{:S(2)}) collective-permute-start(bf16[144,128]{1,0:T(8,128)(2,1)S(1)} %add.17), channel_id=1, source_target_pairs={{0,4},{1,5},{2,6},{3,7},{4,0},{5,1},{6,2},{7,3},{8,12},{9,13},{10,... | collective-permute-start | bytes 110600 | tf_op jit(solution)/shard_map/ppermute | solution.py:460
  50.1 4.0 %collective-permute-start.14 = (bf16[144,128]{1,0:T(8,128)(2,1)S(1)}, bf16[144,128]{1,0:T(8,128)(2,1)S(1)}, u32[]{:S(2)}, u32[]{:S(2)}) collective-permute-start(bf16[144,128]{1,0:T(8,128)(2,1)S(1)} %add.18), channel_id=1, source_target_pairs={{0,2},{1,3},{2,0},{3,1},{4,6},{5,7},{6,4},{7,5},{8,10},{9,11},{10,... | collective-permute-start | bytes 110600 | tf_op jit(solution)/shard_map/ppermute | solution.py:460
  54.1 1.3 %collective-permute-start.15 = (bf16[144,128]{1,0:T(8,128)(2,1)S(1)}, bf16[144,128]{1,0:T(8,128)(2,1)S(1)}, u32[]{:S(2)}, u32[]{:S(2)}) collective-permute-start(bf16[144,128]{1,0:T(8,128)(2,1)S(1)} %add.19.mine_ref), channel_id=1, source_target_pairs={{0,1},{1,0},{2,3},{3,2},{4,5},{5,4},{6,7},{7,6},{8,9},{9,8},{10,11... | collective-permute-start | bytes 110600 | tf_op jit(solution)/shard_map/ppermute | solution.py:460

commit v2 on v1

--- a/solution.py
+++ b/solution.py
@@ -69,15 +69,18 @@
     )
     parts = [slice(i * per_chunk, (i + 1) * per_chunk) for i in range(chunks)]
     large = copies([(weight_hbm.at[p], weight_ref.at[p]) for p in parts], weight_sems)
-    for copy in small + large:
+    ahead = chunks
+    for copy in small + large[:ahead]:
         copy.start()
     total[...] = jnp.zeros_like(total)
     for copy in small:
         copy.wait()
     split_atoms(feats[...], source)
     live = live_ref[0, 0]
-    for part, copy in zip(parts, large):
+    for i, (part, copy) in enumerate(zip(parts, large)):
         copy.wait()
+        if i + ahead < chunks:
+            large[i + ahead].start()
         add_tiles(part, atom_ref, cell_ref, live, source, weight_ref, total)
     write_parts(total, (down_ref, middle_ref, up_ref))
 
@@ -165,8 +168,9 @@
 def toeplitz_kernel(conv_ref, forward_ref, backward_ref):
     channels = conv_ref.shape[1]
     for flip, out_ref in ((False, forward_ref), (True, backward_ref)):
-        for dx in range(3):
-            for dy in range(3):
+        for dy in range(3):
+            bands = []
+            for dx in range(3):
                 parts = []
                 for dz in range(3):
                     if flip:
@@ -174,24 +178,25 @@
                         parts.append(conv_ref[k].astype(F32).T)
                     else:
                         parts.append(conv_ref[9 * dz + 3 * dy + dx].astype(F32))
-                band = jnp.concatenate(parts, axis=1)
-                for po in range(ZD):
-                    pieces = []
+                bands.append(jnp.concatenate(parts, axis=1))
+            for po in range(ZD):
+                pieces = []
+                for band in bands:
                     if po:
                         pieces.append(jnp.zeros((channels, po * channels), F32))
                     pieces.append(band)
                     rest = (ZD - 1 - po) * channels
                     if rest:
                         pieces.append(jnp.zeros((channels, rest), F32))
-                    row = (dy * ZD + po) * channels
-                    out_ref[dx, row : row + channels] = jnp.concatenate(
-                        pieces, axis=1
-                    ).astype(BF16)
+                row = (dy * ZD + po) * channels
+                out_ref[row : row + channels] = jnp.concatenate(pieces, axis=1).astype(
+                    BF16
+                )
 
 
 def toeplitz(conv_w):
     channels = conv_w.shape[1]
-    shape = pltpu.VMEM((3, 3 * ZD * channels, (ZD + 2) * channels), BF16)
+    shape = pltpu.VMEM((3 * ZD * channels, 3 * (ZD + 2) * channels), BF16)
     return pl.pallas_call(
         toeplitz_kernel,
         in_specs=[whole()],
@@ -217,40 +222,32 @@
     ]
 
 
-def column(shape):
-    return lax.rem(lax.broadcasted_iota(jnp.int32, shape, 1), GX)
-
-
 def store_shifted(out_ref, row, value):
     rows, cells = value.shape
-    x = column(value.shape)
     group = out_ref.shape[0] // 3
-    left = jnp.where(
-        x == 0, pltpu.roll(value, cells - GX + 1, 1), pltpu.roll(value, 1, 1)
-    )
-    right = jnp.where(
-        x == GX - 1, pltpu.roll(value, GX - 1, 1), pltpu.roll(value, cells - 1, 1)
-    )
-    out_ref[row : row + rows] = left.astype(BF16)
-    out_ref[group + row : group + row + rows] = value.astype(BF16)
-    out_ref[2 * group + row : 2 * group + row + rows] = right.astype(BF16)
+    wide = 2 * GX
+    x = lax.rem(lax.broadcasted_iota(jnp.int32, (rows, wide), 1), GX)
+    out_ref[group + row : group + row + rows] = value
+    for first in range(0, cells, wide):
+        cols = slice(first, first + wide)
+        part = value[:, cols]
+        out_ref[row : row + rows, cols] = jnp.where(
+            x == 0, pltpu.roll(part, GX + 1, 1), pltpu.roll(part, 1, 1)
+        )
+        out_ref[2 * group + row : 2 * group + row + rows, cols] = jnp.where(
+            x == GX - 1, pltpu.roll(part, GX - 1, 1), pltpu.roll(part, wide - 1, 1)
+        )
 
 
 def conv_planes(matrix_ref, shifted, partial, low_ref, high_ref):
     cells = shifted.shape[1]
-    group = shifted.shape[0] // 3
     chunk = low_ref.shape[2]
-    for q in range(cells // chunk):
-        cols = slice(q * chunk, (q + 1) * chunk)
-        acc = None
-        for dx in range(3):
-            term = jnp.dot(
-                matrix_ref[dx],
-                shifted[dx * group : (dx + 1) * group, cols],
-                preferred_element_type=F32,
-            )
-            acc = term if acc is None else acc + term
-        partial[:, cols] = acc
+    width = chunk // 2
+    for first in range(0, cells, width):
+        cols = slice(first, first + width)
+        partial[:, cols] = jnp.dot(
+            matrix_ref[...], shifted[:, cols], preferred_element_type=F32
+        )
     channels = low_ref.shape[1]
     quarters = cells // chunk
     for po in range(ZD):
@@ -280,7 +277,7 @@
         plane = plane.astype(BF16)
         plain_ref[p * channels : (p + 1) * channels] = plane
         mixed = jnp.dot(mix_ref[...], plane, preferred_element_type=F32)
-        store_shifted(shifted, p * channels, mixed.astype(BF16).astype(F32))
+        store_shifted(shifted, p * channels, mixed.astype(BF16))
     conv_planes(matrix_ref, shifted, partial, low_ref, high_ref)
 
 
@@ -293,7 +290,7 @@
     cells = plain_ref.shape[1]
     for p in range(ZD + 2):
         rows = slice(p * channels, (p + 1) * channels)
-        store_shifted(shifted, p * channels, plain_ref[rows].astype(F32))
+        store_shifted(shifted, p * channels, plain_ref[rows])
     own = ((low, 0, 1), (middle, 0, ZD - 2), (high, 0, 1))
     planes = joined_planes(own, ((below, 0, ZH), (above, 0, ZH)), quarters)
     third = ZD * channels
@@ -348,11 +345,11 @@
     quarters = below.shape[0]
     (first,) = joined_planes(((down, 1, 1),), ((below, 0, 1),), quarters)
     (last,) = joined_planes(((up, 0, 1),), ((above, 0, 1),), quarters)
-    store_shifted(shifted, 0, first.astype(BF16).astype(F32))
+    store_shifted(shifted, 0, first.astype(BF16))
     for p in range(ZD):
         rows = slice(p * channels, (p + 1) * channels)
-        store_shifted(shifted, (p + 1) * channels, sums_ref[rows].astype(F32))
-    store_shifted(shifted, (ZD + 1) * channels, last.astype(BF16).astype(F32))
+        store_shifted(shifted, (p + 1) * channels, sums_ref[rows])
+    store_shifted(shifted, (ZD + 1) * channels, last.astype(BF16))
     conv_planes(matrix_ref, shifted, partial, low_ref, high_ref)
 
 
@@ -362,36 +359,61 @@
     atom_ref, cell_ref, small_sems, field, total,
 ):
     channels = mix_ref.shape[0]
-    tiles, tile_a, _ = weight_ref.shape
+    tiles, tile_a, tile_c = weight_ref.shape
+    half = tile_c // 2
     small = copies(((atom_hbm, atom_ref), (cell_hbm, cell_ref)), small_sems)
     for copy in small:
         copy.start()
     first = 0
     for a, b in ((a0, b0), (a1, b1), (a2, b2), (a3, b3)):
         count = a.shape[0]
-        field[first : first + count, :channels] = a[...]
-        field[first : first + count, channels:] = b[...]
+        for i, cols in enumerate((slice(0, half), slice(half, tile_c))):
+            row = 2 * i * channels
+            field[first : first + count, row : row + channels] = a[:, :, cols]
+            field[first : first + count, row + channels : row + 2 * channels] = b[
+                :, :, cols
+            ]
         first += count
     total[...] = jnp.zeros_like(total)
     for copy in small:
         copy.wait()
     live = live_ref[0, 0]
-    for j in range(tiles):
+    lane = lax.broadcasted_iota(jnp.int32, (2 * channels, 2 * tile_a), 1)
+    for j in range(0, tiles, 2):
+        pair = (j, j + 1)
+        left = jnp.concatenate([field[cell_ref[0, t]] for t in pair], axis=0)
+        right = jnp.concatenate(
+            [
+                weight_ref[t, :, cols]
+                for t in pair
+                for cols in (slice(0, half), slice(half, tile_c))
+            ],
+            axis=0,
+        )
         product = lax.dot_general(
-            field[cell_ref[0, j]],
-            weight_ref[j],
-            (((1,), (1,)), ((), ())),
-            preferred_element_type=F32,
-        )
-        total[atom_ref[0, j]] += jnp.where(j < live, product, jnp.zeros_like(product))
-
-    mix_t = mix_ref[...].astype(F32).T.astype(BF16)
+            left, right, (((1,), (1,)), ((), ())), preferred_element_type=F32
+        )
+        for i, t in enumerate(pair):
+            row, col = 4 * i * channels, 2 * i * tile_a
+            both = jnp.where(
+                lane < tile_a,
+                product[row : row + 2 * channels, col : col + 2 * tile_a],
+                product[row + 2 * channels : row + 4 * channels, col : col + 2 * tile_a],
+            )
+            total[atom_ref[0, t]] += jnp.where(t < live, both, jnp.zeros_like(both))
+
     for a in range(0, total.shape[0], 2):
-        pair = jnp.concatenate([total[a], total[a + 1]], axis=1).astype(BF16)
+        lower, upper = total[a], total[a + 1]
+        pair = jnp.where(
+            lane < tile_a,
+            lower + pltpu.roll(lower, tile_a, 1),
+            upper + pltpu.roll(upper, tile_a, 1),
+        ).astype(BF16)
         cols = slice(a * tile_a, (a + 2) * tile_a)
         potential_ref[:, cols] = pair[:channels]
-        grad_ref[:, cols] = jnp.dot(
-            mix_t, pair[channels:], preferred_element_type=F32
+        grad_ref[:, cols] = lax.dot_general(
+            mix_ref[...], pair[channels:], (((0,), (0,)), ((), ())),
+            preferred_element_type=F32,
         ).astype(BF16)
 
 
@@ -407,8 +429,8 @@
         out_shape=[shape, shape],
         scratch_shapes=list_scratch(atom_ids, cell_ids)
         + [
-            pltpu.VMEM((blocks, 2 * channels, tile_c), BF16),
-            pltpu.VMEM((atoms // tile_a, 2 * channels, tile_a), F32),
+            pltpu.VMEM((blocks, 4 * channels, tile_c // 2), BF16),
+            pltpu.VMEM((atoms // tile_a, 2 * channels, 2 * tile_a), F32),
         ],
         compiler_params=params(),
         name="gather",
@@ -425,25 +447,28 @@
     total = jnp.concatenate(
         [jnp.where(odd, other, mine), jnp.where(odd, mine, other)], axis=0
     )
-    mix = mix_ref[...].astype(F32)
+    mix = mix_ref[...]
     acc = jnp.zeros((channels, channels), F32)
     for dz in range(3):
         part = total[:, dz * channels : (dz + 1) * channels]
-        scaled = lax.dot_general(
-            part, mix, (((1,), (1,)), ((), ())),
-            precision=lax.Precision.HIGHEST, preferred_element_type=F32,
-        ) * (1.0 / conv_scale)
-        kernels = []
-        for dx in range(3):
-            for dy in range(3):
-                row = (3 * dx + dy) * channels
-                k = 9 * dz + 3 * dy + dx
-                conv_out[k] = scaled[row : row + channels]
-                kernels.append(conv_ref[k].astype(F32))
-        acc = acc + lax.dot_general(
-            jnp.concatenate(kernels, axis=0), part, (((0,), (0,)), ((), ())),
-            precision=lax.Precision.HIGHEST, preferred_element_type=F32,
-        )
+        upper = part.astype(BF16)
+        pieces = (upper, (part - upper.astype(F32)).astype(BF16))
+        kernels = jnp.concatenate(
+            [conv_ref[9 * dz + 3 * (n % 3) + n // 3] for n in range(9)], axis=0
+        )
+        scaled = jnp.zeros(part.shape, F32)
+        for piece in pieces:
+            scaled = scaled + lax.dot_general(
+                piece, mix, (((1,), (1,)), ((), ())), preferred_element_type=F32
+            )
+            acc = acc + lax.dot_general(
+                kernels, piece, (((0,), (0,)), ((), ())), preferred_element_type=F32
+            )
+        scaled = scaled * (1.0 / conv_scale)
+        for n in range(9):
+            conv_out[9 * dz + 3 * (n % 3) + n // 3] = scaled[
+                n * channels : (n + 1) * channels
+            ]
     mix_out[...] = acc * (1.0 / mix_scale)
 
 
@@ -503,7 +528,7 @@
         gradient_kernel,
         in_specs=[whole()] * 6,
         out_specs=[whole()] * 3,
-        out_shape=[part, part, pltpu.VMEM((ZD * channels, cells), BF16)],
+        out_shape=[pltpu.VMEM(part.shape, F32), part, pltpu.VMEM((ZD * channels, cells), BF16)],
         scratch_shapes=[scratch[0], pltpu.VMEM((3 * ZD * channels, cells), BF16)],
         compiler_params=params(),
         name="gradient",
@@ -520,15 +545,17 @@
     )(ed, eu, f_below, f_above, sums, backward)
     drho_below, drho_above = ring(drho_high, "slab", 1), ring(drho_low, "slab", -1)
 
-    total = keep + arrived
-    turns = [("rep", 1 << i) for i in range((lax.axis_size("rep") - 1).bit_length())]
-    turns += [
-        ("slab", 1 << i)
-        for i in reversed(range(1, (lax.axis_size("slab") - 1).bit_length()))
-    ]
-    for axis, stride in turns:
-        arrived = exchanged(total, axis, stride)
+    total = (keep + arrived.astype(F32)).astype(BF16)
+    for turn in range((lax.axis_size("rep") - 1).bit_length()):
+        arrived = exchanged(total, "rep", 1 << turn)
         total = total + arrived
+    strides = [1 << i for i in range(1, (lax.axis_size("slab") - 1).bit_length())]
+    for stride in strides[:-2]:
+        arrived = exchanged(total, "slab", stride)
+        total = total + arrived
+    near, far = strides[-2:]
+    across = [exchanged(total, "slab", s) for s in (near, far, near | far)]
+    total = ((total + across[0]) + (across[1] + across[2])).astype(BF16)
     other = exchanged(total, "slab", 1)
 
     groups = lax.axis_size("rep") * lax.axis_size("slab")

time: 60.8 us -> 62.3 us (1.025)
  starting transfers between devices: 19.2 us -> 22.1 us
  Pallas kernels: 20.2 us -> 18.3 us
    ppermute x10, waiting for transfers between devices: 4.85 us -> 14.2 us  [ring(): lax.ppermute(value, axis, pairs)]
    ppermute x6 -> x7, waiting for transfers between devices: 14.6 us -> 5.85 us  [exchanged(): return lax.ppermute(value, axis, [(i, i ^ stride) for i in range(count)])]
    ppermute x6 -> x7, starting transfers between devices: 4.91 us -> 8 us  [exchanged(): return lax.ppermute(value, axis, [(i, i ^ stride) for i in range(count)])]
    pallas_call x1, Pallas kernels: 1.42 us -> 0.76 us  [toeplitz(): pl.pallas_call(toeplitz_kernel, in_specs=[whole()], out_specs=[whole()] *...]
  transfers between devices with their start and end apart: 16 -> 17, of which waited for: 7 -> 7; matrix products, arithmetic and copies ran while one was open for 0% -> 0% of each run, Pallas kernels for 19% -> 12%
where the time goes in v2:
time: 62.3 us; the launch traced here: 62.1 us
  starting transfers between devices  22.1 us (35%)
  waiting for transfers between devices  20 us (32%)
  Pallas kernels  18.3 us (29%)
  between operations  1.64 us (3%)
    ppermute x10, waiting for transfers between devices, ring(): lax.ppermute(value, axis, pairs)  14.2 us
    ppermute x10, starting transfers between devices, ring(): lax.ppermute(value, axis, pairs)  14.1 us
    ppermute x7, starting transfers between devices, exchanged(): return lax.ppermute(value, axis, [(i, i ^ stride) for i in range(count)])  8 us
    ppermute x7, waiting for transfers between devices, exchanged(): return lax.ppermute(value, axis, [(i, i ^ stride) for i in range(count)])  5.85 us
    pallas_call x1, Pallas kernels, first_deposit(): pl.pallas_call(first_deposit_kernel, in_specs=list_specs() + [hbm()] * 2,...  5.03 us
    pallas_call x1, Pallas kernels, gather(): pl.pallas_call(gather_kernel, in_specs=list_specs() + [whole()] * 10, out...  3.58 us
    pallas_call x1, Pallas kernels, step(): pl.pallas_call(gradient_kernel, in_specs=[whole()] * 6, out_specs=[whole(...  2.05 us
    pallas_call x1, Pallas kernels, second_deposit(): pl.pallas_call(second_deposit_kernel, in_specs=list_specs() + [whole()] *...  1.97 us
  transfers between devices with their start and end apart: 17, of which 7 were waited for; matrix products, arithmetic and copies ran while one was open for 0% of the time, Pallas kernels for 12%

profile of v2, /device:TPU:0, one launch (start us, length us, event | category | flops | bytes accessed | tf_op | source)
XLA Modules:
  0.0 62.1 jit_solution(8983176425355856826)
XLA Ops:
  0.6 0.0 copy-start.1
  1.3 0.0 copy-start
  1.3 0.0 copy-start.2
  1.3 0.0 slice-start
  1.4 5.0 %first_deposit.1 = (bf16[12,32,512]{2,1,0:T(8,128)(2,1)S(1)}, bf16[8,32,512]{2,1,0:T(8,128)(2,1)S(1)}, bf16[12,32,512]{2,1,0:T(8,128)(2,1)S(1)}, bf16[96,64,512]{2,1,0:T(8,128)(2,1)S(1)}) custom-call(s32[1,96]{1,0:T(1,128)} %atom_hbm.5, s32[1,96]{1,0:T(1,128)} %cell_hbm.5, s32[1,1]{1,0:T(1,128)S(6)} %copy.12.live_ref, bf16[32,1536]{1,0:T(8,128)(2,1)} %bitcast.10, ...), custom_call_target="tpu_custom_call" | custom-call | tf_op jit(solution)/shard_map/first_deposit/pallas_call | solution.py:142
  6.4 3.4 %collective-permute-start.1 = (bf16[12,32,512]{2,1,0:T(8,128)(2,1)S(1)}, bf16[12,32,512]{2,1,0:T(8,128)(2,1)S(1)}, u32[]{:S(2)}, u32[]{:S(2)}) collective-permute-start(bf16[12,32,512]{2,1,0:T(8,128)(2,1)S(1)} %get-tuple-element.27.down), channel_id=1, source_target_pairs={{0,7},{1,0},{2,1},{3,2},{4,3},{5,4},{6,5},{7,6},{8,15},{9,8},{10,9... | collective-permute-start | bytes 1179656 | tf_op jit(solution)/shard_map/ppermute | solution.py:479
  9.8 0.0 collective-permute-start
  9.8 0.0 copy-done.1
  9.8 0.0 slice-start.1
  9.8 2.0 %second_deposit.1 = (bf16[8,32,512]{2,1,0:T(8,128)(2,1)S(1)}, bf16[4,32,512]{2,1,0:T(8,128)(2,1)S(1)}, bf16[8,32,512]{2,1,0:T(8,128)(2,1)S(1)}, bf16[4,32,512]{2,1,0:T(8,128)(2,1)S(1)}, bf16[8,32,512]{2,1,0:T(8,128)(2,1)S(1)}) custom-call(s32[1,96]{1,0:T(1,128)} %atom_hbm.5, s32[1,96]{1,0:T(1,128)} %cell_hbm.5, s32[1,1]{1,0:T(1,128)S(6)} %copy.12.live_ref, ...), custom_call_target="tpu_custom_call" | custom-call | tf_op jit(solution)/shard_map/second_deposit/pallas_call | solution.py:157
  11.8 2.7 %collective-permute-start.7 = (bf16[8,32,512]{2,1,0:T(8,128)(2,1)S(1)}, bf16[8,32,512]{2,1,0:T(8,128)(2,1)S(1)}, u32[]{:S(2)}, u32[]{:S(2)}) collective-permute-start(bf16[8,32,512]{2,1,0:T(8,128)(2,1)S(1)} %get-tuple-element.34.down), channel_id=1, source_target_pairs={{0,7},{1,0},{2,1},{3,2},{4,3},{5,4},{6,5},{7,6},{8,15},{9,8},{10,9... | collective-permute-start | bytes 786440 | tf_op jit(solution)/shard_map/ppermute | solution.py:479
  14.5 0.0 collective-permute-start.6
  14.5 0.0 copy-done
  14.5 0.8 %toeplitz.1 = (bf16[384,576]{1,0:T(8,128)(2,1)S(1)}, bf16[384,576]{1,0:T(8,128)(2,1)S(1)}) custom-call(bf16[27,32,32]{2,1,0:T(8,128)(2,1)S(1)} %copy-done), custom_call_target="tpu_custom_call" | custom-call | tf_op jit(solution)/shard_map/toeplitz/pallas_call | solution.py:200
  15.3 4.1 %collective-permute-done.1.above = bf16[12,32,512]{2,1,0:T(8,128)(2,1)S(1)} collective-permute-done((bf16[12,32,512]{2,1,0:T(8,128)(2,1)S(1)}, bf16[12,32,512]{2,1,0:T(8,128)(2,1)S(1)}, u32[]{:S(2)}, u32[]{:S(2)}) %collective-permute-start.1) | collective-permute-done | bytes 393248 | tf_op jit(solution)/shard_map/ppermute | solution.py:479
  19.3 2.8 %collective-permute-done.below = bf16[12,32,512]{2,1,0:T(8,128)(2,1)S(1)} collective-permute-done((bf16[12,32,512]{2,1,0:T(8,128)(2,1)S(1)}, bf16[12,32,512]{2,1,0:T(8,128)(2,1)S(1)}, u32[]{:S(2)}, u32[]{:S(2)}) %collective-permute-start) | collective-permute-done | bytes 393248 | tf_op jit(solution)/shard_map/ppermute | solution.py:479
  22.1 0.0 copy-done.2
  22.1 2.0 %forward.1 = (bf16[8,32,512]{2,1,0:T(8,128)(2,1)S(1)}, bf16[8,32,512]{2,1,0:T(8,128)(2,1)S(1)}, bf16[192,2048]{1,0:T(8,128)(2,1)S(1)}) custom-call(bf16[12,32,512]{2,1,0:T(8,128)(2,1)S(1)} %get-tuple-element.27.down, bf16[8,32,512]{2,1,0:T(8,128)(2,1)S(1)} %get-tuple-element.28.middle, bf16[12,32,512]{2,1,0:T(8,128)(2,1)S(1)} %get-tuple-element.29.up, ...), custom_call_target="tpu_custom_call" | custom-call | tf_op jit(solution)/shard_map/forward/pallas_call | solution.py:515
  24.1 0.0 collective-permute-done.7.above
  24.1 1.9 %collective-permute-done.6.below = bf16[8,32,512]{2,1,0:T(8,128)(2,1)S(1)} collective-permute-done((bf16[8,32,512]{2,1,0:T(8,128)(2,1)S(1)}, bf16[8,32,512]{2,1,0:T(8,128)(2,1)S(1)}, u32[]{:S(2)}, u32[]{:S(2)}) %collective-permute-start.6) | collective-permute-done | bytes 262176 | tf_op jit(solution)/shard_map/ppermute | solution.py:479
  26.0 2.0 %gradient.1 = (f32[144,128]{1,0:T(8,128)S(1)}, bf16[144,128]{1,0:T(8,128)(2,1)S(1)}, bf16[128,2048]{1,0:T(8,128)(2,1)S(1)}) custom-call(bf16[4,32,512]{2,1,0:T(8,128)(2,1)S(1)} %get-tuple-element.37.low, bf16[8,32,512]{2,1,0:T(8,128)(2,1)S(1)} %get-tuple-element.38.middle, bf16[4,32,512]{2,1,0:T(8,128)(2,1)S(1)} %get-tuple-element.36.high, ...), custom_call_target="tpu_custom_call" | custom-call | tf_op jit(solution)/shard_map/gradient/pallas_call | solution.py:527
  28.0 0.1 collective-permute-start.10
  28.1 0.5 collective-permute-start.4
  28.6 2.2 %collective-permute-start.5 = (bf16[4,32,512]{2,1,0:T(8,128)(2,1)S(1)}, bf16[4,32,512]{2,1,0:T(8,128)(2,1)S(1)}, u32[]{:S(2)}, u32[]{:S(2)}) collective-permute-start(bf16[4,32,512]{2,1,0:T(8,128)(2,1)S(1)} %get-tuple-element.37.low), channel_id=1, source_target_pairs={{0,7},{1,0},{2,1},{3,2},{4,3},{5,4},{6,5},{7,6},{8,15},{9,8},{10,9... | collective-permute-start | bytes 393224 | tf_op jit(solution)/shard_map/ppermute | solution.py:479
  30.8 0.0 collective-permute-done.10
  30.8 1.6 %collective-permute-start.11 = (bf16[144,128]{1,0:T(8,128)(2,1)S(1)}, bf16[144,128]{1,0:T(8,128)(2,1)S(1)}, u32[]{:S(2)}, u32[]{:S(2)}) collective-permute-start(bf16[144,128]{1,0:T(8,128)(2,1)S(1)} %add_convert_fusion), channel_id=1, source_target_pairs={{0,8},{8,0},{16,24},{24,16},{1,9},{9,1},{17,25},{25,17},{2,10},{10... | collective-permute-start | bytes 110600 | tf_op jit(solution)/shard_map/ppermute | solution.py:485
  32.5 2.4 %collective-permute-done.11 = bf16[144,128]{1,0:T(8,128)(2,1)S(1)} collective-permute-done((bf16[144,128]{1,0:T(8,128)(2,1)S(1)}, bf16[144,128]{1,0:T(8,128)(2,1)S(1)}, u32[]{:S(2)}, u32[]{:S(2)}) %collective-permute-start.11) | collective-permute-done | bytes 36896 | tf_op jit(solution)/shard_map/ppermute | solution.py:485
  34.9 2.7 %collective-permute-start.12 = (bf16[144,128]{1,0:T(8,128)(2,1)S(1)}, bf16[144,128]{1,0:T(8,128)(2,1)S(1)}, u32[]{:S(2)}, u32[]{:S(2)}) collective-permute-start(bf16[144,128]{1,0:T(8,128)(2,1)S(1)} %add.19), channel_id=1, source_target_pairs={{0,16},{8,24},{16,0},{24,8},{1,17},{9,25},{17,1},{25,9},{2,18},{10... | collective-permute-start | bytes 110600 | tf_op jit(solution)/shard_map/ppermute | solution.py:485
  37.5 2.3 %collective-permute-done.12 = bf16[144,128]{1,0:T(8,128)(2,1)S(1)} collective-permute-done((bf16[144,128]{1,0:T(8,128)(2,1)S(1)}, bf16[144,128]{1,0:T(8,128)(2,1)S(1)}, u32[]{:S(2)}, u32[]{:S(2)}) %collective-permute-start.12) | collective-permute-done | bytes 36896 | tf_op jit(solution)/shard_map/ppermute | solution.py:485
  39.8 0.6 collective-permute-start.15
  40.4 1.1 %collective-permute-start.14 = (bf16[144,128]{1,0:T(8,128)(2,1)S(1)}, bf16[144,128]{1,0:T(8,128)(2,1)S(1)}, u32[]{:S(2)}, u32[]{:S(2)}) collective-permute-start(bf16[144,128]{1,0:T(8,128)(2,1)S(1)} %add.20), channel_id=1, source_target_pairs={{0,4},{1,5},{2,6},{3,7},{4,0},{5,1},{6,2},{7,3},{8,12},{9,13},{10,... | collective-permute-start | bytes 110600 | tf_op jit(solution)/shard_map/ppermute | solution.py:485
  41.5 1.9 %collective-permute-start.13 = (bf16[144,128]{1,0:T(8,128)(2,1)S(1)}, bf16[144,128]{1,0:T(8,128)(2,1)S(1)}, u32[]{:S(2)}, u32[]{:S(2)}) collective-permute-start(bf16[144,128]{1,0:T(8,128)(2,1)S(1)} %add.20), channel_id=1, source_target_pairs={{0,2},{1,3},{2,0},{3,1},{4,6},{5,7},{6,4},{7,5},{8,10},{9,11},{10,... | collective-permute-start | bytes 110600 | tf_op jit(solution)/shard_map/ppermute | solution.py:485
  43.4 0.0 collective-permute-done.4.below
  43.4 0.0 collective-permute-start.2
  43.4 0.0 collective-permute-done.5.above
  43.4 2.6 %collective-permute-start.3 = (bf16[8,32,512]{2,1,0:T(8,128)(2,1)S(1)}, bf16[8,32,512]{2,1,0:T(8,128)(2,1)S(1)}, u32[]{:S(2)}, u32[]{:S(2)}) collective-permute-start(bf16[8,32,512]{2,1,0:T(8,128)(2,1)S(1)} %get-tuple-element.32.a1), channel_id=1, source_target_pairs={{0,7},{1,0},{2,1},{3,2},{4,3},{5,4},{6,5},{7,6},{8,15},{9,8},{10,9... | collective-permute-start | bytes 786440 | tf_op jit(solution)/shard_map/ppermute | solution.py:479
  46.0 1.7 %backward.1 = (bf16[8,32,512]{2,1,0:T(8,128)(2,1)S(1)}, bf16[8,32,512]{2,1,0:T(8,128)(2,1)S(1)}) custom-call(bf16[8,32,512]{2,1,0:T(8,128)(2,1)S(1)} %get-tuple-element.34.down, bf16[8,32,512]{2,1,0:T(8,128)(2,1)S(1)} %get-tuple-element.35.up, bf16[4,32,512]{2,1,0:T(8,128)(2,1)S(1)} %collective-permute-done.4.below, ...), custom_call_target="tpu_custom_call" | custom-call | tf_op jit(solution)/shard_map/backward/pallas_call | solution.py:537
  47.7 0.0 collective-permute-done.15
  47.7 0.1 collective-permute-start.8
  47.8 0.0 collective-permute-done.14
  47.8 2.6 %collective-permute-start.9 = (bf16[8,32,512]{2,1,0:T(8,128)(2,1)S(1)}, bf16[8,32,512]{2,1,0:T(8,128)(2,1)S(1)}, u32[]{:S(2)}, u32[]{:S(2)}) collective-permute-start(bf16[8,32,512]{2,1,0:T(8,128)(2,1)S(1)} %get-tuple-element.43.b1), channel_id=1, source_target_pairs={{0,7},{1,0},{2,1},{3,2},{4,3},{5,4},{6,5},{7,6},{8,15},{9,8},{10,9... | collective-permute-start | bytes 786440 | tf_op jit(solution)/shard_map/ppermute | solution.py:479
  50.5 0.0 collective-permute-done.13
  50.5 0.1 collective-permute-start.16
  50.5 1.2 %collective-permute-done.16.other_ref = bf16[144,128]{1,0:T(8,128)(2,1)S(1)} collective-permute-done((bf16[144,128]{1,0:T(8,128)(2,1)S(1)}, bf16[144,128]{1,0:T(8,128)(2,1)S(1)}, u32[]{:S(2)}, u32[]{:S(2)}) %collective-permute-start.16) | collective-permute-done | bytes 36896 | tf_op jit(solution)/shard_map/ppermute | solution.py:485
  51.7 1.2 %finish.1 = (f32[27,32,32]{2,1,0:T(8,128)}, f32[32,32]{1,0:T(8,128)}) custom-call(bf16[144,128]{1,0:T(8,128)(2,1)S(1)} %add_add_fusion.mine_ref, bf16[144,128]{1,0:T(8,128)(2,1)S(1)} %collective-permute-done.16.other_ref, bf16[32,32]{1,0:T(8,128)(2,1)S(1)} %copy-done.2, bf16[27,32,32]{2,1,0:T(8,128)(2,1)S(1)} %copy-done), custom_call_target="tpu_custom_call" | custom-call | tf_op jit(solution)/shard_map/finish/pallas_call | solution.py:562
  52.9 0.0 collective-permute-done.2.a0
  52.9 0.0 collective-permute-done.3.a3
  52.9 5.4 %collective-permute-done.8.b0 = bf16[8,32,512]{2,1,0:T(8,128)(2,1)S(1)} collective-permute-done((bf16[8,32,512]{2,1,0:T(8,128)(2,1)S(1)}, bf16[8,32,512]{2,1,0:T(8,128)(2,1)S(1)}, u32[]{:S(2)}, u32[]{:S(2)}) %collective-permute-start.8) | collective-permute-done | bytes 262176 | tf_op jit(solution)/shard_map/ppermute | solution.py:479
  58.4 0.0 collective-permute-done.9.b3
  58.4 0.0 slice-done
  58.4 0.0 slice-done.1
  58.4 3.6 %gather.1 = (bf16[32,1536]{1,0:T(8,128)(2,1)}, bf16[32,1536]{1,0:T(8,128)(2,1)}) custom-call(s32[1,96]{1,0:T(1,128)} %atom_hbm.5, s32[1,96]{1,0:T(1,128)} %cell_hbm.5, s32[1,1]{1,0:T(1,128)S(6)} %copy.12.live_ref, bf16[96,64,512]{2,1,0:T(8,128)(2,1)S(1)} %bitcast.8, bf16[32,32]{1,0:T(8,128)(2,1)S(1)} %copy-done.2, ...), custom_call_target="tpu_custom_call" | custom-call | tf_op jit(solution)/shard_map/gather/pallas_call | solution.py:425
  (5 shorter events, 0.0 us)
Async XLA Ops:
  0.6 9.2 %copy-start.1 = (bf16[1,32,1536]{2,1,0:T(8,128)(2,1)S(1)}, bf16[1,32,1536]{2,1,0:T(8,128)(2,1)}, u32[]{:S(2)}) copy-start(bf16[1,32,1536]{2,1,0:T(8,128)(2,1)} %param.15) | copy-start | bytes 294916
  1.3 13.2 %copy-start = (bf16[27,32,32]{2,1,0:T(8,128)(2,1)S(1)}, bf16[27,32,32]{2,1,0:T(8,128)(2,1)}, u32[]{:S(2)}) copy-start(bf16[27,32,32]{2,1,0:T(8,128)(2,1)} %conv_ref.3) | copy-start | bytes 165892
  1.3 20.8 %copy-start.2 = (bf16[32,32]{1,0:T(8,128)(2,1)S(1)}, bf16[32,32]{1,0:T(8,128)(2,1)}, u32[]{:S(2)}) copy-start(bf16[32,32]{1,0:T(8,128)(2,1)} %mix_ref.5) | copy-start | bytes 6148
  1.3 57.0 %slice-start = ((s8[6291456]{0:T(1024)(128)(4,1)}), s8[4194304]{0:T(1024)(128)(4,1)S(1)}, s32[]{:S(2)}) async-start(s8[6291456]{0:T(1024)(128)(4,1)} %bitcast.6), calls=%async_computation | async-start | bytes 8388608
  6.4 12.9 %collective-permute-start.1 = (bf16[12,32,512]{2,1,0:T(8,128)(2,1)S(1)}, bf16[12,32,512]{2,1,0:T(8,128)(2,1)S(1)}, u32[]{:S(2)}, u32[]{:S(2)}) collective-permute-start(bf16[12,32,512]{2,1,0:T(8,128)(2,1)S(1)} %get-tuple-element.27.down), channel_id=1, source_target_pairs={{0,7},{1,0},{2,1},{3,2},{4,3},{5,4},{6,5},{7,6},{8,15},{9,8},{10,9... | collective-permute-start | bytes 1179656 | tf_op jit(solution)/shard_map/ppermute | solution.py:479
  9.8 12.3 %collective-permute-start = (bf16[12,32,512]{2,1,0:T(8,128)(2,1)S(1)}, bf16[12,32,512]{2,1,0:T(8,128)(2,1)S(1)}, u32[]{:S(2)}, u32[]{:S(2)}) collective-permute-start(bf16[12,32,512]{2,1,0:T(8,128)(2,1)S(1)} %get-tuple-element.29.up), channel_id=1, source_target_pairs={{0,1},{1,2},{2,3},{3,4},{4,5},{5,6},{6,7},{7,0},{8,9},{9,10},{10,1... | collective-permute-start | bytes 1179656 | tf_op jit(solution)/shard_map/ppermute | solution.py:479
  9.8 48.6 %slice-start.1 = ((s8[6291456]{0:T(1024)(128)(4,1)}), s8[2097152]{0:T(1024)(128)(4,1)S(1)}, s32[]{:S(2)}) async-start(s8[6291456]{0:T(1024)(128)(4,1)} %bitcast.6), calls=%async_computation.1 | async-start | bytes 4194304
  11.8 12.3 %collective-permute-start.7 = (bf16[8,32,512]{2,1,0:T(8,128)(2,1)S(1)}, bf16[8,32,512]{2,1,0:T(8,128)(2,1)S(1)}, u32[]{:S(2)}, u32[]{:S(2)}) collective-permute-start(bf16[8,32,512]{2,1,0:T(8,128)(2,1)S(1)} %get-tuple-element.34.down), channel_id=1, source_target_pairs={{0,7},{1,0},{2,1},{3,2},{4,3},{5,4},{6,5},{7,6},{8,15},{9,8},{10,9... | collective-permute-start | bytes 786440 | tf_op jit(solution)/shard_map/ppermute | solution.py:479
  14.5 11.5 %collective-permute-start.6 = (bf16[8,32,512]{2,1,0:T(8,128)(2,1)S(1)}, bf16[8,32,512]{2,1,0:T(8,128)(2,1)S(1)}, u32[]{:S(2)}, u32[]{:S(2)}) collective-permute-start(bf16[8,32,512]{2,1,0:T(8,128)(2,1)S(1)} %get-tuple-element.35.up), channel_id=1, source_target_pairs={{0,1},{1,2},{2,3},{3,4},{4,5},{5,6},{6,7},{7,0},{8,9},{9,10},{10,1... | collective-permute-start | bytes 786440 | tf_op jit(solution)/shard_map/ppermute | solution.py:479
  28.0 2.8 %collective-permute-start.10 = (bf16[144,128]{1,0:T(8,128)(2,1)S(1)}, bf16[144,128]{1,0:T(8,128)(2,1)S(1)}, u32[]{:S(2)}, u32[]{:S(2)}) collective-permute-start(bf16[144,128]{1,0:T(8,128)(2,1)S(1)} %get-tuple-element.47), channel_id=1, source_target_pairs={{0,1},{1,0},{2,3},{3,2},{4,5},{5,4},{6,7},{7,6},{8,9},{9,8},{10,11... | collective-permute-start | bytes 110600 | tf_op jit(solution)/shard_map/ppermute | solution.py:485
  28.1 15.3 %collective-permute-start.4 = (bf16[4,32,512]{2,1,0:T(8,128)(2,1)S(1)}, bf16[4,32,512]{2,1,0:T(8,128)(2,1)S(1)}, u32[]{:S(2)}, u32[]{:S(2)}) collective-permute-start(bf16[4,32,512]{2,1,0:T(8,128)(2,1)S(1)} %get-tuple-element.36.high), channel_id=1, source_target_pairs={{0,1},{1,2},{2,3},{3,4},{4,5},{5,6},{6,7},{7,0},{8,9},{9,10},{10,1... | collective-permute-start | bytes 393224 | tf_op jit(solution)/shard_map/ppermute | solution.py:479
  28.6 14.8 %collective-permute-start.5 = (bf16[4,32,512]{2,1,0:T(8,128)(2,1)S(1)}, bf16[4,32,512]{2,1,0:T(8,128)(2,1)S(1)}, u32[]{:S(2)}, u32[]{:S(2)}) collective-permute-start(bf16[4,32,512]{2,1,0:T(8,128)(2,1)S(1)} %get-tuple-element.37.low), channel_id=1, source_target_pairs={{0,7},{1,0},{2,1},{3,2},{4,3},{5,4},{6,5},{7,6},{8,15},{9,8},{10,9... | collective-permute-start | bytes 393224 | tf_op jit(solution)/shard_map/ppermute | solution.py:479
  30.8 4.0 %collective-permute-start.11 = (bf16[144,128]{1,0:T(8,128)(2,1)S(1)}, bf16[144,128]{1,0:T(8,128)(2,1)S(1)}, u32[]{:S(2)}, u32[]{:S(2)}) collective-permute-start(bf16[144,128]{1,0:T(8,128)(2,1)S(1)} %add_convert_fusion), channel_id=1, source_target_pairs={{0,8},{8,0},{16,24},{24,16},{1,9},{9,1},{17,25},{25,17},{2,10},{10... | collective-permute-start | bytes 110600 | tf_op jit(solution)/shard_map/ppermute | solution.py:485
  34.9 4.9 %collective-permute-start.12 = (bf16[144,128]{1,0:T(8,128)(2,1)S(1)}, bf16[144,128]{1,0:T(8,128)(2,1)S(1)}, u32[]{:S(2)}, u32[]{:S(2)}) collective-permute-start(bf16[144,128]{1,0:T(8,128)(2,1)S(1)} %add.19), channel_id=1, source_target_pairs={{0,16},{8,24},{16,0},{24,8},{1,17},{9,25},{17,1},{25,9},{2,18},{10... | collective-permute-start | bytes 110600 | tf_op jit(solution)/shard_map/ppermute | solution.py:485
  39.8 7.9 %collective-permute-start.15 = (bf16[144,128]{1,0:T(8,128)(2,1)S(1)}, bf16[144,128]{1,0:T(8,128)(2,1)S(1)}, u32[]{:S(2)}, u32[]{:S(2)}) collective-permute-start(bf16[144,128]{1,0:T(8,128)(2,1)S(1)} %add.20), channel_id=1, source_target_pairs={{0,6},{1,7},{2,4},{3,5},{4,2},{5,3},{6,0},{7,1},{8,14},{9,15},{10,... | collective-permute-start | bytes 110600 | tf_op jit(solution)/shard_map/ppermute | solution.py:485
  40.4 7.4 %collective-permute-start.14 = (bf16[144,128]{1,0:T(8,128)(2,1)S(1)}, bf16[144,128]{1,0:T(8,128)(2,1)S(1)}, u32[]{:S(2)}, u32[]{:S(2)}) collective-permute-start(bf16[144,128]{1,0:T(8,128)(2,1)S(1)} %add.20), channel_id=1, source_target_pairs={{0,4},{1,5},{2,6},{3,7},{4,0},{5,1},{6,2},{7,3},{8,12},{9,13},{10,... | collective-permute-start | bytes 110600 | tf_op jit(solution)/shard_map/ppermute | solution.py:485
  41.5 9.0 %collective-permute-start.13 = (bf16[144,128]{1,0:T(8,128)(2,1)S(1)}, bf16[144,128]{1,0:T(8,128)(2,1)S(1)}, u32[]{:S(2)}, u32[]{:S(2)}) collective-permute-start(bf16[144,128]{1,0:T(8,128)(2,1)S(1)} %add.20), channel_id=1, source_target_pairs={{0,2},{1,3},{2,0},{3,1},{4,6},{5,7},{6,4},{7,5},{8,10},{9,11},{10,... | collective-permute-start | bytes 110600 | tf_op jit(solution)/shard_map/ppermute | solution.py:485
  43.4 9.6 %collective-permute-start.2 = (bf16[8,32,512]{2,1,0:T(8,128)(2,1)S(1)}, bf16[8,32,512]{2,1,0:T(8,128)(2,1)S(1)}, u32[]{:S(2)}, u32[]{:S(2)}) collective-permute-start(bf16[8,32,512]{2,1,0:T(8,128)(2,1)S(1)} %get-tuple-element.31.a2), channel_id=1, source_target_pairs={{0,1},{1,2},{2,3},{3,4},{4,5},{5,6},{6,7},{7,0},{8,9},{9,10},{10,1... | collective-permute-start | bytes 786440 | tf_op jit(solution)/shard_map/ppermute | solution.py:479
  43.4 9.6 %collective-permute-start.3 = (bf16[8,32,512]{2,1,0:T(8,128)(2,1)S(1)}, bf16[8,32,512]{2,1,0:T(8,128)(2,1)S(1)}, u32[]{:S(2)}, u32[]{:S(2)}) collective-permute-start(bf16[8,32,512]{2,1,0:T(8,128)(2,1)S(1)} %get-tuple-element.32.a1), channel_id=1, source_target_pairs={{0,7},{1,0},{2,1},{3,2},{4,3},{5,4},{6,5},{7,6},{8,15},{9,8},{10,9... | collective-permute-start | bytes 786440 | tf_op jit(solution)/shard_map/ppermute | solution.py:479
  47.7 10.6 %collective-permute-start.8 = (bf16[8,32,512]{2,1,0:T(8,128)(2,1)S(1)}, bf16[8,32,512]{2,1,0:T(8,128)(2,1)S(1)}, u32[]{:S(2)}, u32[]{:S(2)}) collective-permute-start(bf16[8,32,512]{2,1,0:T(8,128)(2,1)S(1)} %get-tuple-element.42.b2), channel_id=1, source_target_pairs={{0,1},{1,2},{2,3},{3,4},{4,5},{5,6},{6,7},{7,0},{8,9},{9,10},{10,1... | collective-permute-start | bytes 786440 | tf_op jit(solution)/shard_map/ppermute | solution.py:479
  47.8 10.6 %collective-permute-start.9 = (bf16[8,32,512]{2,1,0:T(8,128)(2,1)S(1)}, bf16[8,32,512]{2,1,0:T(8,128)(2,1)S(1)}, u32[]{:S(2)}, u32[]{:S(2)}) collective-permute-start(bf16[8,32,512]{2,1,0:T(8,128)(2,1)S(1)} %get-tuple-element.43.b1), channel_id=1, source_target_pairs={{0,7},{1,0},{2,1},{3,2},{4,3},{5,4},{6,5},{7,6},{8,15},{9,8},{10,9... | collective-permute-start | bytes 786440 | tf_op jit(solution)/shard_map/ppermute | solution.py:479
  50.5 1.3 %collective-permute-start.16 = (bf16[144,128]{1,0:T(8,128)(2,1)S(1)}, bf16[144,128]{1,0:T(8,128)(2,1)S(1)}, u32[]{:S(2)}, u32[]{:S(2)}) collective-permute-start(bf16[144,128]{1,0:T(8,128)(2,1)S(1)} %add_add_fusion.mine_ref), channel_id=1, source_target_pairs={{0,1},{1,0},{2,3},{3,2},{4,5},{5,4},{6,7},{7,6},{8,9},{9,8},{10,11... | collective-permute-start | bytes 110600 | tf_op jit(solution)/shard_map/ppermute | solution.py:485

commit v3 on v2

--- a/solution.py
+++ b/solution.py
@@ -146,7 +146,7 @@
         out_shape=parts + [pltpu.VMEM(weights.shape, BF16)],
         scratch_shapes=list_scratch(atom_ids, cell_ids)
         + scratch
-        + [pltpu.VMEM(feats.shape, BF16), pltpu.SemaphoreType.DMA((8,))],
+        + [pltpu.VMEM(feats.shape, BF16), pltpu.SemaphoreType.DMA((2,))],
         compiler_params=params(),
         name="first_deposit",
     )(*in_hbm(atom_ids, cell_ids), live, *in_hbm(feats, weights))
@@ -275,33 +275,29 @@
     other = ((below, 0, ZH + 1), (above, 0, ZH + 1))
     for p, plane in enumerate(joined_planes(own, other, quarters)):
         plane = plane.astype(BF16)
-        plain_ref[p * channels : (p + 1) * channels] = plane
+        store_shifted(plain_ref, p * channels, plane)
         mixed = jnp.dot(mix_ref[...], plane, preferred_element_type=F32)
         store_shifted(shifted, p * channels, mixed.astype(BF16))
     conv_planes(matrix_ref, shifted, partial, low_ref, high_ref)
 
 
 def gradient_kernel(
-    low, middle, high, below, above, plain_ref,
-    keep_ref, send_ref, sums_ref, shifted, upstream,
+    low, middle, high, below, above, shifted,
+    keep_ref, send_ref, sums_ref, upstream,
 ):
     channels = low.shape[1]
     quarters = low.shape[0]
-    cells = plain_ref.shape[1]
-    for p in range(ZD + 2):
-        rows = slice(p * channels, (p + 1) * channels)
-        store_shifted(shifted, p * channels, plain_ref[rows])
+    cells = shifted.shape[1]
     own = ((low, 0, 1), (middle, 0, ZD - 2), (high, 0, 1))
     planes = joined_planes(own, ((below, 0, ZH), (above, 0, ZH)), quarters)
     third = ZD * channels
     for p, plane in enumerate(planes):
         row = p * channels
-        sums_ref[row : row + channels] = plane.astype(BF16)
-        upstream[row : row + channels] = pltpu.roll(plane, cells - GX, 1).astype(BF16)
-        upstream[third + row : third + row + channels] = plane.astype(BF16)
-        upstream[2 * third + row : 2 * third + row + channels] = pltpu.roll(
-            plane, GX, 1
-        ).astype(BF16)
+        plane = plane.astype(BF16)
+        sums_ref[row : row + channels] = plane
+        upstream[row : row + channels] = pltpu.roll(plane, cells - GX, 1)
+        upstream[third + row : third + row + channels] = plane
+        upstream[2 * third + row : 2 * third + row + channels] = pltpu.roll(plane, GX, 1)
     wide = (ZD + 2) * channels
     blocks = []
     for dx in range(3):
@@ -354,16 +350,12 @@
 
 
 def gather_kernel(
-    atom_hbm, cell_hbm, live_ref, weight_ref, mix_ref,
-    a0, a1, a2, a3, b0, b1, b2, b3, potential_ref, grad_ref,
-    atom_ref, cell_ref, small_sems, field, total,
+    atom_ref, cell_ref, live_ref, weight_ref, mix_ref,
+    a0, a1, a2, a3, b0, b1, b2, b3, potential_ref, grad_ref, field, total,
 ):
     channels = mix_ref.shape[0]
     tiles, tile_a, tile_c = weight_ref.shape
     half = tile_c // 2
-    small = copies(((atom_hbm, atom_ref), (cell_hbm, cell_ref)), small_sems)
-    for copy in small:
-        copy.start()
     first = 0
     for a, b in ((a0, b0), (a1, b1), (a2, b2), (a3, b3)):
         count = a.shape[0]
@@ -375,8 +367,6 @@
             ]
         first += count
     total[...] = jnp.zeros_like(total)
-    for copy in small:
-        copy.wait()
     live = live_ref[0, 0]
     lane = lax.broadcasted_iota(jnp.int32, (2 * channels, 2 * tile_a), 1)
     for j in range(0, tiles, 2):
@@ -424,17 +414,16 @@
     shape = jax.ShapeDtypeStruct((channels, atoms), BF16)
     return pl.pallas_call(
         gather_kernel,
-        in_specs=list_specs() + [whole()] * 10,
+        in_specs=[pl.BlockSpec(memory_space=pltpu.SMEM)] * 3 + [whole()] * 10,
         out_specs=[whole()] * 2,
         out_shape=[shape, shape],
-        scratch_shapes=list_scratch(atom_ids, cell_ids)
-        + [
+        scratch_shapes=[
             pltpu.VMEM((blocks, 4 * channels, tile_c // 2), BF16),
             pltpu.VMEM((atoms // tile_a, 2 * channels, 2 * tile_a), F32),
         ],
         compiler_params=params(),
         name="gather",
-    )(*in_hbm(atom_ids, cell_ids), live, weights, w_mix, *phi, *drho)
+    )(atom_ids, cell_ids, live, weights, w_mix, *phi, *drho)
 
 
 def finish_kernel(
@@ -516,7 +505,7 @@
         forward_kernel,
         in_specs=[whole()] * 7,
         out_specs=[whole()] * 3,
-        out_shape=[half, half, pltpu.VMEM((rows, cells), BF16)],
+        out_shape=[half, half, pltpu.VMEM((3 * rows, cells), BF16)],
         scratch_shapes=scratch,
         compiler_params=params(),
         name="forward",
@@ -529,7 +518,7 @@
         in_specs=[whole()] * 6,
         out_specs=[whole()] * 3,
         out_shape=[pltpu.VMEM(part.shape, F32), part, pltpu.VMEM((ZD * channels, cells), BF16)],
-        scratch_shapes=[scratch[0], pltpu.VMEM((3 * ZD * channels, cells), BF16)],
+        scratch_shapes=[pltpu.VMEM((3 * ZD * channels, cells), BF16)],
         compiler_params=params(),
         name="gradient",
     )(el, em, eh, e_below, e_above, plain)
@@ -578,7 +567,7 @@
     potential, feats_grad = gather(
         (phi_below, phi_low, phi_high, phi_above),
         (drho_below, drho_low, drho_high, drho_above),
-        weights, atom_ids, cell_ids, live, w_mix, atoms,
+        held, atom_ids, cell_ids, live, w_mix, atoms,
     )
     return potential[None], feats_grad[None], conv_grad, mix_grad
 

time: 62.3 us -> 61.8 us (level)
  starting transfers between devices: 22.1 us -> 23.9 us
  waiting for transfers between devices: 20 us -> 18.9 us
  Pallas kernels: 18.3 us -> 17.3 us
    ppermute x7, starting transfers between devices: 8 us -> 9.74 us  [exchanged(): return lax.ppermute(value, axis, [(i, i ^ stride) for i in range(count)])]
    pallas_call x1, Pallas kernels: 5.03 us -> 3.64 us  [first_deposit(): pl.pallas_call(first_deposit_kernel, in_specs=list_specs() + [hbm()] * 2,...]
    ppermute x10, waiting for transfers between devices: 14.2 us -> 13.1 us  [ring(): lax.ppermute(value, axis, pairs)]
    pallas_call x1, Pallas kernels: 1.95 us -> 2.85 us  [step(): pl.pallas_call(forward_kernel, in_specs=[whole()] * 7, out_specs=[whole()...]
  transfers between devices with their start and end apart: 17 -> 17, of which waited for: 7 -> 9; matrix products, arithmetic and copies ran while one was open for 0% -> 0% of each run, Pallas kernels for 12% -> 14%
where the time goes in v3:
time: 61.8 us; the launch traced here: 61.6 us
  starting transfers between devices  23.9 us (39%)
  waiting for transfers between devices  18.9 us (31%)
  Pallas kernels  17.3 us (28%)
  between operations  1.44 us (2%)
    ppermute x10, starting transfers between devices, ring(): lax.ppermute(value, axis, pairs)  14.2 us
    ppermute x10, waiting for transfers between devices, ring(): lax.ppermute(value, axis, pairs)  13.1 us
    ppermute x7, starting transfers between devices, exchanged(): return lax.ppermute(value, axis, [(i, i ^ stride) for i in range(count)])  9.74 us
    ppermute x7, waiting for transfers between devices, exchanged(): return lax.ppermute(value, axis, [(i, i ^ stride) for i in range(count)])  5.87 us
    pallas_call x1, Pallas kernels, first_deposit(): pl.pallas_call(first_deposit_kernel, in_specs=list_specs() + [hbm()] * 2,...  3.64 us
    pallas_call x1, Pallas kernels, gather(): pl.pallas_call(gather_kernel, in_specs=[pl.BlockSpec(memory_space=pltpu.S...  3.51 us
    pallas_call x1, Pallas kernels, step(): pl.pallas_call(forward_kernel, in_specs=[whole()] * 7, out_specs=[whole()...  2.85 us
    pallas_call x1, Pallas kernels, second_deposit(): pl.pallas_call(second_deposit_kernel, in_specs=list_specs() + [whole()] *...  1.97 us
  transfers between devices with their start and end apart: 17, of which 9 were waited for; matrix products, arithmetic and copies ran while one was open for 0% of the time, Pallas kernels for 14%

profile of v3, /device:TPU:0, one launch (start us, length us, event | category | flops | bytes accessed | tf_op | source)
XLA Modules:
  0.0 61.6 jit_solution(17022762013338576617)
XLA Ops:
  0.6 0.0 copy-start.1
  1.3 0.0 copy-start
  1.3 0.0 copy-start.2
  1.3 3.6 %first_deposit.1 = (bf16[12,32,512]{2,1,0:T(8,128)(2,1)S(1)}, bf16[8,32,512]{2,1,0:T(8,128)(2,1)S(1)}, bf16[12,32,512]{2,1,0:T(8,128)(2,1)S(1)}, bf16[96,64,512]{2,1,0:T(8,128)(2,1)S(1)}) custom-call(s32[1,96]{1,0:T(1,128)} %atom_ref.1, s32[1,96]{1,0:T(1,128)} %cell_ref.1, s32[1,1]{1,0:T(1,128)S(6)} %copy.12.live_ref, bf16[32,1536]{1,0:T(8,128)(2,1)} %bitcast.7, ...), custom_call_target="tpu_custom_call" | custom-call | tf_op jit(solution)/shard_map/first_deposit/pallas_call | solution.py:142
  5.0 0.6 collective-permute-start
  5.5 2.9 %collective-permute-start.1 = (bf16[12,32,512]{2,1,0:T(8,128)(2,1)S(1)}, bf16[12,32,512]{2,1,0:T(8,128)(2,1)S(1)}, u32[]{:S(2)}, u32[]{:S(2)}) collective-permute-start(bf16[12,32,512]{2,1,0:T(8,128)(2,1)S(1)} %get-tuple-element.28.down), channel_id=1, source_target_pairs={{0,7},{1,0},{2,1},{3,2},{4,3},{5,4},{6,5},{7,6},{8,15},{9,8},{10,9... | collective-permute-start | bytes 1179656 | tf_op jit(solution)/shard_map/ppermute | solution.py:468
  8.5 0.0 copy-done.1
  8.5 0.0 copy-start.3
  8.5 0.0 copy-start.4
  8.5 2.0 %second_deposit.1 = (bf16[8,32,512]{2,1,0:T(8,128)(2,1)S(1)}, bf16[4,32,512]{2,1,0:T(8,128)(2,1)S(1)}, bf16[8,32,512]{2,1,0:T(8,128)(2,1)S(1)}, bf16[4,32,512]{2,1,0:T(8,128)(2,1)S(1)}, bf16[8,32,512]{2,1,0:T(8,128)(2,1)S(1)}) custom-call(s32[1,96]{1,0:T(1,128)} %atom_ref.1, s32[1,96]{1,0:T(1,128)} %cell_ref.1, s32[1,1]{1,0:T(1,128)S(6)} %copy.12.live_ref, ...), custom_call_target="tpu_custom_call" | custom-call | tf_op jit(solution)/shard_map/second_deposit/pallas_call | solution.py:157
  10.5 0.1 collective-permute-start.6
  10.5 2.6 %collective-permute-start.7 = (bf16[8,32,512]{2,1,0:T(8,128)(2,1)S(1)}, bf16[8,32,512]{2,1,0:T(8,128)(2,1)S(1)}, u32[]{:S(2)}, u32[]{:S(2)}) collective-permute-start(bf16[8,32,512]{2,1,0:T(8,128)(2,1)S(1)} %get-tuple-element.34.down), channel_id=1, source_target_pairs={{0,7},{1,0},{2,1},{3,2},{4,3},{5,4},{6,5},{7,6},{8,15},{9,8},{10,9... | collective-permute-start | bytes 786440 | tf_op jit(solution)/shard_map/ppermute | solution.py:468
  13.2 0.0 copy-done
  13.2 0.8 %toeplitz.1 = (bf16[384,576]{1,0:T(8,128)(2,1)S(1)}, bf16[384,576]{1,0:T(8,128)(2,1)S(1)}) custom-call(bf16[27,32,32]{2,1,0:T(8,128)(2,1)S(1)} %copy-done), custom_call_target="tpu_custom_call" | custom-call | tf_op jit(solution)/shard_map/toeplitz/pallas_call | solution.py:200
  13.9 1.6 %collective-permute-done.below = bf16[12,32,512]{2,1,0:T(8,128)(2,1)S(1)} collective-permute-done((bf16[12,32,512]{2,1,0:T(8,128)(2,1)S(1)}, bf16[12,32,512]{2,1,0:T(8,128)(2,1)S(1)}, u32[]{:S(2)}, u32[]{:S(2)}) %collective-permute-start) | collective-permute-done | bytes 393248 | tf_op jit(solution)/shard_map/ppermute | solution.py:468
  15.5 2.5 %collective-permute-done.1.above = bf16[12,32,512]{2,1,0:T(8,128)(2,1)S(1)} collective-permute-done((bf16[12,32,512]{2,1,0:T(8,128)(2,1)S(1)}, bf16[12,32,512]{2,1,0:T(8,128)(2,1)S(1)}, u32[]{:S(2)}, u32[]{:S(2)}) %collective-permute-start.1) | collective-permute-done | bytes 393248 | tf_op jit(solution)/shard_map/ppermute | solution.py:468
  18.0 0.0 copy-done.2
  18.0 2.9 %forward.1 = (bf16[8,32,512]{2,1,0:T(8,128)(2,1)S(1)}, bf16[8,32,512]{2,1,0:T(8,128)(2,1)S(1)}, bf16[576,2048]{1,0:T(8,128)(2,1)S(1)}) custom-call(bf16[12,32,512]{2,1,0:T(8,128)(2,1)S(1)} %get-tuple-element.28.down, bf16[8,32,512]{2,1,0:T(8,128)(2,1)S(1)} %get-tuple-element.29.middle, bf16[12,32,512]{2,1,0:T(8,128)(2,1)S(1)} %get-tuple-element.30.up, ...), custom_call_target="tpu_custom_call" | custom-call | tf_op jit(solution)/shard_map/forward/pallas_call | solution.py:504
  20.8 0.3 collective-permute-done.6.below
  21.1 1.5 %collective-permute-done.7.above = bf16[8,32,512]{2,1,0:T(8,128)(2,1)S(1)} collective-permute-done((bf16[8,32,512]{2,1,0:T(8,128)(2,1)S(1)}, bf16[8,32,512]{2,1,0:T(8,128)(2,1)S(1)}, u32[]{:S(2)}, u32[]{:S(2)}) %collective-permute-start.7) | collective-permute-done | bytes 262176 | tf_op jit(solution)/shard_map/ppermute | solution.py:468
  22.6 1.6 %gradient.1 = (f32[144,128]{1,0:T(8,128)S(1)}, bf16[144,128]{1,0:T(8,128)(2,1)S(1)}, bf16[128,2048]{1,0:T(8,128)(2,1)S(1)}) custom-call(bf16[4,32,512]{2,1,0:T(8,128)(2,1)S(1)} %get-tuple-element.37.low, bf16[8,32,512]{2,1,0:T(8,128)(2,1)S(1)} %get-tuple-element.38.middle, bf16[4,32,512]{2,1,0:T(8,128)(2,1)S(1)} %get-tuple-element.36.high, ...), custom_call_target="tpu_custom_call" | custom-call | tf_op jit(solution)/shard_map/gradient/pallas_call | solution.py:516
  24.2 1.8 %collective-permute-start.10 = (bf16[144,128]{1,0:T(8,128)(2,1)S(1)}, bf16[144,128]{1,0:T(8,128)(2,1)S(1)}, u32[]{:S(2)}, u32[]{:S(2)}) collective-permute-start(bf16[144,128]{1,0:T(8,128)(2,1)S(1)} %get-tuple-element.47), channel_id=1, source_target_pairs={{0,1},{1,0},{2,3},{3,2},{4,5},{5,4},{6,7},{7,6},{8,9},{9,8},{10,11... | collective-permute-start | bytes 110600 | tf_op jit(solution)/shard_map/ppermute | solution.py:474
  26.0 0.1 collective-permute-start.4
  26.1 2.6 %collective-permute-start.5 = (bf16[4,32,512]{2,1,0:T(8,128)(2,1)S(1)}, bf16[4,32,512]{2,1,0:T(8,128)(2,1)S(1)}, u32[]{:S(2)}, u32[]{:S(2)}) collective-permute-start(bf16[4,32,512]{2,1,0:T(8,128)(2,1)S(1)} %get-tuple-element.37.low), channel_id=1, source_target_pairs={{0,7},{1,0},{2,1},{3,2},{4,3},{5,4},{6,5},{7,6},{8,15},{9,8},{10,9... | collective-permute-start | bytes 393224 | tf_op jit(solution)/shard_map/ppermute | solution.py:468
  28.6 0.0 collective-permute-done.10
  28.7 1.6 %collective-permute-start.11 = (bf16[144,128]{1,0:T(8,128)(2,1)S(1)}, bf16[144,128]{1,0:T(8,128)(2,1)S(1)}, u32[]{:S(2)}, u32[]{:S(2)}) collective-permute-start(bf16[144,128]{1,0:T(8,128)(2,1)S(1)} %add_convert_fusion), channel_id=1, source_target_pairs={{0,8},{8,0},{16,24},{24,16},{1,9},{9,1},{17,25},{25,17},{2,10},{10... | collective-permute-start | bytes 110600 | tf_op jit(solution)/shard_map/ppermute | solution.py:474
  30.3 2.4 %collective-permute-done.11 = bf16[144,128]{1,0:T(8,128)(2,1)S(1)} collective-permute-done((bf16[144,128]{1,0:T(8,128)(2,1)S(1)}, bf16[144,128]{1,0:T(8,128)(2,1)S(1)}, u32[]{:S(2)}, u32[]{:S(2)}) %collective-permute-start.11) | collective-permute-done | bytes 36896 | tf_op jit(solution)/shard_map/ppermute | solution.py:474
  32.7 2.7 %collective-permute-start.12 = (bf16[144,128]{1,0:T(8,128)(2,1)S(1)}, bf16[144,128]{1,0:T(8,128)(2,1)S(1)}, u32[]{:S(2)}, u32[]{:S(2)}) collective-permute-start(bf16[144,128]{1,0:T(8,128)(2,1)S(1)} %add.19), channel_id=1, source_target_pairs={{0,16},{8,24},{16,0},{24,8},{1,17},{9,25},{17,1},{25,9},{2,18},{10... | collective-permute-start | bytes 110600 | tf_op jit(solution)/shard_map/ppermute | solution.py:474
  35.3 2.3 %collective-permute-done.12 = bf16[144,128]{1,0:T(8,128)(2,1)S(1)} collective-permute-done((bf16[144,128]{1,0:T(8,128)(2,1)S(1)}, bf16[144,128]{1,0:T(8,128)(2,1)S(1)}, u32[]{:S(2)}, u32[]{:S(2)}) %collective-permute-start.12) | collective-permute-done | bytes 36896 | tf_op jit(solution)/shard_map/ppermute | solution.py:474
  37.6 0.7 %collective-permute-start.13 = (bf16[144,128]{1,0:T(8,128)(2,1)S(1)}, bf16[144,128]{1,0:T(8,128)(2,1)S(1)}, u32[]{:S(2)}, u32[]{:S(2)}) collective-permute-start(bf16[144,128]{1,0:T(8,128)(2,1)S(1)} %add.20), channel_id=1, source_target_pairs={{0,2},{1,3},{2,0},{3,1},{4,6},{5,7},{6,4},{7,5},{8,10},{9,11},{10,... | collective-permute-start | bytes 110600 | tf_op jit(solution)/shard_map/ppermute | solution.py:474
  38.3 0.5 collective-permute-start.14
  38.8 2.4 %collective-permute-start.15 = (bf16[144,128]{1,0:T(8,128)(2,1)S(1)}, bf16[144,128]{1,0:T(8,128)(2,1)S(1)}, u32[]{:S(2)}, u32[]{:S(2)}) collective-permute-start(bf16[144,128]{1,0:T(8,128)(2,1)S(1)} %add.20), channel_id=1, source_target_pairs={{0,6},{1,7},{2,4},{3,5},{4,2},{5,3},{6,0},{7,1},{8,14},{9,15},{10,... | collective-permute-start | bytes 110600 | tf_op jit(solution)/shard_map/ppermute | solution.py:474
  41.2 0.0 collective-permute-done.4.below
  41.2 0.0 collective-permute-done.5.above
  41.2 1.8 %backward.1 = (bf16[8,32,512]{2,1,0:T(8,128)(2,1)S(1)}, bf16[8,32,512]{2,1,0:T(8,128)(2,1)S(1)}) custom-call(bf16[8,32,512]{2,1,0:T(8,128)(2,1)S(1)} %get-tuple-element.34.down, bf16[8,32,512]{2,1,0:T(8,128)(2,1)S(1)} %get-tuple-element.35.up, bf16[4,32,512]{2,1,0:T(8,128)(2,1)S(1)} %collective-permute-done.4.below, ...), custom_call_target="tpu_custom_call" | custom-call | tf_op jit(solution)/shard_map/backward/pallas_call | solution.py:526
  43.0 0.1 collective-permute-start.8
  43.0 2.6 %collective-permute-start.9 = (bf16[8,32,512]{2,1,0:T(8,128)(2,1)S(1)}, bf16[8,32,512]{2,1,0:T(8,128)(2,1)S(1)}, u32[]{:S(2)}, u32[]{:S(2)}) collective-permute-start(bf16[8,32,512]{2,1,0:T(8,128)(2,1)S(1)} %get-tuple-element.43.b1), channel_id=1, source_target_pairs={{0,7},{1,0},{2,1},{3,2},{4,3},{5,4},{6,5},{7,6},{8,15},{9,8},{10,9... | collective-permute-start | bytes 786440 | tf_op jit(solution)/shard_map/ppermute | solution.py:468
  45.7 0.0 collective-permute-done.13
  45.7 0.0 collective-permute-start.2
  45.7 0.0 collective-permute-done.14
  45.7 2.6 %collective-permute-start.3 = (bf16[8,32,512]{2,1,0:T(8,128)(2,1)S(1)}, bf16[8,32,512]{2,1,0:T(8,128)(2,1)S(1)}, u32[]{:S(2)}, u32[]{:S(2)}) collective-permute-start(bf16[8,32,512]{2,1,0:T(8,128)(2,1)S(1)} %get-tuple-element.33.a1), channel_id=1, source_target_pairs={{0,7},{1,0},{2,1},{3,2},{4,3},{5,4},{6,5},{7,6},{8,15},{9,8},{10,9... | collective-permute-start | bytes 786440 | tf_op jit(solution)/shard_map/ppermute | solution.py:468
  48.3 0.0 collective-permute-done.15
  48.3 0.1 collective-permute-start.16
  48.4 1.2 %collective-permute-done.16.other_ref = bf16[144,128]{1,0:T(8,128)(2,1)S(1)} collective-permute-done((bf16[144,128]{1,0:T(8,128)(2,1)S(1)}, bf16[144,128]{1,0:T(8,128)(2,1)S(1)}, u32[]{:S(2)}, u32[]{:S(2)}) %collective-permute-start.16) | collective-permute-done | bytes 36896 | tf_op jit(solution)/shard_map/ppermute | solution.py:474
  49.6 1.2 %finish.1 = (f32[27,32,32]{2,1,0:T(8,128)}, f32[32,32]{1,0:T(8,128)}) custom-call(bf16[144,128]{1,0:T(8,128)(2,1)S(1)} %add_add_fusion.mine_ref, bf16[144,128]{1,0:T(8,128)(2,1)S(1)} %collective-permute-done.16.other_ref, bf16[32,32]{1,0:T(8,128)(2,1)S(1)} %copy-done.2, bf16[27,32,32]{2,1,0:T(8,128)(2,1)S(1)} %copy-done), custom_call_target="tpu_custom_call" | custom-call | tf_op jit(solution)/shard_map/finish/pallas_call | solution.py:551
  50.8 1.7 %collective-permute-done.8.b0 = bf16[8,32,512]{2,1,0:T(8,128)(2,1)S(1)} collective-permute-done((bf16[8,32,512]{2,1,0:T(8,128)(2,1)S(1)}, bf16[8,32,512]{2,1,0:T(8,128)(2,1)S(1)}, u32[]{:S(2)}, u32[]{:S(2)}) %collective-permute-start.8) | collective-permute-done | bytes 262176 | tf_op jit(solution)/shard_map/ppermute | solution.py:468
  52.5 0.0 collective-permute-done.9.b3
  52.5 5.6 %collective-permute-done.2.a0 = bf16[8,32,512]{2,1,0:T(8,128)(2,1)S(1)} collective-permute-done((bf16[8,32,512]{2,1,0:T(8,128)(2,1)S(1)}, bf16[8,32,512]{2,1,0:T(8,128)(2,1)S(1)}, u32[]{:S(2)}, u32[]{:S(2)}) %collective-permute-start.2) | collective-permute-done | bytes 262176 | tf_op jit(solution)/shard_map/ppermute | solution.py:468
  58.1 0.0 collective-permute-done.3.a3
  58.1 0.0 copy-done.3
  58.1 0.0 copy-done.4
  58.1 3.5 %gather.1 = (bf16[32,1536]{1,0:T(8,128)(2,1)}, bf16[32,1536]{1,0:T(8,128)(2,1)}) custom-call(s32[1,96]{1,0:T(1,128)S(1)} %copy-done.3, s32[1,96]{1,0:T(1,128)S(1)} %copy-done.4, s32[1,1]{1,0:T(1,128)S(6)} %copy.12.live_ref, bf16[96,64,512]{2,1,0:T(8,128)(2,1)S(1)} %get-tuple-element.27.weight_ref, bf16[32,32]{1,0:T(8,128)(2,1)S(1)} %copy-done.2, ...), custom_call_target="tpu_custom_call" | custom-call | tf_op jit(solution)/shard_map/gather/pallas_call | solution.py:415
  (4 shorter events, 0.1 us)
Async XLA Ops:
  0.6 7.8 %copy-start.1 = (bf16[1,32,1536]{2,1,0:T(8,128)(2,1)S(1)}, bf16[1,32,1536]{2,1,0:T(8,128)(2,1)}, u32[]{:S(2)}) copy-start(bf16[1,32,1536]{2,1,0:T(8,128)(2,1)} %param.15) | copy-start | bytes 294916
  1.3 11.8 %copy-start = (bf16[27,32,32]{2,1,0:T(8,128)(2,1)S(1)}, bf16[27,32,32]{2,1,0:T(8,128)(2,1)}, u32[]{:S(2)}) copy-start(bf16[27,32,32]{2,1,0:T(8,128)(2,1)} %conv_ref.3) | copy-start | bytes 165892
  1.3 16.6 %copy-start.2 = (bf16[32,32]{1,0:T(8,128)(2,1)S(1)}, bf16[32,32]{1,0:T(8,128)(2,1)}, u32[]{:S(2)}) copy-start(bf16[32,32]{1,0:T(8,128)(2,1)} %mix_ref.5) | copy-start | bytes 6148
  5.0 10.5 %collective-permute-start = (bf16[12,32,512]{2,1,0:T(8,128)(2,1)S(1)}, bf16[12,32,512]{2,1,0:T(8,128)(2,1)S(1)}, u32[]{:S(2)}, u32[]{:S(2)}) collective-permute-start(bf16[12,32,512]{2,1,0:T(8,128)(2,1)S(1)} %get-tuple-element.30.up), channel_id=1, source_target_pairs={{0,1},{1,2},{2,3},{3,4},{4,5},{5,6},{6,7},{7,0},{8,9},{9,10},{10,1... | collective-permute-start | bytes 1179656 | tf_op jit(solution)/shard_map/ppermute | solution.py:468
  5.5 12.4 %collective-permute-start.1 = (bf16[12,32,512]{2,1,0:T(8,128)(2,1)S(1)}, bf16[12,32,512]{2,1,0:T(8,128)(2,1)S(1)}, u32[]{:S(2)}, u32[]{:S(2)}) collective-permute-start(bf16[12,32,512]{2,1,0:T(8,128)(2,1)S(1)} %get-tuple-element.28.down), channel_id=1, source_target_pairs={{0,7},{1,0},{2,1},{3,2},{4,3},{5,4},{6,5},{7,6},{8,15},{9,8},{10,9... | collective-permute-start | bytes 1179656 | tf_op jit(solution)/shard_map/ppermute | solution.py:468
  8.5 49.6 %copy-start.3 = (s32[1,96]{1,0:T(1,128)S(1)}, s32[1,96]{1,0:T(1,128)}, u32[]{:S(2)}) copy-start(s32[1,96]{1,0:T(1,128)} %atom_ref.1) | copy-start | bytes 1156
  8.5 49.6 %copy-start.4 = (s32[1,96]{1,0:T(1,128)S(1)}, s32[1,96]{1,0:T(1,128)}, u32[]{:S(2)}) copy-start(s32[1,96]{1,0:T(1,128)} %cell_ref.1) | copy-start | bytes 1156
  10.5 10.6 %collective-permute-start.6 = (bf16[8,32,512]{2,1,0:T(8,128)(2,1)S(1)}, bf16[8,32,512]{2,1,0:T(8,128)(2,1)S(1)}, u32[]{:S(2)}, u32[]{:S(2)}) collective-permute-start(bf16[8,32,512]{2,1,0:T(8,128)(2,1)S(1)} %get-tuple-element.35.up), channel_id=1, source_target_pairs={{0,1},{1,2},{2,3},{3,4},{4,5},{5,6},{6,7},{7,0},{8,9},{9,10},{10,1... | collective-permute-start | bytes 786440 | tf_op jit(solution)/shard_map/ppermute | solution.py:468
  10.5 12.0 %collective-permute-start.7 = (bf16[8,32,512]{2,1,0:T(8,128)(2,1)S(1)}, bf16[8,32,512]{2,1,0:T(8,128)(2,1)S(1)}, u32[]{:S(2)}, u32[]{:S(2)}) collective-permute-start(bf16[8,32,512]{2,1,0:T(8,128)(2,1)S(1)} %get-tuple-element.34.down), channel_id=1, source_target_pairs={{0,7},{1,0},{2,1},{3,2},{4,3},{5,4},{6,5},{7,6},{8,15},{9,8},{10,9... | collective-permute-start | bytes 786440 | tf_op jit(solution)/shard_map/ppermute | solution.py:468
  24.2 4.5 %collective-permute-start.10 = (bf16[144,128]{1,0:T(8,128)(2,1)S(1)}, bf16[144,128]{1,0:T(8,128)(2,1)S(1)}, u32[]{:S(2)}, u32[]{:S(2)}) collective-permute-start(bf16[144,128]{1,0:T(8,128)(2,1)S(1)} %get-tuple-element.47), channel_id=1, source_target_pairs={{0,1},{1,0},{2,3},{3,2},{4,5},{5,4},{6,7},{7,6},{8,9},{9,8},{10,11... | collective-permute-start | bytes 110600 | tf_op jit(solution)/shard_map/ppermute | solution.py:474
  26.0 15.2 %collective-permute-start.4 = (bf16[4,32,512]{2,1,0:T(8,128)(2,1)S(1)}, bf16[4,32,512]{2,1,0:T(8,128)(2,1)S(1)}, u32[]{:S(2)}, u32[]{:S(2)}) collective-permute-start(bf16[4,32,512]{2,1,0:T(8,128)(2,1)S(1)} %get-tuple-element.36.high), channel_id=1, source_target_pairs={{0,1},{1,2},{2,3},{3,4},{4,5},{5,6},{6,7},{7,0},{8,9},{9,10},{10,1... | collective-permute-start | bytes 393224 | tf_op jit(solution)/shard_map/ppermute | solution.py:468
  26.1 15.1 %collective-permute-start.5 = (bf16[4,32,512]{2,1,0:T(8,128)(2,1)S(1)}, bf16[4,32,512]{2,1,0:T(8,128)(2,1)S(1)}, u32[]{:S(2)}, u32[]{:S(2)}) collective-permute-start(bf16[4,32,512]{2,1,0:T(8,128)(2,1)S(1)} %get-tuple-element.37.low), channel_id=1, source_target_pairs={{0,7},{1,0},{2,1},{3,2},{4,3},{5,4},{6,5},{7,6},{8,15},{9,8},{10,9... | collective-permute-start | bytes 393224 | tf_op jit(solution)/shard_map/ppermute | solution.py:468
  28.7 4.0 %collective-permute-start.11 = (bf16[144,128]{1,0:T(8,128)(2,1)S(1)}, bf16[144,128]{1,0:T(8,128)(2,1)S(1)}, u32[]{:S(2)}, u32[]{:S(2)}) collective-permute-start(bf16[144,128]{1,0:T(8,128)(2,1)S(1)} %add_convert_fusion), channel_id=1, source_target_pairs={{0,8},{8,0},{16,24},{24,16},{1,9},{9,1},{17,25},{25,17},{2,10},{10... | collective-permute-start | bytes 110600 | tf_op jit(solution)/shard_map/ppermute | solution.py:474
  32.7 4.9 %collective-permute-start.12 = (bf16[144,128]{1,0:T(8,128)(2,1)S(1)}, bf16[144,128]{1,0:T(8,128)(2,1)S(1)}, u32[]{:S(2)}, u32[]{:S(2)}) collective-permute-start(bf16[144,128]{1,0:T(8,128)(2,1)S(1)} %add.19), channel_id=1, source_target_pairs={{0,16},{8,24},{16,0},{24,8},{1,17},{9,25},{17,1},{25,9},{2,18},{10... | collective-permute-start | bytes 110600 | tf_op jit(solution)/shard_map/ppermute | solution.py:474
  37.6 8.0 %collective-permute-start.13 = (bf16[144,128]{1,0:T(8,128)(2,1)S(1)}, bf16[144,128]{1,0:T(8,128)(2,1)S(1)}, u32[]{:S(2)}, u32[]{:S(2)}) collective-permute-start(bf16[144,128]{1,0:T(8,128)(2,1)S(1)} %add.20), channel_id=1, source_target_pairs={{0,2},{1,3},{2,0},{3,1},{4,6},{5,7},{6,4},{7,5},{8,10},{9,11},{10,... | collective-permute-start | bytes 110600 | tf_op jit(solution)/shard_map/ppermute | solution.py:474
  38.3 7.4 %collective-permute-start.14 = (bf16[144,128]{1,0:T(8,128)(2,1)S(1)}, bf16[144,128]{1,0:T(8,128)(2,1)S(1)}, u32[]{:S(2)}, u32[]{:S(2)}) collective-permute-start(bf16[144,128]{1,0:T(8,128)(2,1)S(1)} %add.20), channel_id=1, source_target_pairs={{0,4},{1,5},{2,6},{3,7},{4,0},{5,1},{6,2},{7,3},{8,12},{9,13},{10,... | collective-permute-start | bytes 110600 | tf_op jit(solution)/shard_map/ppermute | solution.py:474
  38.8 9.5 %collective-permute-start.15 = (bf16[144,128]{1,0:T(8,128)(2,1)S(1)}, bf16[144,128]{1,0:T(8,128)(2,1)S(1)}, u32[]{:S(2)}, u32[]{:S(2)}) collective-permute-start(bf16[144,128]{1,0:T(8,128)(2,1)S(1)} %add.20), channel_id=1, source_target_pairs={{0,6},{1,7},{2,4},{3,5},{4,2},{5,3},{6,0},{7,1},{8,14},{9,15},{10,... | collective-permute-start | bytes 110600 | tf_op jit(solution)/shard_map/ppermute | solution.py:474
  43.0 9.6 %collective-permute-start.8 = (bf16[8,32,512]{2,1,0:T(8,128)(2,1)S(1)}, bf16[8,32,512]{2,1,0:T(8,128)(2,1)S(1)}, u32[]{:S(2)}, u32[]{:S(2)}) collective-permute-start(bf16[8,32,512]{2,1,0:T(8,128)(2,1)S(1)} %get-tuple-element.42.b2), channel_id=1, source_target_pairs={{0,1},{1,2},{2,3},{3,4},{4,5},{5,6},{6,7},{7,0},{8,9},{9,10},{10,1... | collective-permute-start | bytes 786440 | tf_op jit(solution)/shard_map/ppermute | solution.py:468
  43.0 9.5 %collective-permute-start.9 = (bf16[8,32,512]{2,1,0:T(8,128)(2,1)S(1)}, bf16[8,32,512]{2,1,0:T(8,128)(2,1)S(1)}, u32[]{:S(2)}, u32[]{:S(2)}) collective-permute-start(bf16[8,32,512]{2,1,0:T(8,128)(2,1)S(1)} %get-tuple-element.43.b1), channel_id=1, source_target_pairs={{0,7},{1,0},{2,1},{3,2},{4,3},{5,4},{6,5},{7,6},{8,15},{9,8},{10,9... | collective-permute-start | bytes 786440 | tf_op jit(solution)/shard_map/ppermute | solution.py:468
  45.7 12.4 %collective-permute-start.2 = (bf16[8,32,512]{2,1,0:T(8,128)(2,1)S(1)}, bf16[8,32,512]{2,1,0:T(8,128)(2,1)S(1)}, u32[]{:S(2)}, u32[]{:S(2)}) collective-permute-start(bf16[8,32,512]{2,1,0:T(8,128)(2,1)S(1)} %get-tuple-element.32.a2), channel_id=1, source_target_pairs={{0,1},{1,2},{2,3},{3,4},{4,5},{5,6},{6,7},{7,0},{8,9},{9,10},{10,1... | collective-permute-start | bytes 786440 | tf_op jit(solution)/shard_map/ppermute | solution.py:468
  45.7 12.4 %collective-permute-start.3 = (bf16[8,32,512]{2,1,0:T(8,128)(2,1)S(1)}, bf16[8,32,512]{2,1,0:T(8,128)(2,1)S(1)}, u32[]{:S(2)}, u32[]{:S(2)}) collective-permute-start(bf16[8,32,512]{2,1,0:T(8,128)(2,1)S(1)} %get-tuple-element.33.a1), channel_id=1, source_target_pairs={{0,7},{1,0},{2,1},{3,2},{4,3},{5,4},{6,5},{7,6},{8,15},{9,8},{10,9... | collective-permute-start | bytes 786440 | tf_op jit(solution)/shard_map/ppermute | solution.py:468
  48.3 1.3 %collective-permute-start.16 = (bf16[144,128]{1,0:T(8,128)(2,1)S(1)}, bf16[144,128]{1,0:T(8,128)(2,1)S(1)}, u32[]{:S(2)}, u32[]{:S(2)}) collective-permute-start(bf16[144,128]{1,0:T(8,128)(2,1)S(1)} %add_add_fusion.mine_ref), channel_id=1, source_target_pairs={{0,1},{1,0},{2,3},{3,2},{4,5},{5,4},{6,7},{7,6},{8,9},{9,8},{10,11... | collective-permute-start | bytes 110600 | tf_op jit(solution)/shard_map/ppermute | solution.py:474

commit v4 on v3

--- a/solution.py
+++ b/solution.py
@@ -535,8 +535,9 @@
     drho_below, drho_above = ring(drho_high, "slab", 1), ring(drho_low, "slab", -1)
 
     total = (keep + arrived.astype(F32)).astype(BF16)
-    for turn in range((lax.axis_size("rep") - 1).bit_length()):
-        arrived = exchanged(total, "rep", 1 << turn)
+    turns = (lax.axis_size("rep") - 1).bit_length()
+    for turn in range(turns):
+        arrived = exchanged(total, "rep", 1 << (turns - 1 - turn))
         total = total + arrived
     strides = [1 << i for i in range(1, (lax.axis_size("slab") - 1).bit_length())]
     for stride in strides[:-2]:
@@ -544,7 +545,8 @@
         total = total + arrived
     near, far = strides[-2:]
     across = [exchanged(total, "slab", s) for s in (near, far, near | far)]
-    total = ((total + across[0]) + (across[1] + across[2])).astype(BF16)
+    one, two, three = (value.astype(F32) for value in across)
+    total = (total.astype(F32) + one) + (two + three)
     other = exchanged(total, "slab", 1)
 
     groups = lax.axis_size("rep") * lax.axis_size("slab")

time: 61.8 us -> 61.6 us (level)
  transfers between devices with their start and end apart: 17 -> 17, of which waited for: 9 -> 10; matrix products, arithmetic and copies ran while one was open for 0% -> 0% of each run, Pallas kernels for 14% -> 14%
where the time goes in v4:
time: 61.6 us; the launch traced here: 61.4 us
  starting transfers between devices  23.9 us (39%)
  waiting for transfers between devices  18.7 us (30%)
  Pallas kernels  17.3 us (28%)
  between operations  1.44 us (2%)
    ppermute x10, starting transfers between devices, ring(): lax.ppermute(value, axis, pairs)  14.2 us
    ppermute x10, waiting for transfers between devices, ring(): lax.ppermute(value, axis, pairs)  12.8 us
    ppermute x7, starting transfers between devices, exchanged(): return lax.ppermute(value, axis, [(i, i ^ stride) for i in range(count)])  9.74 us
    ppermute x7, waiting for transfers between devices, exchanged(): return lax.ppermute(value, axis, [(i, i ^ stride) for i in range(count)])  5.92 us
    pallas_call x1, Pallas kernels, first_deposit(): pl.pallas_call(first_deposit_kernel, in_specs=list_specs() + [hbm()] * 2,...  3.64 us
    pallas_call x1, Pallas kernels, gather(): pl.pallas_call(gather_kernel, in_specs=[pl.BlockSpec(memory_space=pltpu.S...  3.51 us
    pallas_call x1, Pallas kernels, step(): pl.pallas_call(forward_kernel, in_specs=[whole()] * 7, out_specs=[whole()...  2.85 us
    pallas_call x1, Pallas kernels, second_deposit(): pl.pallas_call(second_deposit_kernel, in_specs=list_specs() + [whole()] *...  1.97 us
  transfers between devices with their start and end apart: 17, of which 10 were waited for; matrix products, arithmetic and copies ran while one was open for 0% of the time, Pallas kernels for 14%

profile of v4, /device:TPU:0, one launch (start us, length us, event | category | flops | bytes accessed | tf_op | source)
XLA Modules:
  0.0 61.4 jit_solution(7992604359419606196)
XLA Ops:
  0.6 0.0 copy-start.1
  1.3 0.0 copy-start
  1.3 0.0 copy-start.2
  1.3 3.6 %first_deposit.1 = (bf16[12,32,512]{2,1,0:T(8,128)(2,1)S(1)}, bf16[8,32,512]{2,1,0:T(8,128)(2,1)S(1)}, bf16[12,32,512]{2,1,0:T(8,128)(2,1)S(1)}, bf16[96,64,512]{2,1,0:T(8,128)(2,1)S(1)}) custom-call(s32[1,96]{1,0:T(1,128)} %atom_ref.1, s32[1,96]{1,0:T(1,128)} %cell_ref.1, s32[1,1]{1,0:T(1,128)S(6)} %copy.12.live_ref, bf16[32,1536]{1,0:T(8,128)(2,1)} %bitcast.7, ...), custom_call_target="tpu_custom_call" | custom-call | tf_op jit(solution)/shard_map/first_deposit/pallas_call | solution.py:142
  5.0 0.6 collective-permute-start
  5.5 2.9 %collective-permute-start.1 = (bf16[12,32,512]{2,1,0:T(8,128)(2,1)S(1)}, bf16[12,32,512]{2,1,0:T(8,128)(2,1)S(1)}, u32[]{:S(2)}, u32[]{:S(2)}) collective-permute-start(bf16[12,32,512]{2,1,0:T(8,128)(2,1)S(1)} %get-tuple-element.28.down), channel_id=1, source_target_pairs={{0,7},{1,0},{2,1},{3,2},{4,3},{5,4},{6,5},{7,6},{8,15},{9,8},{10,9... | collective-permute-start | bytes 1179656 | tf_op jit(solution)/shard_map/ppermute | solution.py:468
  8.5 0.0 copy-done.1
  8.5 0.0 copy-start.3
  8.5 0.0 copy-start.4
  8.5 2.0 %second_deposit.1 = (bf16[8,32,512]{2,1,0:T(8,128)(2,1)S(1)}, bf16[4,32,512]{2,1,0:T(8,128)(2,1)S(1)}, bf16[8,32,512]{2,1,0:T(8,128)(2,1)S(1)}, bf16[4,32,512]{2,1,0:T(8,128)(2,1)S(1)}, bf16[8,32,512]{2,1,0:T(8,128)(2,1)S(1)}) custom-call(s32[1,96]{1,0:T(1,128)} %atom_ref.1, s32[1,96]{1,0:T(1,128)} %cell_ref.1, s32[1,1]{1,0:T(1,128)S(6)} %copy.12.live_ref, ...), custom_call_target="tpu_custom_call" | custom-call | tf_op jit(solution)/shard_map/second_deposit/pallas_call | solution.py:157
  10.5 0.1 collective-permute-start.6
  10.5 2.6 %collective-permute-start.7 = (bf16[8,32,512]{2,1,0:T(8,128)(2,1)S(1)}, bf16[8,32,512]{2,1,0:T(8,128)(2,1)S(1)}, u32[]{:S(2)}, u32[]{:S(2)}) collective-permute-start(bf16[8,32,512]{2,1,0:T(8,128)(2,1)S(1)} %get-tuple-element.34.down), channel_id=1, source_target_pairs={{0,7},{1,0},{2,1},{3,2},{4,3},{5,4},{6,5},{7,6},{8,15},{9,8},{10,9... | collective-permute-start | bytes 786440 | tf_op jit(solution)/shard_map/ppermute | solution.py:468
  13.2 0.0 copy-done
  13.2 0.8 %toeplitz.1 = (bf16[384,576]{1,0:T(8,128)(2,1)S(1)}, bf16[384,576]{1,0:T(8,128)(2,1)S(1)}) custom-call(bf16[27,32,32]{2,1,0:T(8,128)(2,1)S(1)} %copy-done), custom_call_target="tpu_custom_call" | custom-call | tf_op jit(solution)/shard_map/toeplitz/pallas_call | solution.py:200
  13.9 1.6 %collective-permute-done.below = bf16[12,32,512]{2,1,0:T(8,128)(2,1)S(1)} collective-permute-done((bf16[12,32,512]{2,1,0:T(8,128)(2,1)S(1)}, bf16[12,32,512]{2,1,0:T(8,128)(2,1)S(1)}, u32[]{:S(2)}, u32[]{:S(2)}) %collective-permute-start) | collective-permute-done | bytes 393248 | tf_op jit(solution)/shard_map/ppermute | solution.py:468
  15.5 2.5 %collective-permute-done.1.above = bf16[12,32,512]{2,1,0:T(8,128)(2,1)S(1)} collective-permute-done((bf16[12,32,512]{2,1,0:T(8,128)(2,1)S(1)}, bf16[12,32,512]{2,1,0:T(8,128)(2,1)S(1)}, u32[]{:S(2)}, u32[]{:S(2)}) %collective-permute-start.1) | collective-permute-done | bytes 393248 | tf_op jit(solution)/shard_map/ppermute | solution.py:468
  18.0 0.0 copy-done.2
  18.0 2.9 %forward.1 = (bf16[8,32,512]{2,1,0:T(8,128)(2,1)S(1)}, bf16[8,32,512]{2,1,0:T(8,128)(2,1)S(1)}, bf16[576,2048]{1,0:T(8,128)(2,1)S(1)}) custom-call(bf16[12,32,512]{2,1,0:T(8,128)(2,1)S(1)} %get-tuple-element.28.down, bf16[8,32,512]{2,1,0:T(8,128)(2,1)S(1)} %get-tuple-element.29.middle, bf16[12,32,512]{2,1,0:T(8,128)(2,1)S(1)} %get-tuple-element.30.up, ...), custom_call_target="tpu_custom_call" | custom-call | tf_op jit(solution)/shard_map/forward/pallas_call | solution.py:504
  20.8 0.3 collective-permute-done.6.below
  21.1 1.5 %collective-permute-done.7.above = bf16[8,32,512]{2,1,0:T(8,128)(2,1)S(1)} collective-permute-done((bf16[8,32,512]{2,1,0:T(8,128)(2,1)S(1)}, bf16[8,32,512]{2,1,0:T(8,128)(2,1)S(1)}, u32[]{:S(2)}, u32[]{:S(2)}) %collective-permute-start.7) | collective-permute-done | bytes 262176 | tf_op jit(solution)/shard_map/ppermute | solution.py:468
  22.6 1.6 %gradient.1 = (f32[144,128]{1,0:T(8,128)S(1)}, bf16[144,128]{1,0:T(8,128)(2,1)S(1)}, bf16[128,2048]{1,0:T(8,128)(2,1)S(1)}) custom-call(bf16[4,32,512]{2,1,0:T(8,128)(2,1)S(1)} %get-tuple-element.37.low, bf16[8,32,512]{2,1,0:T(8,128)(2,1)S(1)} %get-tuple-element.38.middle, bf16[4,32,512]{2,1,0:T(8,128)(2,1)S(1)} %get-tuple-element.36.high, ...), custom_call_target="tpu_custom_call" | custom-call | tf_op jit(solution)/shard_map/gradient/pallas_call | solution.py:516
  24.2 1.8 %collective-permute-start.10 = (bf16[144,128]{1,0:T(8,128)(2,1)S(1)}, bf16[144,128]{1,0:T(8,128)(2,1)S(1)}, u32[]{:S(2)}, u32[]{:S(2)}) collective-permute-start(bf16[144,128]{1,0:T(8,128)(2,1)S(1)} %get-tuple-element.47), channel_id=1, source_target_pairs={{0,1},{1,0},{2,3},{3,2},{4,5},{5,4},{6,7},{7,6},{8,9},{9,8},{10,11... | collective-permute-start | bytes 110600 | tf_op jit(solution)/shard_map/ppermute | solution.py:474
  26.0 0.1 collective-permute-start.4
  26.1 2.6 %collective-permute-start.5 = (bf16[4,32,512]{2,1,0:T(8,128)(2,1)S(1)}, bf16[4,32,512]{2,1,0:T(8,128)(2,1)S(1)}, u32[]{:S(2)}, u32[]{:S(2)}) collective-permute-start(bf16[4,32,512]{2,1,0:T(8,128)(2,1)S(1)} %get-tuple-element.37.low), channel_id=1, source_target_pairs={{0,7},{1,0},{2,1},{3,2},{4,3},{5,4},{6,5},{7,6},{8,15},{9,8},{10,9... | collective-permute-start | bytes 393224 | tf_op jit(solution)/shard_map/ppermute | solution.py:468
  28.6 0.0 collective-permute-done.10
  28.7 2.7 %collective-permute-start.11 = (bf16[144,128]{1,0:T(8,128)(2,1)S(1)}, bf16[144,128]{1,0:T(8,128)(2,1)S(1)}, u32[]{:S(2)}, u32[]{:S(2)}) collective-permute-start(bf16[144,128]{1,0:T(8,128)(2,1)S(1)} %add_convert_fusion), channel_id=1, source_target_pairs={{0,16},{8,24},{16,0},{24,8},{1,17},{9,25},{17,1},{25,9},{2,18},{10... | collective-permute-start | bytes 110600 | tf_op jit(solution)/shard_map/ppermute | solution.py:474
  31.3 2.3 %collective-permute-done.11 = bf16[144,128]{1,0:T(8,128)(2,1)S(1)} collective-permute-done((bf16[144,128]{1,0:T(8,128)(2,1)S(1)}, bf16[144,128]{1,0:T(8,128)(2,1)S(1)}, u32[]{:S(2)}, u32[]{:S(2)}) %collective-permute-start.11) | collective-permute-done | bytes 36896 | tf_op jit(solution)/shard_map/ppermute | solution.py:474
  33.6 1.6 %collective-permute-start.12 = (bf16[144,128]{1,0:T(8,128)(2,1)S(1)}, bf16[144,128]{1,0:T(8,128)(2,1)S(1)}, u32[]{:S(2)}, u32[]{:S(2)}) collective-permute-start(bf16[144,128]{1,0:T(8,128)(2,1)S(1)} %add.19), channel_id=1, source_target_pairs={{0,8},{8,0},{16,24},{24,16},{1,9},{9,1},{17,25},{25,17},{2,10},{10... | collective-permute-start | bytes 110600 | tf_op jit(solution)/shard_map/ppermute | solution.py:474
  35.2 2.4 %collective-permute-done.12 = bf16[144,128]{1,0:T(8,128)(2,1)S(1)} collective-permute-done((bf16[144,128]{1,0:T(8,128)(2,1)S(1)}, bf16[144,128]{1,0:T(8,128)(2,1)S(1)}, u32[]{:S(2)}, u32[]{:S(2)}) %collective-permute-start.12) | collective-permute-done | bytes 36896 | tf_op jit(solution)/shard_map/ppermute | solution.py:474
  37.6 0.7 %collective-permute-start.13 = (bf16[144,128]{1,0:T(8,128)(2,1)S(1)}, bf16[144,128]{1,0:T(8,128)(2,1)S(1)}, u32[]{:S(2)}, u32[]{:S(2)}) collective-permute-start(bf16[144,128]{1,0:T(8,128)(2,1)S(1)} %add.20), channel_id=1, source_target_pairs={{0,2},{1,3},{2,0},{3,1},{4,6},{5,7},{6,4},{7,5},{8,10},{9,11},{10,... | collective-permute-start | bytes 110600 | tf_op jit(solution)/shard_map/ppermute | solution.py:474
  38.3 0.8 %collective-permute-start.14 = (bf16[144,128]{1,0:T(8,128)(2,1)S(1)}, bf16[144,128]{1,0:T(8,128)(2,1)S(1)}, u32[]{:S(2)}, u32[]{:S(2)}) collective-permute-start(bf16[144,128]{1,0:T(8,128)(2,1)S(1)} %add.20), channel_id=1, source_target_pairs={{0,4},{1,5},{2,6},{3,7},{4,0},{5,1},{6,2},{7,3},{8,12},{9,13},{10,... | collective-permute-start | bytes 110600 | tf_op jit(solution)/shard_map/ppermute | solution.py:474
  39.1 2.1 %collective-permute-start.15 = (bf16[144,128]{1,0:T(8,128)(2,1)S(1)}, bf16[144,128]{1,0:T(8,128)(2,1)S(1)}, u32[]{:S(2)}, u32[]{:S(2)}) collective-permute-start(bf16[144,128]{1,0:T(8,128)(2,1)S(1)} %add.20), channel_id=1, source_target_pairs={{0,6},{1,7},{2,4},{3,5},{4,2},{5,3},{6,0},{7,1},{8,14},{9,15},{10,... | collective-permute-start | bytes 110600 | tf_op jit(solution)/shard_map/ppermute | solution.py:474
  41.2 0.0 collective-permute-done.4.below
  41.2 0.0 collective-permute-done.5.above
  41.2 1.8 %backward.1 = (bf16[8,32,512]{2,1,0:T(8,128)(2,1)S(1)}, bf16[8,32,512]{2,1,0:T(8,128)(2,1)S(1)}) custom-call(bf16[8,32,512]{2,1,0:T(8,128)(2,1)S(1)} %get-tuple-element.34.down, bf16[8,32,512]{2,1,0:T(8,128)(2,1)S(1)} %get-tuple-element.35.up, bf16[4,32,512]{2,1,0:T(8,128)(2,1)S(1)} %collective-permute-done.4.below, ...), custom_call_target="tpu_custom_call" | custom-call | tf_op jit(solution)/shard_map/backward/pallas_call | solution.py:526
  43.0 0.1 collective-permute-start.8
  43.0 2.6 %collective-permute-start.9 = (bf16[8,32,512]{2,1,0:T(8,128)(2,1)S(1)}, bf16[8,32,512]{2,1,0:T(8,128)(2,1)S(1)}, u32[]{:S(2)}, u32[]{:S(2)}) collective-permute-start(bf16[8,32,512]{2,1,0:T(8,128)(2,1)S(1)} %get-tuple-element.43.b1), channel_id=1, source_target_pairs={{0,7},{1,0},{2,1},{3,2},{4,3},{5,4},{6,5},{7,6},{8,15},{9,8},{10,9... | collective-permute-start | bytes 786440 | tf_op jit(solution)/shard_map/ppermute | solution.py:468
  45.7 0.0 collective-permute-done.13
  45.7 0.0 collective-permute-start.2
  45.7 0.0 collective-permute-done.14
  45.7 2.6 %collective-permute-start.3 = (bf16[8,32,512]{2,1,0:T(8,128)(2,1)S(1)}, bf16[8,32,512]{2,1,0:T(8,128)(2,1)S(1)}, u32[]{:S(2)}, u32[]{:S(2)}) collective-permute-start(bf16[8,32,512]{2,1,0:T(8,128)(2,1)S(1)} %get-tuple-element.33.a1), channel_id=1, source_target_pairs={{0,7},{1,0},{2,1},{3,2},{4,3},{5,4},{6,5},{7,6},{8,15},{9,8},{10,9... | collective-permute-start | bytes 786440 | tf_op jit(solution)/shard_map/ppermute | solution.py:468
  48.3 0.0 collective-permute-done.15
  48.3 0.1 collective-permute-start.16
  48.4 1.3 %collective-permute-done.16.other_ref = f32[144,128]{1,0:T(8,128)S(1)} collective-permute-done((f32[144,128]{1,0:T(8,128)S(1)}, f32[144,128]{1,0:T(8,128)S(1)}, u32[]{:S(2)}, u32[]{:S(2)}) %collective-permute-start.16) | collective-permute-done | bytes 73760 | tf_op jit(solution)/shard_map/ppermute | solution.py:474
  49.7 1.2 %finish.1 = (f32[27,32,32]{2,1,0:T(8,128)}, f32[32,32]{1,0:T(8,128)}) custom-call(f32[144,128]{1,0:T(8,128)S(1)} %add_add_fusion.mine_ref, f32[144,128]{1,0:T(8,128)S(1)} %collective-permute-done.16.other_ref, bf16[32,32]{1,0:T(8,128)(2,1)S(1)} %copy-done.2, bf16[27,32,32]{2,1,0:T(8,128)(2,1)S(1)} %copy-done), custom_call_target="tpu_custom_call" | custom-call | tf_op jit(solution)/shard_map/finish/pallas_call | solution.py:553
  50.9 1.4 %collective-permute-done.8.b0 = bf16[8,32,512]{2,1,0:T(8,128)(2,1)S(1)} collective-permute-done((bf16[8,32,512]{2,1,0:T(8,128)(2,1)S(1)}, bf16[8,32,512]{2,1,0:T(8,128)(2,1)S(1)}, u32[]{:S(2)}, u32[]{:S(2)}) %collective-permute-start.8) | collective-permute-done | bytes 262176 | tf_op jit(solution)/shard_map/ppermute | solution.py:468
  52.3 0.1 collective-permute-done.9.b3
  52.4 5.5 %collective-permute-done.2.a0 = bf16[8,32,512]{2,1,0:T(8,128)(2,1)S(1)} collective-permute-done((bf16[8,32,512]{2,1,0:T(8,128)(2,1)S(1)}, bf16[8,32,512]{2,1,0:T(8,128)(2,1)S(1)}, u32[]{:S(2)}, u32[]{:S(2)}) %collective-permute-start.2) | collective-permute-done | bytes 262176 | tf_op jit(solution)/shard_map/ppermute | solution.py:468
  57.9 0.0 collective-permute-done.3.a3
  57.9 0.0 copy-done.3
  57.9 0.0 copy-done.4
  57.9 3.5 %gather.1 = (bf16[32,1536]{1,0:T(8,128)(2,1)}, bf16[32,1536]{1,0:T(8,128)(2,1)}) custom-call(s32[1,96]{1,0:T(1,128)S(1)} %copy-done.3, s32[1,96]{1,0:T(1,128)S(1)} %copy-done.4, s32[1,1]{1,0:T(1,128)S(6)} %copy.12.live_ref, bf16[96,64,512]{2,1,0:T(8,128)(2,1)S(1)} %get-tuple-element.27.weight_ref, bf16[32,32]{1,0:T(8,128)(2,1)S(1)} %copy-done.2, ...), custom_call_target="tpu_custom_call" | custom-call | tf_op jit(solution)/shard_map/gather/pallas_call | solution.py:415
  (4 shorter events, 0.1 us)
Async XLA Ops:
  0.6 7.8 %copy-start.1 = (bf16[1,32,1536]{2,1,0:T(8,128)(2,1)S(1)}, bf16[1,32,1536]{2,1,0:T(8,128)(2,1)}, u32[]{:S(2)}) copy-start(bf16[1,32,1536]{2,1,0:T(8,128)(2,1)} %param.15) | copy-start | bytes 294916
  1.3 11.8 %copy-start = (bf16[27,32,32]{2,1,0:T(8,128)(2,1)S(1)}, bf16[27,32,32]{2,1,0:T(8,128)(2,1)}, u32[]{:S(2)}) copy-start(bf16[27,32,32]{2,1,0:T(8,128)(2,1)} %conv_ref.3) | copy-start | bytes 165892
  1.3 16.6 %copy-start.2 = (bf16[32,32]{1,0:T(8,128)(2,1)S(1)}, bf16[32,32]{1,0:T(8,128)(2,1)}, u32[]{:S(2)}) copy-start(bf16[32,32]{1,0:T(8,128)(2,1)} %mix_ref.5) | copy-start | bytes 6148
  5.0 10.5 %collective-permute-start = (bf16[12,32,512]{2,1,0:T(8,128)(2,1)S(1)}, bf16[12,32,512]{2,1,0:T(8,128)(2,1)S(1)}, u32[]{:S(2)}, u32[]{:S(2)}) collective-permute-start(bf16[12,32,512]{2,1,0:T(8,128)(2,1)S(1)} %get-tuple-element.30.up), channel_id=1, source_target_pairs={{0,1},{1,2},{2,3},{3,4},{4,5},{5,6},{6,7},{7,0},{8,9},{9,10},{10,1... | collective-permute-start | bytes 1179656 | tf_op jit(solution)/shard_map/ppermute | solution.py:468
  5.5 12.4 %collective-permute-start.1 = (bf16[12,32,512]{2,1,0:T(8,128)(2,1)S(1)}, bf16[12,32,512]{2,1,0:T(8,128)(2,1)S(1)}, u32[]{:S(2)}, u32[]{:S(2)}) collective-permute-start(bf16[12,32,512]{2,1,0:T(8,128)(2,1)S(1)} %get-tuple-element.28.down), channel_id=1, source_target_pairs={{0,7},{1,0},{2,1},{3,2},{4,3},{5,4},{6,5},{7,6},{8,15},{9,8},{10,9... | collective-permute-start | bytes 1179656 | tf_op jit(solution)/shard_map/ppermute | solution.py:468
  8.5 49.4 %copy-start.3 = (s32[1,96]{1,0:T(1,128)S(1)}, s32[1,96]{1,0:T(1,128)}, u32[]{:S(2)}) copy-start(s32[1,96]{1,0:T(1,128)} %atom_ref.1) | copy-start | bytes 1156
  8.5 49.4 %copy-start.4 = (s32[1,96]{1,0:T(1,128)S(1)}, s32[1,96]{1,0:T(1,128)}, u32[]{:S(2)}) copy-start(s32[1,96]{1,0:T(1,128)} %cell_ref.1) | copy-start | bytes 1156
  10.5 10.6 %collective-permute-start.6 = (bf16[8,32,512]{2,1,0:T(8,128)(2,1)S(1)}, bf16[8,32,512]{2,1,0:T(8,128)(2,1)S(1)}, u32[]{:S(2)}, u32[]{:S(2)}) collective-permute-start(bf16[8,32,512]{2,1,0:T(8,128)(2,1)S(1)} %get-tuple-element.35.up), channel_id=1, source_target_pairs={{0,1},{1,2},{2,3},{3,4},{4,5},{5,6},{6,7},{7,0},{8,9},{9,10},{10,1... | collective-permute-start | bytes 786440 | tf_op jit(solution)/shard_map/ppermute | solution.py:468
  10.5 12.0 %collective-permute-start.7 = (bf16[8,32,512]{2,1,0:T(8,128)(2,1)S(1)}, bf16[8,32,512]{2,1,0:T(8,128)(2,1)S(1)}, u32[]{:S(2)}, u32[]{:S(2)}) collective-permute-start(bf16[8,32,512]{2,1,0:T(8,128)(2,1)S(1)} %get-tuple-element.34.down), channel_id=1, source_target_pairs={{0,7},{1,0},{2,1},{3,2},{4,3},{5,4},{6,5},{7,6},{8,15},{9,8},{10,9... | collective-permute-start | bytes 786440 | tf_op jit(solution)/shard_map/ppermute | solution.py:468
  24.2 4.5 %collective-permute-start.10 = (bf16[144,128]{1,0:T(8,128)(2,1)S(1)}, bf16[144,128]{1,0:T(8,128)(2,1)S(1)}, u32[]{:S(2)}, u32[]{:S(2)}) collective-permute-start(bf16[144,128]{1,0:T(8,128)(2,1)S(1)} %get-tuple-element.47), channel_id=1, source_target_pairs={{0,1},{1,0},{2,3},{3,2},{4,5},{5,4},{6,7},{7,6},{8,9},{9,8},{10,11... | collective-permute-start | bytes 110600 | tf_op jit(solution)/shard_map/ppermute | solution.py:474
  26.0 15.2 %collective-permute-start.4 = (bf16[4,32,512]{2,1,0:T(8,128)(2,1)S(1)}, bf16[4,32,512]{2,1,0:T(8,128)(2,1)S(1)}, u32[]{:S(2)}, u32[]{:S(2)}) collective-permute-start(bf16[4,32,512]{2,1,0:T(8,128)(2,1)S(1)} %get-tuple-element.36.high), channel_id=1, source_target_pairs={{0,1},{1,2},{2,3},{3,4},{4,5},{5,6},{6,7},{7,0},{8,9},{9,10},{10,1... | collective-permute-start | bytes 393224 | tf_op jit(solution)/shard_map/ppermute | solution.py:468
  26.1 15.1 %collective-permute-start.5 = (bf16[4,32,512]{2,1,0:T(8,128)(2,1)S(1)}, bf16[4,32,512]{2,1,0:T(8,128)(2,1)S(1)}, u32[]{:S(2)}, u32[]{:S(2)}) collective-permute-start(bf16[4,32,512]{2,1,0:T(8,128)(2,1)S(1)} %get-tuple-element.37.low), channel_id=1, source_target_pairs={{0,7},{1,0},{2,1},{3,2},{4,3},{5,4},{6,5},{7,6},{8,15},{9,8},{10,9... | collective-permute-start | bytes 393224 | tf_op jit(solution)/shard_map/ppermute | solution.py:468
  28.7 4.9 %collective-permute-start.11 = (bf16[144,128]{1,0:T(8,128)(2,1)S(1)}, bf16[144,128]{1,0:T(8,128)(2,1)S(1)}, u32[]{:S(2)}, u32[]{:S(2)}) collective-permute-start(bf16[144,128]{1,0:T(8,128)(2,1)S(1)} %add_convert_fusion), channel_id=1, source_target_pairs={{0,16},{8,24},{16,0},{24,8},{1,17},{9,25},{17,1},{25,9},{2,18},{10... | collective-permute-start | bytes 110600 | tf_op jit(solution)/shard_map/ppermute | solution.py:474
  33.6 4.0 %collective-permute-start.12 = (bf16[144,128]{1,0:T(8,128)(2,1)S(1)}, bf16[144,128]{1,0:T(8,128)(2,1)S(1)}, u32[]{:S(2)}, u32[]{:S(2)}) collective-permute-start(bf16[144,128]{1,0:T(8,128)(2,1)S(1)} %add.19), channel_id=1, source_target_pairs={{0,8},{8,0},{16,24},{24,16},{1,9},{9,1},{17,25},{25,17},{2,10},{10... | collective-permute-start | bytes 110600 | tf_op jit(solution)/shard_map/ppermute | solution.py:474
  37.6 8.0 %collective-permute-start.13 = (bf16[144,128]{1,0:T(8,128)(2,1)S(1)}, bf16[144,128]{1,0:T(8,128)(2,1)S(1)}, u32[]{:S(2)}, u32[]{:S(2)}) collective-permute-start(bf16[144,128]{1,0:T(8,128)(2,1)S(1)} %add.20), channel_id=1, source_target_pairs={{0,2},{1,3},{2,0},{3,1},{4,6},{5,7},{6,4},{7,5},{8,10},{9,11},{10,... | collective-permute-start | bytes 110600 | tf_op jit(solution)/shard_map/ppermute | solution.py:474
  38.3 7.4 %collective-permute-start.14 = (bf16[144,128]{1,0:T(8,128)(2,1)S(1)}, bf16[144,128]{1,0:T(8,128)(2,1)S(1)}, u32[]{:S(2)}, u32[]{:S(2)}) collective-permute-start(bf16[144,128]{1,0:T(8,128)(2,1)S(1)} %add.20), channel_id=1, source_target_pairs={{0,4},{1,5},{2,6},{3,7},{4,0},{5,1},{6,2},{7,3},{8,12},{9,13},{10,... | collective-permute-start | bytes 110600 | tf_op jit(solution)/shard_map/ppermute | solution.py:474
  39.1 9.2 %collective-permute-start.15 = (bf16[144,128]{1,0:T(8,128)(2,1)S(1)}, bf16[144,128]{1,0:T(8,128)(2,1)S(1)}, u32[]{:S(2)}, u32[]{:S(2)}) collective-permute-start(bf16[144,128]{1,0:T(8,128)(2,1)S(1)} %add.20), channel_id=1, source_target_pairs={{0,6},{1,7},{2,4},{3,5},{4,2},{5,3},{6,0},{7,1},{8,14},{9,15},{10,... | collective-permute-start | bytes 110600 | tf_op jit(solution)/shard_map/ppermute | solution.py:474
  43.0 9.3 %collective-permute-start.8 = (bf16[8,32,512]{2,1,0:T(8,128)(2,1)S(1)}, bf16[8,32,512]{2,1,0:T(8,128)(2,1)S(1)}, u32[]{:S(2)}, u32[]{:S(2)}) collective-permute-start(bf16[8,32,512]{2,1,0:T(8,128)(2,1)S(1)} %get-tuple-element.42.b2), channel_id=1, source_target_pairs={{0,1},{1,2},{2,3},{3,4},{4,5},{5,6},{6,7},{7,0},{8,9},{9,10},{10,1... | collective-permute-start | bytes 786440 | tf_op jit(solution)/shard_map/ppermute | solution.py:468
  43.0 9.3 %collective-permute-start.9 = (bf16[8,32,512]{2,1,0:T(8,128)(2,1)S(1)}, bf16[8,32,512]{2,1,0:T(8,128)(2,1)S(1)}, u32[]{:S(2)}, u32[]{:S(2)}) collective-permute-start(bf16[8,32,512]{2,1,0:T(8,128)(2,1)S(1)} %get-tuple-element.43.b1), channel_id=1, source_target_pairs={{0,7},{1,0},{2,1},{3,2},{4,3},{5,4},{6,5},{7,6},{8,15},{9,8},{10,9... | collective-permute-start | bytes 786440 | tf_op jit(solution)/shard_map/ppermute | solution.py:468
  45.7 12.2 %collective-permute-start.2 = (bf16[8,32,512]{2,1,0:T(8,128)(2,1)S(1)}, bf16[8,32,512]{2,1,0:T(8,128)(2,1)S(1)}, u32[]{:S(2)}, u32[]{:S(2)}) collective-permute-start(bf16[8,32,512]{2,1,0:T(8,128)(2,1)S(1)} %get-tuple-element.32.a2), channel_id=1, source_target_pairs={{0,1},{1,2},{2,3},{3,4},{4,5},{5,6},{6,7},{7,0},{8,9},{9,10},{10,1... | collective-permute-start | bytes 786440 | tf_op jit(solution)/shard_map/ppermute | solution.py:468
  45.7 12.2 %collective-permute-start.3 = (bf16[8,32,512]{2,1,0:T(8,128)(2,1)S(1)}, bf16[8,32,512]{2,1,0:T(8,128)(2,1)S(1)}, u32[]{:S(2)}, u32[]{:S(2)}) collective-permute-start(bf16[8,32,512]{2,1,0:T(8,128)(2,1)S(1)} %get-tuple-element.33.a1), channel_id=1, source_target_pairs={{0,7},{1,0},{2,1},{3,2},{4,3},{5,4},{6,5},{7,6},{8,15},{9,8},{10,9... | collective-permute-start | bytes 786440 | tf_op jit(solution)/shard_map/ppermute | solution.py:468
  48.3 1.3 %collective-permute-start.16 = (f32[144,128]{1,0:T(8,128)S(1)}, f32[144,128]{1,0:T(8,128)S(1)}, u32[]{:S(2)}, u32[]{:S(2)}) collective-permute-start(f32[144,128]{1,0:T(8,128)S(1)} %add_add_fusion.mine_ref), channel_id=1, source_target_pairs={{0,1},{1,0},{2,3},{3,2},{4,5},{5,4},{6,7},{7,6},{8,9},{9,8},{10,11... | collective-permute-start | bytes 221192 | tf_op jit(solution)/shard_map/ppermute | solution.py:474

commit v5 on v4

--- a/solution.py
+++ b/solution.py
@@ -250,19 +250,27 @@
         )
     channels = low_ref.shape[1]
     quarters = cells // chunk
+    third = ZD * channels
+    wide = 2 * GX
+    count = cells // wide
+    lane = lax.broadcasted_iota(jnp.int32, (channels, wide), 1)
     for po in range(ZD):
-        rows = slice(po * channels, (po + 1) * channels)
-        third = ZD * channels
-        before = partial[rows, :]
-        here = partial[third + po * channels : third + (po + 1) * channels, :]
-        after = partial[2 * third + po * channels : 2 * third + (po + 1) * channels, :]
-        result = (
-            here + pltpu.roll(before, GX, 1) + pltpu.roll(after, cells - GX, 1)
-        ).astype(BF16)
+
+        def group(dy, j):
+            row = dy * third + po * channels
+            first = (j % count) * wide
+            return partial[row : row + channels, first : first + wide]
+
         out_ref = low_ref if po < ZH else high_ref
-        first = (po % ZH) * quarters
-        for q in range(quarters):
-            out_ref[first + q] = result[:, q * chunk : (q + 1) * chunk]
+        block = (po % ZH) * quarters
+        before = group(0, count - 1) + group(2, 0)
+        for j in range(count):
+            after = group(0, j) + group(2, j + 1)
+            mixed = jnp.where(lane < GX, after, before)
+            result = (group(1, j) + pltpu.roll(mixed, GX, 1)).astype(BF16)
+            first = j * wide % chunk
+            out_ref[block + j * wide // chunk, :, first : first + wide] = result
+            before = after
 
 
 def forward_kernel(

time: 61.6 us -> 61.6 us (level)
  transfers between devices with their start and end apart: 17 -> 17, of which waited for: 10 -> 10; matrix products, arithmetic and copies ran while one was open for 0% -> 0% of each run, Pallas kernels for 14% -> 13%
where the time goes in v5:
time: 61.6 us; the launch traced here: 61.4 us
  starting transfers between devices  23.9 us (39%)
  waiting for transfers between devices  19.1 us (31%)
  Pallas kernels  16.9 us (27%)
  between operations  1.44 us (2%)
    ppermute x10, starting transfers between devices, ring(): lax.ppermute(value, axis, pairs)  14.2 us
    ppermute x10, waiting for transfers between devices, ring(): lax.ppermute(value, axis, pairs)  13.2 us
    ppermute x7, starting transfers between devices, exchanged(): return lax.ppermute(value, axis, [(i, i ^ stride) for i in range(count)])  9.74 us
    ppermute x7, waiting for transfers between devices, exchanged(): return lax.ppermute(value, axis, [(i, i ^ stride) for i in range(count)])  5.92 us
    pallas_call x1, Pallas kernels, first_deposit(): pl.pallas_call(first_deposit_kernel, in_specs=list_specs() + [hbm()] * 2,...  3.64 us
    pallas_call x1, Pallas kernels, gather(): pl.pallas_call(gather_kernel, in_specs=[pl.BlockSpec(memory_space=pltpu.S...  3.51 us
    pallas_call x1, Pallas kernels, step(): pl.pallas_call(forward_kernel, in_specs=[whole()] * 7, out_specs=[whole()...  2.47 us
    pallas_call x1, Pallas kernels, second_deposit(): pl.pallas_call(second_deposit_kernel, in_specs=list_specs() + [whole()] *...  1.97 us
  transfers between devices with their start and end apart: 17, of which 10 were waited for; matrix products, arithmetic and copies ran while one was open for 0% of the time, Pallas kernels for 13%

profile of v5, /device:TPU:0, one launch (start us, length us, event | category | flops | bytes accessed | tf_op | source)
XLA Modules:
  0.0 61.4 jit_solution(17814005768515325569)
XLA Ops:
  0.6 0.0 copy-start.1
  1.3 0.0 copy-start
  1.3 0.0 copy-start.2
  1.3 3.6 %first_deposit.1 = (bf16[12,32,512]{2,1,0:T(8,128)(2,1)S(1)}, bf16[8,32,512]{2,1,0:T(8,128)(2,1)S(1)}, bf16[12,32,512]{2,1,0:T(8,128)(2,1)S(1)}, bf16[96,64,512]{2,1,0:T(8,128)(2,1)S(1)}) custom-call(s32[1,96]{1,0:T(1,128)} %atom_ref.1, s32[1,96]{1,0:T(1,128)} %cell_ref.1, s32[1,1]{1,0:T(1,128)S(6)} %copy.12.live_ref, bf16[32,1536]{1,0:T(8,128)(2,1)} %bitcast.7, ...), custom_call_target="tpu_custom_call" | custom-call | tf_op jit(solution)/shard_map/first_deposit/pallas_call | solution.py:142
  5.0 0.6 collective-permute-start
  5.5 2.9 %collective-permute-start.1 = (bf16[12,32,512]{2,1,0:T(8,128)(2,1)S(1)}, bf16[12,32,512]{2,1,0:T(8,128)(2,1)S(1)}, u32[]{:S(2)}, u32[]{:S(2)}) collective-permute-start(bf16[12,32,512]{2,1,0:T(8,128)(2,1)S(1)} %get-tuple-element.28.down), channel_id=1, source_target_pairs={{0,7},{1,0},{2,1},{3,2},{4,3},{5,4},{6,5},{7,6},{8,15},{9,8},{10,9... | collective-permute-start | bytes 1179656 | tf_op jit(solution)/shard_map/ppermute | solution.py:476
  8.5 0.0 copy-done.1
  8.5 0.0 copy-start.3
  8.5 0.0 copy-start.4
  8.5 2.0 %second_deposit.1 = (bf16[8,32,512]{2,1,0:T(8,128)(2,1)S(1)}, bf16[4,32,512]{2,1,0:T(8,128)(2,1)S(1)}, bf16[8,32,512]{2,1,0:T(8,128)(2,1)S(1)}, bf16[4,32,512]{2,1,0:T(8,128)(2,1)S(1)}, bf16[8,32,512]{2,1,0:T(8,128)(2,1)S(1)}) custom-call(s32[1,96]{1,0:T(1,128)} %atom_ref.1, s32[1,96]{1,0:T(1,128)} %cell_ref.1, s32[1,1]{1,0:T(1,128)S(6)} %copy.12.live_ref, ...), custom_call_target="tpu_custom_call" | custom-call | tf_op jit(solution)/shard_map/second_deposit/pallas_call | solution.py:157
  10.5 0.1 collective-permute-start.6
  10.5 2.6 %collective-permute-start.7 = (bf16[8,32,512]{2,1,0:T(8,128)(2,1)S(1)}, bf16[8,32,512]{2,1,0:T(8,128)(2,1)S(1)}, u32[]{:S(2)}, u32[]{:S(2)}) collective-permute-start(bf16[8,32,512]{2,1,0:T(8,128)(2,1)S(1)} %get-tuple-element.34.down), channel_id=1, source_target_pairs={{0,7},{1,0},{2,1},{3,2},{4,3},{5,4},{6,5},{7,6},{8,15},{9,8},{10,9... | collective-permute-start | bytes 786440 | tf_op jit(solution)/shard_map/ppermute | solution.py:476
  13.2 0.0 copy-done
  13.2 0.8 %toeplitz.1 = (bf16[384,576]{1,0:T(8,128)(2,1)S(1)}, bf16[384,576]{1,0:T(8,128)(2,1)S(1)}) custom-call(bf16[27,32,32]{2,1,0:T(8,128)(2,1)S(1)} %copy-done), custom_call_target="tpu_custom_call" | custom-call | tf_op jit(solution)/shard_map/toeplitz/pallas_call | solution.py:200
  13.9 1.6 %collective-permute-done.below = bf16[12,32,512]{2,1,0:T(8,128)(2,1)S(1)} collective-permute-done((bf16[12,32,512]{2,1,0:T(8,128)(2,1)S(1)}, bf16[12,32,512]{2,1,0:T(8,128)(2,1)S(1)}, u32[]{:S(2)}, u32[]{:S(2)}) %collective-permute-start) | collective-permute-done | bytes 393248 | tf_op jit(solution)/shard_map/ppermute | solution.py:476
  15.5 2.5 %collective-permute-done.1.above = bf16[12,32,512]{2,1,0:T(8,128)(2,1)S(1)} collective-permute-done((bf16[12,32,512]{2,1,0:T(8,128)(2,1)S(1)}, bf16[12,32,512]{2,1,0:T(8,128)(2,1)S(1)}, u32[]{:S(2)}, u32[]{:S(2)}) %collective-permute-start.1) | collective-permute-done | bytes 393248 | tf_op jit(solution)/shard_map/ppermute | solution.py:476
  18.0 0.0 copy-done.2
  18.0 2.5 %forward.1 = (bf16[8,32,512]{2,1,0:T(8,128)(2,1)S(1)}, bf16[8,32,512]{2,1,0:T(8,128)(2,1)S(1)}, bf16[576,2048]{1,0:T(8,128)(2,1)S(1)}) custom-call(bf16[12,32,512]{2,1,0:T(8,128)(2,1)S(1)} %get-tuple-element.28.down, bf16[8,32,512]{2,1,0:T(8,128)(2,1)S(1)} %get-tuple-element.29.middle, bf16[12,32,512]{2,1,0:T(8,128)(2,1)S(1)} %get-tuple-element.30.up, ...), custom_call_target="tpu_custom_call" | custom-call | tf_op jit(solution)/shard_map/forward/pallas_call | solution.py:512
  20.5 0.6 %collective-permute-done.6.below = bf16[8,32,512]{2,1,0:T(8,128)(2,1)S(1)} collective-permute-done((bf16[8,32,512]{2,1,0:T(8,128)(2,1)S(1)}, bf16[8,32,512]{2,1,0:T(8,128)(2,1)S(1)}, u32[]{:S(2)}, u32[]{:S(2)}) %collective-permute-start.6) | collective-permute-done | bytes 262176 | tf_op jit(solution)/shard_map/ppermute | solution.py:476
  21.1 1.5 %collective-permute-done.7.above = bf16[8,32,512]{2,1,0:T(8,128)(2,1)S(1)} collective-permute-done((bf16[8,32,512]{2,1,0:T(8,128)(2,1)S(1)}, bf16[8,32,512]{2,1,0:T(8,128)(2,1)S(1)}, u32[]{:S(2)}, u32[]{:S(2)}) %collective-permute-start.7) | collective-permute-done | bytes 262176 | tf_op jit(solution)/shard_map/ppermute | solution.py:476
  22.6 1.6 %gradient.1 = (f32[144,128]{1,0:T(8,128)S(1)}, bf16[144,128]{1,0:T(8,128)(2,1)S(1)}, bf16[128,2048]{1,0:T(8,128)(2,1)S(1)}) custom-call(bf16[4,32,512]{2,1,0:T(8,128)(2,1)S(1)} %get-tuple-element.37.low, bf16[8,32,512]{2,1,0:T(8,128)(2,1)S(1)} %get-tuple-element.38.middle, bf16[4,32,512]{2,1,0:T(8,128)(2,1)S(1)} %get-tuple-element.36.high, ...), custom_call_target="tpu_custom_call" | custom-call | tf_op jit(solution)/shard_map/gradient/pallas_call | solution.py:524
  24.2 1.8 %collective-permute-start.10 = (bf16[144,128]{1,0:T(8,128)(2,1)S(1)}, bf16[144,128]{1,0:T(8,128)(2,1)S(1)}, u32[]{:S(2)}, u32[]{:S(2)}) collective-permute-start(bf16[144,128]{1,0:T(8,128)(2,1)S(1)} %get-tuple-element.47), channel_id=1, source_target_pairs={{0,1},{1,0},{2,3},{3,2},{4,5},{5,4},{6,7},{7,6},{8,9},{9,8},{10,11... | collective-permute-start | bytes 110600 | tf_op jit(solution)/shard_map/ppermute | solution.py:482
  26.0 0.1 collective-permute-start.4
  26.1 2.6 %collective-permute-start.5 = (bf16[4,32,512]{2,1,0:T(8,128)(2,1)S(1)}, bf16[4,32,512]{2,1,0:T(8,128)(2,1)S(1)}, u32[]{:S(2)}, u32[]{:S(2)}) collective-permute-start(bf16[4,32,512]{2,1,0:T(8,128)(2,1)S(1)} %get-tuple-element.37.low), channel_id=1, source_target_pairs={{0,7},{1,0},{2,1},{3,2},{4,3},{5,4},{6,5},{7,6},{8,15},{9,8},{10,9... | collective-permute-start | bytes 393224 | tf_op jit(solution)/shard_map/ppermute | solution.py:476
  28.6 0.0 collective-permute-done.10
  28.7 2.7 %collective-permute-start.11 = (bf16[144,128]{1,0:T(8,128)(2,1)S(1)}, bf16[144,128]{1,0:T(8,128)(2,1)S(1)}, u32[]{:S(2)}, u32[]{:S(2)}) collective-permute-start(bf16[144,128]{1,0:T(8,128)(2,1)S(1)} %add_convert_fusion), channel_id=1, source_target_pairs={{0,16},{8,24},{16,0},{24,8},{1,17},{9,25},{17,1},{25,9},{2,18},{10... | collective-permute-start | bytes 110600 | tf_op jit(solution)/shard_map/ppermute | solution.py:482
  31.3 2.3 %collective-permute-done.11 = bf16[144,128]{1,0:T(8,128)(2,1)S(1)} collective-permute-done((bf16[144,128]{1,0:T(8,128)(2,1)S(1)}, bf16[144,128]{1,0:T(8,128)(2,1)S(1)}, u32[]{:S(2)}, u32[]{:S(2)}) %collective-permute-start.11) | collective-permute-done | bytes 36896 | tf_op jit(solution)/shard_map/ppermute | solution.py:482
  33.6 1.6 %collective-permute-start.12 = (bf16[144,128]{1,0:T(8,128)(2,1)S(1)}, bf16[144,128]{1,0:T(8,128)(2,1)S(1)}, u32[]{:S(2)}, u32[]{:S(2)}) collective-permute-start(bf16[144,128]{1,0:T(8,128)(2,1)S(1)} %add.19), channel_id=1, source_target_pairs={{0,8},{8,0},{16,24},{24,16},{1,9},{9,1},{17,25},{25,17},{2,10},{10... | collective-permute-start | bytes 110600 | tf_op jit(solution)/shard_map/ppermute | solution.py:482
  35.2 2.4 %collective-permute-done.12 = bf16[144,128]{1,0:T(8,128)(2,1)S(1)} collective-permute-done((bf16[144,128]{1,0:T(8,128)(2,1)S(1)}, bf16[144,128]{1,0:T(8,128)(2,1)S(1)}, u32[]{:S(2)}, u32[]{:S(2)}) %collective-permute-start.12) | collective-permute-done | bytes 36896 | tf_op jit(solution)/shard_map/ppermute | solution.py:482
  37.6 0.7 %collective-permute-start.13 = (bf16[144,128]{1,0:T(8,128)(2,1)S(1)}, bf16[144,128]{1,0:T(8,128)(2,1)S(1)}, u32[]{:S(2)}, u32[]{:S(2)}) collective-permute-start(bf16[144,128]{1,0:T(8,128)(2,1)S(1)} %add.20), channel_id=1, source_target_pairs={{0,2},{1,3},{2,0},{3,1},{4,6},{5,7},{6,4},{7,5},{8,10},{9,11},{10,... | collective-permute-start | bytes 110600 | tf_op jit(solution)/shard_map/ppermute | solution.py:482
  38.3 0.8 %collective-permute-start.14 = (bf16[144,128]{1,0:T(8,128)(2,1)S(1)}, bf16[144,128]{1,0:T(8,128)(2,1)S(1)}, u32[]{:S(2)}, u32[]{:S(2)}) collective-permute-start(bf16[144,128]{1,0:T(8,128)(2,1)S(1)} %add.20), channel_id=1, source_target_pairs={{0,4},{1,5},{2,6},{3,7},{4,0},{5,1},{6,2},{7,3},{8,12},{9,13},{10,... | collective-permute-start | bytes 110600 | tf_op jit(solution)/shard_map/ppermute | solution.py:482
  39.1 2.1 %collective-permute-start.15 = (bf16[144,128]{1,0:T(8,128)(2,1)S(1)}, bf16[144,128]{1,0:T(8,128)(2,1)S(1)}, u32[]{:S(2)}, u32[]{:S(2)}) collective-permute-start(bf16[144,128]{1,0:T(8,128)(2,1)S(1)} %add.20), channel_id=1, source_target_pairs={{0,6},{1,7},{2,4},{3,5},{4,2},{5,3},{6,0},{7,1},{8,14},{9,15},{10,... | collective-permute-start | bytes 110600 | tf_op jit(solution)/shard_map/ppermute | solution.py:482
  41.2 0.0 collective-permute-done.4.below
  41.2 0.0 collective-permute-done.5.above
  41.2 1.8 %backward.1 = (bf16[8,32,512]{2,1,0:T(8,128)(2,1)S(1)}, bf16[8,32,512]{2,1,0:T(8,128)(2,1)S(1)}) custom-call(bf16[8,32,512]{2,1,0:T(8,128)(2,1)S(1)} %get-tuple-element.34.down, bf16[8,32,512]{2,1,0:T(8,128)(2,1)S(1)} %get-tuple-element.35.up, bf16[4,32,512]{2,1,0:T(8,128)(2,1)S(1)} %collective-permute-done.4.below, ...), custom_call_target="tpu_custom_call" | custom-call | tf_op jit(solution)/shard_map/backward/pallas_call | solution.py:534
  43.0 0.1 collective-permute-start.8
  43.0 2.6 %collective-permute-start.9 = (bf16[8,32,512]{2,1,0:T(8,128)(2,1)S(1)}, bf16[8,32,512]{2,1,0:T(8,128)(2,1)S(1)}, u32[]{:S(2)}, u32[]{:S(2)}) collective-permute-start(bf16[8,32,512]{2,1,0:T(8,128)(2,1)S(1)} %get-tuple-element.43.b1), channel_id=1, source_target_pairs={{0,7},{1,0},{2,1},{3,2},{4,3},{5,4},{6,5},{7,6},{8,15},{9,8},{10,9... | collective-permute-start | bytes 786440 | tf_op jit(solution)/shard_map/ppermute | solution.py:476
  45.7 0.0 collective-permute-done.13
  45.7 0.0 collective-permute-start.2
  45.7 0.0 collective-permute-done.14
  45.7 2.6 %collective-permute-start.3 = (bf16[8,32,512]{2,1,0:T(8,128)(2,1)S(1)}, bf16[8,32,512]{2,1,0:T(8,128)(2,1)S(1)}, u32[]{:S(2)}, u32[]{:S(2)}) collective-permute-start(bf16[8,32,512]{2,1,0:T(8,128)(2,1)S(1)} %get-tuple-element.33.a1), channel_id=1, source_target_pairs={{0,7},{1,0},{2,1},{3,2},{4,3},{5,4},{6,5},{7,6},{8,15},{9,8},{10,9... | collective-permute-start | bytes 786440 | tf_op jit(solution)/shard_map/ppermute | solution.py:476
  48.3 0.0 collective-permute-done.15
  48.3 0.1 collective-permute-start.16
  48.4 1.3 %collective-permute-done.16.other_ref = f32[144,128]{1,0:T(8,128)S(1)} collective-permute-done((f32[144,128]{1,0:T(8,128)S(1)}, f32[144,128]{1,0:T(8,128)S(1)}, u32[]{:S(2)}, u32[]{:S(2)}) %collective-permute-start.16) | collective-permute-done | bytes 73760 | tf_op jit(solution)/shard_map/ppermute | solution.py:482
  49.7 1.2 %finish.1 = (f32[27,32,32]{2,1,0:T(8,128)}, f32[32,32]{1,0:T(8,128)}) custom-call(f32[144,128]{1,0:T(8,128)S(1)} %add_add_fusion.mine_ref, f32[144,128]{1,0:T(8,128)S(1)} %collective-permute-done.16.other_ref, bf16[32,32]{1,0:T(8,128)(2,1)S(1)} %copy-done.2, bf16[27,32,32]{2,1,0:T(8,128)(2,1)S(1)} %copy-done), custom_call_target="tpu_custom_call" | custom-call | tf_op jit(solution)/shard_map/finish/pallas_call | solution.py:561
  50.9 1.4 %collective-permute-done.8.b0 = bf16[8,32,512]{2,1,0:T(8,128)(2,1)S(1)} collective-permute-done((bf16[8,32,512]{2,1,0:T(8,128)(2,1)S(1)}, bf16[8,32,512]{2,1,0:T(8,128)(2,1)S(1)}, u32[]{:S(2)}, u32[]{:S(2)}) %collective-permute-start.8) | collective-permute-done | bytes 262176 | tf_op jit(solution)/shard_map/ppermute | solution.py:476
  52.3 0.1 collective-permute-done.9.b3
  52.4 5.5 %collective-permute-done.2.a0 = bf16[8,32,512]{2,1,0:T(8,128)(2,1)S(1)} collective-permute-done((bf16[8,32,512]{2,1,0:T(8,128)(2,1)S(1)}, bf16[8,32,512]{2,1,0:T(8,128)(2,1)S(1)}, u32[]{:S(2)}, u32[]{:S(2)}) %collective-permute-start.2) | collective-permute-done | bytes 262176 | tf_op jit(solution)/shard_map/ppermute | solution.py:476
  57.9 0.0 collective-permute-done.3.a3
  57.9 0.0 copy-done.3
  57.9 0.0 copy-done.4
  57.9 3.5 %gather.1 = (bf16[32,1536]{1,0:T(8,128)(2,1)}, bf16[32,1536]{1,0:T(8,128)(2,1)}) custom-call(s32[1,96]{1,0:T(1,128)S(1)} %copy-done.3, s32[1,96]{1,0:T(1,128)S(1)} %copy-done.4, s32[1,1]{1,0:T(1,128)S(6)} %copy.12.live_ref, bf16[96,64,512]{2,1,0:T(8,128)(2,1)S(1)} %get-tuple-element.27.weight_ref, bf16[32,32]{1,0:T(8,128)(2,1)S(1)} %copy-done.2, ...), custom_call_target="tpu_custom_call" | custom-call | tf_op jit(solution)/shard_map/gather/pallas_call | solution.py:423
  (4 shorter events, 0.1 us)
Async XLA Ops:
  0.6 7.8 %copy-start.1 = (bf16[1,32,1536]{2,1,0:T(8,128)(2,1)S(1)}, bf16[1,32,1536]{2,1,0:T(8,128)(2,1)}, u32[]{:S(2)}) copy-start(bf16[1,32,1536]{2,1,0:T(8,128)(2,1)} %param.15) | copy-start | bytes 294916
  1.3 11.8 %copy-start = (bf16[27,32,32]{2,1,0:T(8,128)(2,1)S(1)}, bf16[27,32,32]{2,1,0:T(8,128)(2,1)}, u32[]{:S(2)}) copy-start(bf16[27,32,32]{2,1,0:T(8,128)(2,1)} %conv_ref.3) | copy-start | bytes 165892
  1.3 16.6 %copy-start.2 = (bf16[32,32]{1,0:T(8,128)(2,1)S(1)}, bf16[32,32]{1,0:T(8,128)(2,1)}, u32[]{:S(2)}) copy-start(bf16[32,32]{1,0:T(8,128)(2,1)} %mix_ref.5) | copy-start | bytes 6148
  5.0 10.5 %collective-permute-start = (bf16[12,32,512]{2,1,0:T(8,128)(2,1)S(1)}, bf16[12,32,512]{2,1,0:T(8,128)(2,1)S(1)}, u32[]{:S(2)}, u32[]{:S(2)}) collective-permute-start(bf16[12,32,512]{2,1,0:T(8,128)(2,1)S(1)} %get-tuple-element.30.up), channel_id=1, source_target_pairs={{0,1},{1,2},{2,3},{3,4},{4,5},{5,6},{6,7},{7,0},{8,9},{9,10},{10,1... | collective-permute-start | bytes 1179656 | tf_op jit(solution)/shard_map/ppermute | solution.py:476
  5.5 12.4 %collective-permute-start.1 = (bf16[12,32,512]{2,1,0:T(8,128)(2,1)S(1)}, bf16[12,32,512]{2,1,0:T(8,128)(2,1)S(1)}, u32[]{:S(2)}, u32[]{:S(2)}) collective-permute-start(bf16[12,32,512]{2,1,0:T(8,128)(2,1)S(1)} %get-tuple-element.28.down), channel_id=1, source_target_pairs={{0,7},{1,0},{2,1},{3,2},{4,3},{5,4},{6,5},{7,6},{8,15},{9,8},{10,9... | collective-permute-start | bytes 1179656 | tf_op jit(solution)/shard_map/ppermute | solution.py:476
  8.5 49.4 %copy-start.3 = (s32[1,96]{1,0:T(1,128)S(1)}, s32[1,96]{1,0:T(1,128)}, u32[]{:S(2)}) copy-start(s32[1,96]{1,0:T(1,128)} %atom_ref.1) | copy-start | bytes 1156
  8.5 49.4 %copy-start.4 = (s32[1,96]{1,0:T(1,128)S(1)}, s32[1,96]{1,0:T(1,128)}, u32[]{:S(2)}) copy-start(s32[1,96]{1,0:T(1,128)} %cell_ref.1) | copy-start | bytes 1156
  10.5 10.6 %collective-permute-start.6 = (bf16[8,32,512]{2,1,0:T(8,128)(2,1)S(1)}, bf16[8,32,512]{2,1,0:T(8,128)(2,1)S(1)}, u32[]{:S(2)}, u32[]{:S(2)}) collective-permute-start(bf16[8,32,512]{2,1,0:T(8,128)(2,1)S(1)} %get-tuple-element.35.up), channel_id=1, source_target_pairs={{0,1},{1,2},{2,3},{3,4},{4,5},{5,6},{6,7},{7,0},{8,9},{9,10},{10,1... | collective-permute-start | bytes 786440 | tf_op jit(solution)/shard_map/ppermute | solution.py:476
  10.5 12.0 %collective-permute-start.7 = (bf16[8,32,512]{2,1,0:T(8,128)(2,1)S(1)}, bf16[8,32,512]{2,1,0:T(8,128)(2,1)S(1)}, u32[]{:S(2)}, u32[]{:S(2)}) collective-permute-start(bf16[8,32,512]{2,1,0:T(8,128)(2,1)S(1)} %get-tuple-element.34.down), channel_id=1, source_target_pairs={{0,7},{1,0},{2,1},{3,2},{4,3},{5,4},{6,5},{7,6},{8,15},{9,8},{10,9... | collective-permute-start | bytes 786440 | tf_op jit(solution)/shard_map/ppermute | solution.py:476
  24.2 4.5 %collective-permute-start.10 = (bf16[144,128]{1,0:T(8,128)(2,1)S(1)}, bf16[144,128]{1,0:T(8,128)(2,1)S(1)}, u32[]{:S(2)}, u32[]{:S(2)}) collective-permute-start(bf16[144,128]{1,0:T(8,128)(2,1)S(1)} %get-tuple-element.47), channel_id=1, source_target_pairs={{0,1},{1,0},{2,3},{3,2},{4,5},{5,4},{6,7},{7,6},{8,9},{9,8},{10,11... | collective-permute-start | bytes 110600 | tf_op jit(solution)/shard_map/ppermute | solution.py:482
  26.0 15.2 %collective-permute-start.4 = (bf16[4,32,512]{2,1,0:T(8,128)(2,1)S(1)}, bf16[4,32,512]{2,1,0:T(8,128)(2,1)S(1)}, u32[]{:S(2)}, u32[]{:S(2)}) collective-permute-start(bf16[4,32,512]{2,1,0:T(8,128)(2,1)S(1)} %get-tuple-element.36.high), channel_id=1, source_target_pairs={{0,1},{1,2},{2,3},{3,4},{4,5},{5,6},{6,7},{7,0},{8,9},{9,10},{10,1... | collective-permute-start | bytes 393224 | tf_op jit(solution)/shard_map/ppermute | solution.py:476
  26.1 15.1 %collective-permute-start.5 = (bf16[4,32,512]{2,1,0:T(8,128)(2,1)S(1)}, bf16[4,32,512]{2,1,0:T(8,128)(2,1)S(1)}, u32[]{:S(2)}, u32[]{:S(2)}) collective-permute-start(bf16[4,32,512]{2,1,0:T(8,128)(2,1)S(1)} %get-tuple-element.37.low), channel_id=1, source_target_pairs={{0,7},{1,0},{2,1},{3,2},{4,3},{5,4},{6,5},{7,6},{8,15},{9,8},{10,9... | collective-permute-start | bytes 393224 | tf_op jit(solution)/shard_map/ppermute | solution.py:476
  28.7 4.9 %collective-permute-start.11 = (bf16[144,128]{1,0:T(8,128)(2,1)S(1)}, bf16[144,128]{1,0:T(8,128)(2,1)S(1)}, u32[]{:S(2)}, u32[]{:S(2)}) collective-permute-start(bf16[144,128]{1,0:T(8,128)(2,1)S(1)} %add_convert_fusion), channel_id=1, source_target_pairs={{0,16},{8,24},{16,0},{24,8},{1,17},{9,25},{17,1},{25,9},{2,18},{10... | collective-permute-start | bytes 110600 | tf_op jit(solution)/shard_map/ppermute | solution.py:482
  33.6 4.0 %collective-permute-start.12 = (bf16[144,128]{1,0:T(8,128)(2,1)S(1)}, bf16[144,128]{1,0:T(8,128)(2,1)S(1)}, u32[]{:S(2)}, u32[]{:S(2)}) collective-permute-start(bf16[144,128]{1,0:T(8,128)(2,1)S(1)} %add.19), channel_id=1, source_target_pairs={{0,8},{8,0},{16,24},{24,16},{1,9},{9,1},{17,25},{25,17},{2,10},{10... | collective-permute-start | bytes 110600 | tf_op jit(solution)/shard_map/ppermute | solution.py:482
  37.6 8.0 %collective-permute-start.13 = (bf16[144,128]{1,0:T(8,128)(2,1)S(1)}, bf16[144,128]{1,0:T(8,128)(2,1)S(1)}, u32[]{:S(2)}, u32[]{:S(2)}) collective-permute-start(bf16[144,128]{1,0:T(8,128)(2,1)S(1)} %add.20), channel_id=1, source_target_pairs={{0,2},{1,3},{2,0},{3,1},{4,6},{5,7},{6,4},{7,5},{8,10},{9,11},{10,... | collective-permute-start | bytes 110600 | tf_op jit(solution)/shard_map/ppermute | solution.py:482
  38.3 7.4 %collective-permute-start.14 = (bf16[144,128]{1,0:T(8,128)(2,1)S(1)}, bf16[144,128]{1,0:T(8,128)(2,1)S(1)}, u32[]{:S(2)}, u32[]{:S(2)}) collective-permute-start(bf16[144,128]{1,0:T(8,128)(2,1)S(1)} %add.20), channel_id=1, source_target_pairs={{0,4},{1,5},{2,6},{3,7},{4,0},{5,1},{6,2},{7,3},{8,12},{9,13},{10,... | collective-permute-start | bytes 110600 | tf_op jit(solution)/shard_map/ppermute | solution.py:482
  39.1 9.2 %collective-permute-start.15 = (bf16[144,128]{1,0:T(8,128)(2,1)S(1)}, bf16[144,128]{1,0:T(8,128)(2,1)S(1)}, u32[]{:S(2)}, u32[]{:S(2)}) collective-permute-start(bf16[144,128]{1,0:T(8,128)(2,1)S(1)} %add.20), channel_id=1, source_target_pairs={{0,6},{1,7},{2,4},{3,5},{4,2},{5,3},{6,0},{7,1},{8,14},{9,15},{10,... | collective-permute-start | bytes 110600 | tf_op jit(solution)/shard_map/ppermute | solution.py:482
  43.0 9.3 %collective-permute-start.8 = (bf16[8,32,512]{2,1,0:T(8,128)(2,1)S(1)}, bf16[8,32,512]{2,1,0:T(8,128)(2,1)S(1)}, u32[]{:S(2)}, u32[]{:S(2)}) collective-permute-start(bf16[8,32,512]{2,1,0:T(8,128)(2,1)S(1)} %get-tuple-element.42.b2), channel_id=1, source_target_pairs={{0,1},{1,2},{2,3},{3,4},{4,5},{5,6},{6,7},{7,0},{8,9},{9,10},{10,1... | collective-permute-start | bytes 786440 | tf_op jit(solution)/shard_map/ppermute | solution.py:476
  43.0 9.3 %collective-permute-start.9 = (bf16[8,32,512]{2,1,0:T(8,128)(2,1)S(1)}, bf16[8,32,512]{2,1,0:T(8,128)(2,1)S(1)}, u32[]{:S(2)}, u32[]{:S(2)}) collective-permute-start(bf16[8,32,512]{2,1,0:T(8,128)(2,1)S(1)} %get-tuple-element.43.b1), channel_id=1, source_target_pairs={{0,7},{1,0},{2,1},{3,2},{4,3},{5,4},{6,5},{7,6},{8,15},{9,8},{10,9... | collective-permute-start | bytes 786440 | tf_op jit(solution)/shard_map/ppermute | solution.py:476
  45.7 12.2 %collective-permute-start.2 = (bf16[8,32,512]{2,1,0:T(8,128)(2,1)S(1)}, bf16[8,32,512]{2,1,0:T(8,128)(2,1)S(1)}, u32[]{:S(2)}, u32[]{:S(2)}) collective-permute-start(bf16[8,32,512]{2,1,0:T(8,128)(2,1)S(1)} %get-tuple-element.32.a2), channel_id=1, source_target_pairs={{0,1},{1,2},{2,3},{3,4},{4,5},{5,6},{6,7},{7,0},{8,9},{9,10},{10,1... | collective-permute-start | bytes 786440 | tf_op jit(solution)/shard_map/ppermute | solution.py:476
  45.7 12.2 %collective-permute-start.3 = (bf16[8,32,512]{2,1,0:T(8,128)(2,1)S(1)}, bf16[8,32,512]{2,1,0:T(8,128)(2,1)S(1)}, u32[]{:S(2)}, u32[]{:S(2)}) collective-permute-start(bf16[8,32,512]{2,1,0:T(8,128)(2,1)S(1)} %get-tuple-element.33.a1), channel_id=1, source_target_pairs={{0,7},{1,0},{2,1},{3,2},{4,3},{5,4},{6,5},{7,6},{8,15},{9,8},{10,9... | collective-permute-start | bytes 786440 | tf_op jit(solution)/shard_map/ppermute | solution.py:476
  48.3 1.3 %collective-permute-start.16 = (f32[144,128]{1,0:T(8,128)S(1)}, f32[144,128]{1,0:T(8,128)S(1)}, u32[]{:S(2)}, u32[]{:S(2)}) collective-permute-start(f32[144,128]{1,0:T(8,128)S(1)} %add_add_fusion.mine_ref), channel_id=1, source_target_pairs={{0,1},{1,0},{2,3},{3,2},{4,5},{5,4},{6,7},{7,6},{8,9},{9,8},{10,11... | collective-permute-start | bytes 221192 | tf_op jit(solution)/shard_map/ppermute | solution.py:482
